TPU v7x, 256 devices: a whole 4x4x8 slice. The times are simulated.
256 devices in a mesh: pb: 16 (over x, y_lo, core), ha: 16 (over y_hi, z).
Axes of the slice: x: 4, y: 4 (y_hi: 2, y_lo: 2; y = y_hi * 2 + y_lo), z: 8, core: 2. Of those that a mesh axis runs over, the one named last changes fastest.
Arguments:
- main_query: bfloat16 [2048, 128, 576], P('pb', 'ha'), may hold values from -1.8 to 1.8
- latent: bfloat16 [2048, 576], P('pb'), may hold values from -6 to 6
- log_sums: float32 [2048, 128], P('pb', 'ha'), may hold values from 0 to 4
- window_start: int32 [2048], P('pb'), may hold values from 0 to 2046, as said below
- index_query: bfloat16 [2048, 64, 128], P('pb', 'ha'), may hold values from -0.6 to 0.6
- index_key: bfloat16 [2048, 128], P('pb'), may hold values from -4 to 4
- index_weight: float32 [2048, 64], P('pb', 'ha'), may hold values from -4 to 4
Outputs:
- index_query_grad: bfloat16 [2048, 64, 128], P('pb', 'ha')
- index_key_grad: bfloat16 [2048, 128], P('pb')
- index_weight_grad: float32 [2048, 64], P('pb', 'ha')
Inputs may be any that keep to these rules, and one draw needn't show every extreme that they name: window_start[0] is 0, window_start[t] is at most t - 1 for t >= 1, and window_start[2047] is 2046, so every query sees itself and, past the first, at least one earlier key.
All inputs are finite; a program needn't handle non-finite values.
Results may differ from a plain program's by a relative error of at most 0.0049.
Values may be sent and summed in bfloat16 or wider, within the bound.
A program may use at most 64 MiB of HBM per device.

v0:
```python
import math

import jax
import jax.numpy as jnp
from jax import lax
from jax.sharding import PartitionSpec as P

main_scale = 192.0 ** (-0.5)
very_low = -1e30


def visible(window_start, positions, first_row, width):
    columns = first_row + jnp.arange(width, dtype=jnp.int32)
    return (columns[None, :] >= window_start[:, None]) & (columns[None, :] <= positions[:, None])


def on_device(main_query, latent, log_sums, window_start, index_query, index_key, index_weight):
    query_rows, head_count, latent_width = main_query.shape
    index_heads = index_query.shape[1]
    index_width = index_query.shape[2]
    tokens = query_rows * lax.axis_size("pb")
    positions = lax.axis_index("pb") * query_rows + jnp.arange(query_rows, dtype=jnp.int32)
    flat_query = main_query.reshape(query_rows * head_count, latent_width)
    flat_index = index_query.reshape(query_rows * index_heads, index_width)
    probs_part = jnp.zeros((query_rows, tokens), jnp.float32)
    logit_part = jnp.zeros((query_rows, tokens), jnp.float32)
    latent_piece = lax.all_gather(latent, "pb", axis=0, tiled=True)
    key_piece = lax.all_gather(index_key, "pb", axis=0, tiled=True)
    piece_rows = latent_piece.shape[0]
    block_size = math.gcd(piece_rows, 512)

    def one_block(block_index, partial_value):
        probs_inner, logit_inner = partial_value
        offset = block_index * block_size
        latent_block = lax.dynamic_slice_in_dim(latent_piece, offset, block_size, 0)
        key_block = lax.dynamic_slice_in_dim(key_piece, offset, block_size, 0)
        visible_mask = visible(window_start, positions, offset, block_size)
        scores = jnp.einsum(
            "rd,kd->rk", flat_query, latent_block, preferred_element_type=jnp.float32
        )
        scores = scores.reshape(query_rows, head_count, block_size) * main_scale
        head_mass = jnp.where(
            visible_mask, jnp.sum(jnp.exp(scores - log_sums[:, :, None]), axis=1), 0.0
        )
        active = jnp.einsum("rd,kd->rk", flat_index, key_block, preferred_element_type=jnp.float32)
        active = jnp.maximum(active.reshape(query_rows, index_heads, block_size), 0.0)
        logit_block = jnp.sum(index_weight[:, :, None] * active, axis=1)
        probs_inner = lax.dynamic_update_slice_in_dim(probs_inner, head_mass, offset, 1)
        logit_inner = lax.dynamic_update_slice_in_dim(logit_inner, logit_block, offset, 1)
        return (probs_inner, logit_inner)

    probs_part, logit_part = lax.fori_loop(
        0, piece_rows // block_size, one_block, (probs_part, logit_part)
    )
    probs_part, logit_part, keys_all = (probs_part, logit_part, key_piece)
    probs_all, logit_all = lax.psum((probs_part, logit_part), "ha")
    visible_all = visible(window_start, positions, 0, tokens)
    target = probs_all / jnp.sum(probs_all, axis=1, keepdims=True)
    masked = jnp.where(visible_all, logit_all, very_low)
    row_top = jnp.max(masked, axis=1, keepdims=True)
    expo = jnp.where(visible_all, jnp.exp(masked - row_top), 0.0)
    logit_grad = jnp.where(visible_all, expo / jnp.sum(expo, axis=1, keepdims=True) - target, 0.0)
    block_keys = math.gcd(tokens, 512)

    def back_block(block_index, partial_value):
        query_grad, weight_grad, key_grad = partial_value
        offset = block_index * block_keys
        key_block = lax.dynamic_slice_in_dim(keys_all, offset, block_keys, 0)
        grad_block = lax.dynamic_slice_in_dim(logit_grad, offset, block_keys, 1)
        active = jnp.einsum("rd,kd->rk", flat_index, key_block, preferred_element_type=jnp.float32)
        active = active.reshape(query_rows, index_heads, block_keys)
        weight_grad = weight_grad + jnp.sum(
            grad_block[:, None, :] * jnp.maximum(active, 0.0), axis=2
        )
        coeffs = jnp.where(
            active > 0.0, grad_block[:, None, :] * index_weight[:, :, None], 0.0
        ).astype(jnp.bfloat16)
        coeffs = coeffs.reshape(query_rows * index_heads, block_keys)
        query_grad = query_grad + jnp.dot(coeffs, key_block, preferred_element_type=jnp.float32)
        key_terms = jnp.einsum("rk,rd->kd", coeffs, flat_index, preferred_element_type=jnp.float32)
        key_grad = lax.dynamic_update_slice_in_dim(key_grad, key_terms, offset, 0)
        return (query_grad, weight_grad, key_grad)

    start_state = (
        jnp.zeros((query_rows * index_heads, index_width), jnp.float32),
        jnp.zeros((query_rows, index_heads), jnp.float32),
        jnp.zeros((tokens, index_width), jnp.float32),
    )
    query_grad, weight_grad, key_grad = lax.fori_loop(
        0, tokens // block_keys, back_block, start_state
    )
    key_share = lax.psum_scatter(key_grad, ("pb", "ha"), scatter_dimension=0, tiled=True).astype(
        jnp.bfloat16
    )
    key_output = lax.all_gather(key_share, "ha", axis=0, tiled=True)
    query_output = query_grad.astype(jnp.bfloat16).reshape(query_rows, index_heads, index_width)
    return (query_output, key_output, weight_grad)


def solution(mesh):
    return jax.shard_map(
        on_device,
        mesh=mesh,
        in_specs=(
            P("pb", "ha", None),
            P("pb", None),
            P("pb", "ha"),
            P("pb"),
            P("pb", "ha", None),
            P("pb", None),
            P("pb", "ha"),
        ),
        out_specs=(P("pb", "ha", None), P("pb", None), P("pb", "ha")),
        check_vma=False,
    )
```

profile of v0, /device:TPU:8, one launch (start us, length us, event | category | flops | bytes accessed | tf_op | source)
XLA Modules:
  0.0 423.4 jit_solution(11260347915637641972)
XLA Ops:
  7.2 1.7 copy.35
  10.4 2.2 copy.36
  13.4 21.1 %all_gather.9 = bf16[2048,128]{1,0:T(8,128)(2,1)} all-gather(bf16[128,128]{1,0:T(8,128)(2,1)S(1)} %copy-done.7), channel_id=1, replica_groups=mesh['pb'=16,'ha'=16] {'pb'}, dimensions={0}, use_global_device_ids=true | all-gather | bytes 557056 | tf_op jit(solution)/shard_map/all_gather | solution.py:28
  34.6 16.1 %all-gather.2.cloned.1.call-done = bf16[2048,576]{1,0:T(8,128)(2,1)} async-done(((bf16[128,576]{1,0:T(8,128)(2,1)}), bf16[2048,576]{1,0:T(8,128)(2,1)}) %all-gather.2.cloned.1.call-update) | async-done | bytes 2359312 | tf_op jit(solution)/shard_map/all_gather | solution.py:27
  52.9 50.3 %while.35 = (s32[]{:T(128)}, f32[128,2048]{1,0:T(8,128)}, f32[128,2048]{1,0:T(8,128)}, s32[128]{0:T(128)S(1)}, bf16[2048,576]{1,0:T(8,128)(2,1)}, /*index=5*/bf1...) while((s32[]{:T(128)}, f32[128,2048]{1,0:T(8,128)}, ...), condition=%wide.region_3.4_spmd.clone, body=%wide.region_0.3_spmd.clone.sunk | while | flops 673579648 | bytes 16264911 | solution.py:52
  52.9 3.4 multiply_bitcast_fusion.2
  56.3 1.9 copy.47
  58.3 2.3 fusion.47
  62.1 1.6 multiply_reduce_fusion.2
  63.7 1.8 select_dynamic-update-slice_fusion.2
  65.5 3.4 multiply_bitcast_fusion.2
  68.9 1.9 copy.47
  70.8 2.3 fusion.47
  74.6 1.6 multiply_reduce_fusion.2
  76.2 1.8 select_dynamic-update-slice_fusion.2
  78.0 3.4 multiply_bitcast_fusion.2
  81.4 1.9 copy.47
  83.4 2.3 fusion.47
  87.2 1.6 multiply_reduce_fusion.2
  88.8 1.8 select_dynamic-update-slice_fusion.2
  90.6 3.4 multiply_bitcast_fusion.2
  94.0 1.9 copy.47
  96.0 2.3 fusion.47
  99.8 1.6 multiply_reduce_fusion.2
  101.4 1.8 select_dynamic-update-slice_fusion.2
  104.2 161.3 %all-reduce.5.cloned.1.call-done = (f32[128,2048]{1,0:T(8,128)}, f32[128,2048]{1,0:T(8,128)}) async-done(((f32[128,2048]{1,0:T(8,128)}, f32[128,2048]{1,0:T(8,128)}), (f32[128,2048]{1,0:T(8,128)}, f32[128,2048]{1,0:T(8,128)})) %all-reduce.5.cloned.1.call-update) | async-done | bytes 2097168 | tf_op jit(solution)/shard_map/psum | solution.py:56
  265.5 1.7 fusion.18
  267.2 1.8 fusion.16
  269.1 1.7 subtract_select_fusion
  271.9 26.7 %while.36 = (s32[]{:T(128)}, f32[512,128]{1,0:T(8,128)S(1)}, f32[128,4]{1,0:T(8,128)}, f32[2048,128]{1,0:T(8,128)}, bf16[2048,128]{1,0:T(8,128)(2,1)}, /*index=5...) while((s32[]{:T(128)}, f32[512,128]{1,0:T(8,128)S(1)}, ...), condition=%wide.wide.region_11.12_spmd.clone, body=%wide.wide.region_9.11_spmd.clone.sunk | while | flops 203293184 | bytes 15235326 | solution.py:89
  298.6 78.0 %all-reduce.6 = bf16[2048,128]{1,0:T(8,128)(2,1)S(1)} all-reduce(f32[2048,128]{1,0:T(8,128)} %get-tuple-element.332), channel_id=2, replica_groups=mesh['pb'=16,'ha'=16] {'pb','ha'}, use_global_device_ids=true, to_apply=%region_12.13.clone | all-reduce | flops 262144 | bytes 1572864
  376.6 37.2 %all_gather.11 = bf16[128,128]{1,0:T(8,128)(2,1)S(1)} all-gather(bf16[8,128]{1,0:T(8,128)(2,1)S(1)} %dynamic-slice_convert_fusion), channel_id=1, replica_groups=mesh['pb'=16,'ha'=16] {'ha'}, dimensions={0}, use_global_device_ids=true | all-gather | bytes 34816 | tf_op jit(solution)/shard_map/all_gather | solution.py:95
  (108 shorter events, 41.8 us)
Async XLA Ops:
  7.2 5.5 %copy-start.8 = (f32[128,8]{0,1:T(8,128)S(1)}, f32[128,8]{0,1:T(8,128)}, u32[]{:S(2)}) copy-start(f32[128,8]{0,1:T(8,128)} %param.13) | copy-start | bytes 12292
  7.2 6.2 %copy-start.7 = (bf16[128,128]{1,0:T(8,128)(2,1)S(1)}, bf16[128,128]{1,0:T(8,128)(2,1)}, u32[]{:S(2)}) copy-start(bf16[128,128]{1,0:T(8,128)(2,1)} %param.16) | copy-start | bytes 98308
  7.2 43.5 %all-gather.2.cloned.1.call-start = ((), (), s32[]{:S(2)}) async-start(), calls=%async_computation | async-start | bytes 2785280 | tf_op jit(solution)/shard_map/all_gather | solution.py:27
  9.0 256.5 %all-reduce.5.cloned.1.call-start = ((), (), s32[]{:S(2)}) async-start(), calls=%async_computation.1 | async-start | bytes 4194304 | tf_op jit(solution)/shard_map/psum | solution.py:56
  10.4 42.5 %copy-start = (bf16[128,4,128]{2,1,0:T(4,128)(2,1)S(1)}, bf16[128,4,128]{2,1,0:T(4,128)(2,1)}, u32[]{:S(2)}) copy-start(bf16[128,4,128]{2,1,0:T(4,128)(2,1)} %param.15) | copy-start | bytes 393220
  10.4 42.5 %copy-start.6 = (s32[128]{0:T(128)S(1)}, s32[128]{0:T(128)}, u32[]{:S(2)}) copy-start(s32[128]{0:T(128)} %param.14) | copy-start | bytes 1540
  103.2 0.8 copy-start.3
  265.5 3.5 copy-start.2
  265.5 3.7 copy-start.1
  275.3 2.6 copy-start.4
  277.9 0.6 copy-start.5
  282.0 2.6 copy-start.4
  284.6 0.6 copy-start.5
  288.7 2.6 copy-start.4
  291.3 0.6 copy-start.5
  295.3 2.6 copy-start.4
  298.0 0.6 copy-start.5
Sparse Core Ops, SparseCore 0:
  9.9 40.7 all-gather.1
  103.3 162.0 all-reduce.4
where the time goes:
time: 425 us; the launch traced here: 423 us
  waiting for transfers between devices  177 us (42%)
  blocking collectives  136 us (32%)
  local copies, waits for them, and re-layouts  32.9 us (8%)
  matrix products  32.4 us (8%)
  other arithmetic  29.5 us (7%)
  between operations  14.1 us (3%)
    psum x1, waiting for transfers between devices, on_device(): probs_all, logit_all = lax.psum((probs_part, logit_part), 'ha')  161 us
    unnamed x1, blocking collectives  78 us
    all_gather x1, blocking collectives, on_device(): key_output = lax.all_gather(key_share, 'ha', axis=0, tiled=True)  37.2 us
    all_gather x1, blocking collectives, on_device(): key_piece = lax.all_gather(index_key, 'pb', axis=0, tiled=True)  21.1 us
    all_gather x1, waiting for transfers between devices, on_device(): latent_piece = lax.all_gather(latent, 'pb', axis=0, tiled=True)  16.1 us
    dot_general x4, matrix products, one_block(): jnp.einsum('rd,kd->rk', flat_query, latent_block, preferred_element_type=...  13.7 us
    reduce_sum x4, other arithmetic, one_block(): jnp.sum(jnp.exp(scores - log_sums[:, :, None]), axis=1)  9.23 us
    unnamed x20, local copies, waits for them, and re-layouts  9.02 us
  transfers between devices with their start and end apart: 2, of which 2 were waited for; matrix products, arithmetic and copies ran while one was open for 1% of the time, Pallas kernels for 0%

commit v1 on v0

v1 whole, which is shorter than its diff:
```python
import math

import jax
import jax.numpy as jnp
from jax import lax
from jax.sharding import PartitionSpec as P

main_scale = 192.0 ** (-0.5)
very_low = -1e30


def visible(window_start, positions, first_row, width):
    columns = first_row + jnp.arange(width, dtype=jnp.int32)
    return (columns[None, :] >= window_start[:, None]) & (columns[None, :] <= positions[:, None])


def on_device(main_query, latent, log_sums, window_start, index_query, index_key, index_weight):
    query_rows, head_count, latent_width = main_query.shape
    index_width = index_query.shape[2]
    groups = lax.axis_size("ha")
    tokens = query_rows * lax.axis_size("pb")
    own_rows = query_rows // groups
    block_first = lax.axis_index("pb") * query_rows
    flat_query = main_query.reshape(query_rows * head_count, latent_width)
    latent_piece = lax.all_gather(latent, "pb", axis=0, tiled=True)
    keys_all = lax.all_gather(index_key, "pb", axis=0, tiled=True)

    local_index = lax.all_to_all(index_query, "ha", 0, 1, tiled=True)
    local_weight = lax.all_to_all(index_weight, "ha", 0, 1, tiled=True)
    index_heads = local_index.shape[1]
    row_first = block_first + lax.axis_index("ha") * own_rows
    own_positions = row_first + jnp.arange(own_rows, dtype=jnp.int32)
    own_start = lax.dynamic_slice_in_dim(window_start, lax.axis_index("ha") * own_rows, own_rows, 0)

    positions = block_first + jnp.arange(query_rows, dtype=jnp.int32)
    probs_part = jnp.zeros((query_rows, tokens), jnp.float32)
    block_size = math.gcd(tokens, 512)

    def one_block(block_index, probs_inner):
        offset = block_index * block_size
        latent_block = lax.dynamic_slice_in_dim(latent_piece, offset, block_size, 0)
        visible_mask = visible(window_start, positions, offset, block_size)
        scores = jnp.einsum(
            "rd,kd->rk", flat_query, latent_block, preferred_element_type=jnp.float32
        )
        scores = scores.reshape(query_rows, head_count, block_size) * main_scale
        head_mass = jnp.where(
            visible_mask, jnp.sum(jnp.exp(scores - log_sums[:, :, None]), axis=1), 0.0
        )
        return lax.dynamic_update_slice_in_dim(probs_inner, head_mass, offset, 1)

    probs_part = lax.fori_loop(0, tokens // block_size, one_block, probs_part)
    probs_all = lax.psum_scatter(probs_part, "ha", scatter_dimension=0, tiled=True)

    flat_index = local_index.reshape(own_rows * index_heads, index_width)
    active = jnp.einsum("rd,kd->rk", flat_index, keys_all, preferred_element_type=jnp.float32)
    active = active.reshape(own_rows, index_heads, tokens)
    relu_act = jnp.maximum(active, 0.0)
    logit_all = jnp.sum(local_weight[:, :, None] * relu_act, axis=1)

    visible_all = visible(own_start, own_positions, 0, tokens)
    target = probs_all / jnp.sum(probs_all, axis=1, keepdims=True)
    masked = jnp.where(visible_all, logit_all, very_low)
    row_top = jnp.max(masked, axis=1, keepdims=True)
    expo = jnp.where(visible_all, jnp.exp(masked - row_top), 0.0)
    logit_grad = jnp.where(visible_all, expo / jnp.sum(expo, axis=1, keepdims=True) - target, 0.0)

    weight_grad = jnp.sum(logit_grad[:, None, :] * relu_act, axis=2)
    coeffs = jnp.where(
        active > 0.0, logit_grad[:, None, :] * local_weight[:, :, None], 0.0
    ).astype(jnp.bfloat16)
    coeffs = coeffs.reshape(own_rows * index_heads, tokens)
    query_grad = jnp.dot(coeffs, keys_all, preferred_element_type=jnp.float32)
    key_grad = jnp.einsum("rk,rd->kd", coeffs, flat_index, preferred_element_type=jnp.float32)

    key_share = lax.psum_scatter(key_grad, "pb", scatter_dimension=0, tiled=True)
    key_output = lax.psum(key_share, "ha").astype(jnp.bfloat16)
    query_grad = query_grad.astype(jnp.bfloat16).reshape(own_rows, index_heads, index_width)
    query_output = lax.all_to_all(query_grad, "ha", 1, 0, tiled=True)
    weight_output = lax.all_to_all(weight_grad, "ha", 1, 0, tiled=True)
    return (query_output, key_output, weight_output)


def solution(mesh):
    return jax.shard_map(
        on_device,
        mesh=mesh,
        in_specs=(
            P("pb", "ha", None),
            P("pb", None),
            P("pb", "ha"),
            P("pb"),
            P("pb", "ha", None),
            P("pb", None),
            P("pb", "ha"),
        ),
        out_specs=(P("pb", "ha", None), P("pb", None), P("pb", "ha")),
        check_vma=False,
    )
```

time: 425 us -> 432 us (1.016)
  waiting for transfers between devices: 177 us -> 248 us
  blocking collectives: 136 us -> 96.6 us
  starting transfers between devices: 0.08 us -> 22.2 us
  other arithmetic: 29.5 us -> 11.9 us
  local copies, waits for them, and re-layouts: 32.9 us -> 17.2 us
  matrix products: 32.4 us -> 18.8 us
    reduce_scatter x0 -> x2, waiting for transfers between devices: none -> 182 us  [the longest x1 154 us: on_device(): lax.psum_scatter(probs_part, 'ha', scatter_dimension=0, tiled=True)]
    psum x1 -> x0, waiting for transfers between devices: 161 us -> none  [on_device(): probs_all, logit_all = lax.psum((probs_part, logit_part), 'ha')]
    unnamed x1 -> x0, blocking collectives: 78 us -> none
    psum x0 -> x1, blocking collectives: none -> 77.6 us  [on_device(): key_output = lax.psum(key_share, 'ha').astype(jnp.bfloat16)]
    all_gather x2 -> x1, blocking collectives: 58.3 us -> 19 us  [on_device(): keys_all = lax.all_gather(index_key, 'pb', axis=0, tiled=True)]
    all_to_all x0 -> x4, waiting for transfers between devices: none -> 27.9 us  [the longest x1 9.98 us: on_device(): local_weight = lax.all_to_all(index_weight, 'ha', 0, 1, tiled=True)]
    all_to_all x0 -> x4, starting transfers between devices: none -> 22.1 us  [the longest x1 8.5 us: on_device(): local_weight = lax.all_to_all(index_weight, 'ha', 0, 1, tiled=True)]
    all_gather x1, waiting for transfers between devices: 16.1 us -> 37.9 us  [on_device(): latent_piece = lax.all_gather(latent, 'pb', axis=0, tiled=True)]
  transfers between devices with their start and end apart: 2 -> 7, of which waited for: 2 -> 6; matrix products, arithmetic and copies ran while one was open for 1% -> 2% of each run, Pallas kernels for 0% -> 0%
where the time goes in v1:
time: 432 us; the launch traced here: 429 us
  waiting for transfers between devices  248 us (57%)
  blocking collectives  96.6 us (22%)
  starting transfers between devices  22.2 us (5%)
  matrix products  18.8 us (4%)
  local copies, waits for them, and re-layouts  17.2 us (4%)
  between operations  13.9 us (3%)
  other arithmetic  11.9 us (3%)
    reduce_scatter x1, waiting for transfers between devices, on_device(): lax.psum_scatter(probs_part, 'ha', scatter_dimension=0, tiled=True)  154 us
    psum x1, blocking collectives, on_device(): key_output = lax.psum(key_share, 'ha').astype(jnp.bfloat16)  77.6 us
    all_gather x1, waiting for transfers between devices, on_device(): latent_piece = lax.all_gather(latent, 'pb', axis=0, tiled=True)  37.9 us
    reduce_scatter x1, waiting for transfers between devices, on_device(): lax.psum_scatter(key_grad, 'pb', scatter_dimension=0, tiled=True)  28 us
    all_gather x1, blocking collectives, on_device(): keys_all = lax.all_gather(index_key, 'pb', axis=0, tiled=True)  19 us
    dot_general x4, matrix products, one_block(): jnp.einsum('rd,kd->rk', flat_query, latent_block, preferred_element_type=...  13.7 us
    all_to_all x1, waiting for transfers between devices, on_device(): local_weight = lax.all_to_all(index_weight, 'ha', 0, 1, tiled=True)  9.98 us
    all_to_all x1, waiting for transfers between devices, on_device(): query_output = lax.all_to_all(query_grad, 'ha', 1, 0, tiled=True)  9.42 us
  transfers between devices with their start and end apart: 7, of which 6 were waited for; matrix products, arithmetic and copies ran while one was open for 2% of the time, Pallas kernels for 0%

profile of v1, /device:TPU:8, one launch (start us, length us, event | category | flops | bytes accessed | tf_op | source)
XLA Modules:
  0.0 428.6 jit_solution(10439193181329397287)
XLA Ops:
  7.2 1.7 copy.29
  9.8 2.2 copy.30
  12.0 37.9 %all-gather.2.cloned.1.call-done = bf16[2048,576]{1,0:T(8,128)(2,1)} async-done(((bf16[128,576]{1,0:T(8,128)(2,1)}), bf16[2048,576]{1,0:T(8,128)(2,1)}) %all-gather.2.cloned.1.call-update) | async-done | bytes 2359312 | tf_op jit(solution)/shard_map/all_gather | solution.py:25
  49.9 1.1 broadcast_in_dim.47
  51.1 27.8 %while.14 = (s32[]{:T(128)}, f32[128,2048]{1,0:T(8,128)}, s32[128]{0:T(128)S(1)}, bf16[2048,576]{1,0:T(8,128)(2,1)}, bf16[1024,576]{1,0:T(8,128)(2,1)S(1)}, /*in...) while((s32[]{:T(128)}, f32[128,2048]{1,0:T(8,128)}, ...), condition=%wide.region_5.6_spmd.clone, body=%wide.region_3.0_spmd.clone.sunk | while | flops 605749888 | bytes 11019947 | solution.py:52
  51.1 3.4 multiply_bitcast_fusion.2
  54.5 1.9 copy.37
  57.2 0.8 select_dynamic-update-slice_fusion.2
  58.0 3.4 multiply_bitcast_fusion.2
  61.4 1.9 copy.37
  64.1 0.8 select_dynamic-update-slice_fusion.2
  65.0 3.4 multiply_bitcast_fusion.2
  68.4 1.9 copy.37
  71.9 3.4 multiply_bitcast_fusion.2
  75.3 1.9 copy.37
  78.0 0.8 select_dynamic-update-slice_fusion.2
  79.6 8.5 %all-to-all-start.1 = ((f32[16,8,4]{1,2,0:T(4,128)}), f32[16,8,4]{1,2,0:T(4,128)S(1)}, u32[]{:S(2)}, u32[]{:S(2)}) async-start(f32[16,8,4]{1,2,0:T(4,128)} %copy.27), calls=%async_computation.1 | async-start | bytes 65536 | tf_op jit(solution)/shard_map/all_to_all | solution.py:29
  88.2 10.0 %all-to-all-done.1 = f32[16,8,4]{1,2,0:T(4,128)S(1)} async-done(((f32[16,8,4]{1,2,0:T(4,128)}), f32[16,8,4]{1,2,0:T(4,128)S(1)}, u32[]{:S(2)}, u32[]{:S(2)}) %all-to-all-start.1) | async-done | bytes 2080 | tf_op jit(solution)/shard_map/all_to_all | solution.py:29
  98.2 3.5 all-to-all-start
  101.8 19.0 %all_gather.6 = bf16[2048,128]{1,0:T(8,128)(2,1)S(1)} all-gather(bf16[128,128]{1,0:T(8,128)(2,1)S(1)} %copy-done), channel_id=1, replica_groups=mesh['pb'=16,'ha'=16] {'pb'}, dimensions={0}, use_global_device_ids=true | all-gather | bytes 557056 | tf_op jit(solution)/shard_map/all_gather | solution.py:26
  120.9 2.6 multiply_reduce_fusion.1
  124.0 154.1 %reduce-scatter.3.cloned.1.call-done = f32[8,2048]{1,0:T(8,128)} async-done(((f32[128,2048]{1,0:T(8,128)}), f32[8,2048]{1,0:T(8,128)}) %reduce-scatter.3.cloned.1.call-update) | async-done | bytes 65552 | tf_op jit(solution)/shard_map/reduce_scatter | solution.py:53
  278.1 1.0 reduce_sum.51
  279.1 0.9 subtract_select_fusion
  280.0 3.2 multiply_reduce_fusion
  283.2 1.7 fusion.12
  285.6 6.5 %all-to-all-start.3 = ((f32[8,16,4]{0,2,1:T(4,128)}), f32[8,16,4]{0,2,1:T(4,128)S(1)}, u32[]{:S(2)}, u32[]{:S(2)}) async-start(f32[8,16,4]{0,2,1:T(4,128)} %bitcast.13), calls=%async_computation.5 | async-start | bytes 65536 | tf_op jit(solution)/shard_map/all_to_all | solution.py:80
  293.6 8.5 %all-to-all-done.3 = f32[8,16,4]{0,2,1:T(4,128)S(1)} async-done(((f32[8,16,4]{0,2,1:T(4,128)}), f32[8,16,4]{0,2,1:T(4,128)S(1)}, u32[]{:S(2)}, u32[]{:S(2)}) %all-to-all-start.3) | async-done | bytes 2080 | tf_op jit(solution)/shard_map/all_to_all | solution.py:80
  302.2 3.5 all-to-all-start.2
  306.4 9.4 %all-to-all-done.2 = bf16[8,64,128]{2,0,1:T(8,128)(2,1)S(1)} async-done(((bf16[8,64,128]{2,0,1:T(8,128)(2,1)}), bf16[8,64,128]{2,0,1:T(8,128)(2,1)S(1)}, u32[]{:S(2)}, u32[]{:S(2)}) %all-to-all-start.2) | async-done | bytes 131104 | tf_op jit(solution)/shard_map/all_to_all | solution.py:79
  316.5 28.0 %reduce-scatter.5.cloned.1.call-done = f32[128,128]{1,0:T(8,128)} async-done(((f32[2048,128]{1,0:T(8,128)}), f32[128,128]{1,0:T(8,128)}) %reduce-scatter.5.cloned.1.call-update) | async-done | bytes 65552 | tf_op jit(solution)/shard_map/reduce_scatter | solution.py:76
  344.5 77.6 %psum.7 = bf16[128,128]{1,0:T(8,128)(2,1)} all-reduce(f32[128,128]{1,0:T(8,128)} %reduce-scatter.5.cloned.1.call-done), channel_id=1, replica_groups=mesh['pb'=16,'ha'=16] {'ha'}, use_global_device_ids=true, to_apply=%region_9.10 | all-reduce | flops 16384 | bytes 98304 | tf_op jit(solution)/shard_map/psum | solution.py:77
  (41 shorter events, 9.7 us)
Async XLA Ops:
  7.2 43.9 %copy-start.1 = (s32[128]{0:T(128)S(1)}, s32[128]{0:T(128)}, u32[]{:S(2)}) copy-start(s32[128]{0:T(128)} %param.12) | copy-start | bytes 1540
  7.2 42.7 %all-gather.2.cloned.1.call-start = ((), (), s32[]{:S(2)}) async-start(), calls=%async_computation.6 | async-start | bytes 2785280 | tf_op jit(solution)/shard_map/all_gather | solution.py:25
  8.9 269.1 %reduce-scatter.3.cloned.1.call-start = ((), (), s32[]{:S(2)}) async-start(), calls=%async_computation.7 | async-start | bytes 1114112 | tf_op jit(solution)/shard_map/reduce_scatter | solution.py:53
  51.1 27.9 %copy-start.2 = (f32[128,4]{0,1:T(4,128)S(1)}, f32[128,4]{0,1:T(4,128)}, u32[]{:S(2)}) copy-start(f32[128,4]{0,1:T(4,128)} %param.15) | copy-start | bytes 6148
  51.1 50.7 %copy-start = (bf16[128,128]{1,0:T(8,128)(2,1)S(1)}, bf16[128,128]{1,0:T(8,128)(2,1)}, u32[]{:S(2)}) copy-start(bf16[128,128]{1,0:T(8,128)(2,1)} %param.14) | copy-start | bytes 98308
  79.6 18.6 %all-to-all-start.1 = ((f32[16,8,4]{1,2,0:T(4,128)}), f32[16,8,4]{1,2,0:T(4,128)S(1)}, u32[]{:S(2)}, u32[]{:S(2)}) async-start(f32[16,8,4]{1,2,0:T(4,128)} %copy.27), calls=%async_computation.1 | async-start | bytes 65536 | tf_op jit(solution)/shard_map/all_to_all | solution.py:29
  98.2 22.6 %all-to-all-start = ((bf16[128,4,128]{2,1,0:T(4,128)(2,1)}), bf16[128,4,128]{2,1,0:T(4,128)(2,1)S(1)}, u32[]{:S(2)}, u32[]{:S(2)}) async-start(bf16[128,4,128]{2,1,0:T(4,128)(2,1)} %param.13), calls=%async_computation | async-start | bytes 262144 | tf_op jit(solution)/shard_map/all_to_all | solution.py:28
  101.7 242.7 %reduce-scatter.5.cloned.1.call-start = ((), (), s32[]{:S(2)}) async-start(), calls=%async_computation.8 | async-start | bytes 1114112 | tf_op jit(solution)/shard_map/reduce_scatter | solution.py:76
  285.6 16.5 %all-to-all-start.3 = ((f32[8,16,4]{0,2,1:T(4,128)}), f32[8,16,4]{0,2,1:T(4,128)S(1)}, u32[]{:S(2)}, u32[]{:S(2)}) async-start(f32[8,16,4]{0,2,1:T(4,128)} %bitcast.13), calls=%async_computation.5 | async-start | bytes 65536 | tf_op jit(solution)/shard_map/all_to_all | solution.py:80
  302.2 13.6 %all-to-all-start.2 = ((bf16[8,64,128]{2,0,1:T(8,128)(2,1)}), bf16[8,64,128]{2,0,1:T(8,128)(2,1)S(1)}, u32[]{:S(2)}, u32[]{:S(2)}) async-start(bf16[8,64,128]{2,0,1:T(8,128)(2,1)} %copy.32), calls=%async_computation.3 | async-start | bytes 262144 | tf_op jit(solution)/shard_map/all_to_all | solution.py:79
Sparse Core Ops, SparseCore 0:
  9.9 40.0 all-gather.1
  79.0 199.0 reduce-scatter.2
  285.0 59.4 reduce-scatter.4

commit v2 on v1

--- a/solution.py
+++ b/solution.py
@@ -1,12 +1,17 @@
+import functools
 import math
 
 import jax
 import jax.numpy as jnp
 from jax import lax
+from jax.experimental import pallas as pl
+from jax.experimental.pallas import tpu as pltpu
 from jax.sharding import PartitionSpec as P
 
 main_scale = 192.0 ** (-0.5)
 very_low = -1e30
+MESH = pl.DeviceIdType.MESH
+AXES = ("pb", "ha")
 
 
 def visible(window_start, positions, first_row, width):
@@ -14,20 +19,105 @@
     return (columns[None, :] >= window_start[:, None]) & (columns[None, :] <= positions[:, None])
 
 
+def device_of(axis, peer):
+    return tuple(peer if name == axis else lax.axis_index(name) for name in AXES)
+
+
+def exchange_kernel(axis, count, gather, *refs):
+    x_refs, y_refs = refs[:count], refs[count : 2 * count]
+    send_sem, recv_sem = refs[2 * count], refs[2 * count + 1]
+    n = lax.axis_size(axis)
+    me = lax.axis_index(axis)
+
+    barrier = pltpu.get_barrier_semaphore()
+    for step in range(1, n):
+        peer = lax.rem(me + step, n)
+        pl.semaphore_signal(barrier, inc=1, device_id=device_of(axis, peer), device_id_type=MESH)
+    pl.semaphore_wait(barrier, n - 1)
+
+    copies = []
+    for step in range(1, n):
+        peer = lax.rem(me + step, n)
+        for i in range(count):
+            source = x_refs[i] if gather else x_refs[i].at[peer]
+            copy = pltpu.make_async_remote_copy(
+                src_ref=source,
+                dst_ref=y_refs[i].at[me],
+                send_sem=send_sem.at[i * n + peer],
+                recv_sem=recv_sem.at[i * n + me],
+                device_id=device_of(axis, peer),
+                device_id_type=MESH,
+            )
+            copy.start()
+            copies.append(copy)
+    for i in range(count):
+        y_refs[i][me] = x_refs[i][...] if gather else x_refs[i][me]
+    for step in range(1, n):
+        source_device = lax.rem(me + n - step, n)
+        for i in range(count):
+            copies[(step - 1) * count + i].wait_send()
+            incoming = pltpu.make_async_remote_copy(
+                src_ref=y_refs[i].at[source_device],
+                dst_ref=y_refs[i].at[source_device],
+                send_sem=send_sem.at[i * n + source_device],
+                recv_sem=recv_sem.at[i * n + source_device],
+                device_id=device_of(axis, source_device),
+                device_id_type=MESH,
+            )
+            incoming.wait_recv()
+
+
+def exchange(arrays, axis, collective_id, gather=False):
+    n = lax.axis_size(axis)
+    count = len(arrays)
+    out_shapes = [
+        jax.ShapeDtypeStruct(((n,) + a.shape) if gather else a.shape, a.dtype) for a in arrays
+    ]
+    moved = sum(a.size * a.dtype.itemsize for a in arrays) * (n if gather else 1)
+    return pl.pallas_call(
+        functools.partial(exchange_kernel, axis, count, gather),
+        out_shape=out_shapes,
+        in_specs=[pl.BlockSpec(memory_space=pltpu.VMEM)] * count,
+        out_specs=[pl.BlockSpec(memory_space=pltpu.VMEM)] * count,
+        scratch_shapes=[
+            pltpu.SemaphoreType.DMA((count * n,)),
+            pltpu.SemaphoreType.DMA((count * n,)),
+        ],
+        compiler_params=pltpu.CompilerParams(collective_id=collective_id, has_side_effects=True),
+        cost_estimate=pl.CostEstimate(flops=0, transcendentals=0, bytes_accessed=2 * moved),
+    )(*arrays)
+
+
 def on_device(main_query, latent, log_sums, window_start, index_query, index_key, index_weight):
     query_rows, head_count, latent_width = main_query.shape
     index_width = index_query.shape[2]
+    part_heads = index_query.shape[1]
     groups = lax.axis_size("ha")
-    tokens = query_rows * lax.axis_size("pb")
+    blocks = lax.axis_size("pb")
+    tokens = query_rows * blocks
     own_rows = query_rows // groups
     block_first = lax.axis_index("pb") * query_rows
     flat_query = main_query.reshape(query_rows * head_count, latent_width)
     latent_piece = lax.all_gather(latent, "pb", axis=0, tiled=True)
     keys_all = lax.all_gather(index_key, "pb", axis=0, tiled=True)
 
-    local_index = lax.all_to_all(index_query, "ha", 0, 1, tiled=True)
-    local_weight = lax.all_to_all(index_weight, "ha", 0, 1, tiled=True)
-    index_heads = local_index.shape[1]
+    index_parts, weight_parts = exchange(
+        [
+            index_query.reshape(groups, own_rows * part_heads, index_width),
+            index_weight.reshape(groups, 1, own_rows * part_heads),
+        ],
+        "ha",
+        0,
+    )
+    index_heads = part_heads * groups
+    local_index = (
+        index_parts.reshape(groups, own_rows, part_heads, index_width)
+        .transpose(1, 0, 2, 3)
+        .reshape(own_rows, index_heads, index_width)
+    )
+    local_weight = (
+        weight_parts.reshape(groups, own_rows, part_heads).transpose(1, 0, 2).reshape(own_rows, index_heads)
+    )
     row_first = block_first + lax.axis_index("ha") * own_rows
     own_positions = row_first + jnp.arange(own_rows, dtype=jnp.int32)
     own_start = lax.dynamic_slice_in_dim(window_start, lax.axis_index("ha") * own_rows, own_rows, 0)
@@ -50,7 +140,8 @@
         return lax.dynamic_update_slice_in_dim(probs_inner, head_mass, offset, 1)
 
     probs_part = lax.fori_loop(0, tokens // block_size, one_block, probs_part)
-    probs_all = lax.psum_scatter(probs_part, "ha", scatter_dimension=0, tiled=True)
+    probs_parts = exchange([probs_part.reshape(groups, own_rows, tokens)], "ha", 1)[0]
+    probs_all = jnp.sum(probs_parts, axis=0)
 
     flat_index = local_index.reshape(own_rows * index_heads, index_width)
     active = jnp.einsum("rd,kd->rk", flat_index, keys_all, preferred_element_type=jnp.float32)
@@ -73,11 +164,25 @@
     query_grad = jnp.dot(coeffs, keys_all, preferred_element_type=jnp.float32)
     key_grad = jnp.einsum("rk,rd->kd", coeffs, flat_index, preferred_element_type=jnp.float32)
 
-    key_share = lax.psum_scatter(key_grad, "pb", scatter_dimension=0, tiled=True)
-    key_output = lax.psum(key_share, "ha").astype(jnp.bfloat16)
-    query_grad = query_grad.astype(jnp.bfloat16).reshape(own_rows, index_heads, index_width)
-    query_output = lax.all_to_all(query_grad, "ha", 1, 0, tiled=True)
-    weight_output = lax.all_to_all(weight_grad, "ha", 1, 0, tiled=True)
+    query_grad = query_grad.astype(jnp.bfloat16).reshape(own_rows, groups, part_heads, index_width)
+    query_back, weight_back = exchange(
+        [
+            query_grad.transpose(1, 0, 2, 3).reshape(groups, own_rows * part_heads, index_width),
+            weight_grad.reshape(own_rows, groups, part_heads)
+            .transpose(1, 0, 2)
+            .reshape(groups, 1, own_rows * part_heads),
+        ],
+        "ha",
+        2,
+    )
+    query_output = query_back.reshape(query_rows, part_heads, index_width)
+    weight_output = weight_back.reshape(query_rows, part_heads)
+
+    key_parts = exchange([key_grad.reshape(blocks, query_rows, index_width)], "pb", 3)[0]
+    key_share = jnp.sum(key_parts, axis=0).reshape(groups, own_rows, index_width)
+    key_rows = jnp.sum(exchange([key_share], "ha", 4)[0], axis=0)
+    key_output = exchange([key_rows], "ha", 5, gather=True)[0]
+    key_output = key_output.reshape(query_rows, index_width).astype(jnp.bfloat16)
     return (query_output, key_output, weight_output)
 
 

time: 432 us -> 207 us (0.48)
  waiting for transfers between devices: 248 us -> 0.02 us
  Pallas kernels: 0 us -> 110 us
  blocking collectives: 96.6 us -> 19 us
  starting transfers between devices: 22.2 us -> 0.04 us
  other arithmetic: 11.9 us -> 18.4 us
  local copies, waits for them, and re-layouts: 17.2 us -> 23 us
    reduce_scatter x2 -> x0, waiting for transfers between devices: 182 us -> none  [the longest x1 154 us: on_device(): lax.psum_scatter(probs_part, 'ha', scatter_dimension=0, tiled=True)]
    pallas_call x0 -> x6, Pallas kernels: none -> 110 us  [exchange(): pl.pallas_call(functools.partial(exchange_kernel, axis, count, gather), o...]
    psum x1 -> x0, blocking collectives: 77.6 us -> none  [on_device(): key_output = lax.psum(key_share, 'ha').astype(jnp.bfloat16)]
    all_gather x1, waiting for transfers between devices: 37.9 us -> 0.01 us  [on_device(): latent_piece = lax.all_gather(latent, 'pb', axis=0, tiled=True)]
    all_to_all x4 -> x0, waiting for transfers between devices: 27.9 us -> none  [the longest x1 9.98 us: on_device(): local_weight = lax.all_to_all(index_weight, 'ha', 0, 1, tiled=True)]
    all_to_all x4 -> x0, starting transfers between devices: 22.1 us -> none  [the longest x1 8.5 us: on_device(): local_weight = lax.all_to_all(index_weight, 'ha', 0, 1, tiled=True)]
  transfers between devices with their start and end apart: 7 -> 1, of which waited for: 6 -> 0; matrix products, arithmetic and copies ran while one was open for 2% -> 5% of each run, Pallas kernels for 0% -> 8%
where the time goes in v2:
time: 207 us; the launch traced here: 205 us
  Pallas kernels  110 us (53%)
  local copies, waits for them, and re-layouts  23 us (11%)
  matrix products  20.6 us (10%)
  blocking collectives  19 us (9%)
  other arithmetic  18.4 us (9%)
  between operations  14.2 us (7%)
    pallas_call x6, Pallas kernels, exchange(): pl.pallas_call(functools.partial(exchange_kernel, axis, count, gather), o...  110 us
    all_gather x1, blocking collectives, on_device(): keys_all = lax.all_gather(index_key, 'pb', axis=0, tiled=True)  19 us
    dot_general x4, matrix products, one_block(): jnp.einsum('rd,kd->rk', flat_query, latent_block, preferred_element_type=...  14 us
    mul x4, local copies, waits for them, and re-layouts, one_block(): scores = scores.reshape(query_rows, head_count, block_size) * main_scale  7.68 us
    unnamed x34, local copies, waits for them, and re-layouts  6.87 us
  transfers between devices with their start and end apart: 1, of which 0 were waited for; matrix products, arithmetic and copies ran while one was open for 5% of the time, Pallas kernels for 8%

profile of v2, /device:TPU:8, one launch (start us, length us, event | category | flops | bytes accessed | tf_op | source)
XLA Modules:
  0.0 205.3 jit_solution(16334313353660469957)
XLA Ops:
  7.2 1.7 copy.42
  11.2 16.2 %shard_map.94 = (bf16[16,32,128]{2,1,0:T(8,128)(2,1)}, f32[16,1,32]{2,1,0:T(1,128)}) custom-call(bf16[16,32,128]{2,1,0:T(8,128)(2,1)} %bitcast.68, f32[16,1,32]{2,1,0:T(1,128)} %bitcast.73), custom_call_target="tpu_custom_call" | custom-call | bytes 266240 | tf_op jit(solution)/shard_map/pallas_call | solution.py:77
  27.4 1.0 copy.38
  29.3 2.2 %copy.43 = bf16[128,8,576]{2,1,0:T(8,128)(2,1)S(1)} copy(bf16[128,8,576]{0,2,1:T(8,128)(2,1)} %param.9) | data formatting | bytes 2359296 | tf_op args[0]
  31.7 19.0 %all_gather.6 = bf16[2048,128]{1,0:T(8,128)(2,1)S(1)} all-gather(bf16[128,128]{1,0:T(8,128)(2,1)S(1)} %copy-done.5), channel_id=1, replica_groups=mesh['pb'=16,'ha'=16] {'pb'}, dimensions={0}, use_global_device_ids=true | all-gather | bytes 557056 | tf_op jit(solution)/shard_map/all_gather | solution.py:102
  50.7 2.6 %multiply_reduce_fusion.1 = (f32[8,2048]{1,0:T(8,128)S(1)}, f32[8,64,2048]{2,1,0:T(8,128)}) fusion(f32[8,64]{1,0:T(8,128)S(1)} %copy.41, bf16[8,64,128]{2,1,0:T(8,128)(2,1)S(1)} %bitcast.61, bf16[2048,128]{1,0:T(8,128)(2,1)S(1)} %all_gather.6), kind=kOutput, calls=%fused_computation.12 | convolution fusion | flops 271564800 | bytes 4917248 | tf_op jit(solution)/shard_map/rd,kd->rk/dot_general | solution.py:147
  54.3 1.1 broadcast_in_dim.45
  55.4 28.1 %while.14 = (s32[]{:T(128)}, f32[128,2048]{1,0:T(8,128)}, s32[128]{0:T(128)S(1)}, bf16[2048,576]{1,0:T(8,128)(2,1)}, bf16[1024,576]{1,0:T(8,128)(2,1)S(1)}, /*in...) while((s32[]{:T(128)}, f32[128,2048]{1,0:T(8,128)}, ...), condition=%wide.region_5.6_spmd.clone, body=%wide.region_3.0_spmd.clone.sunk | while | flops 605749888 | bytes 11019947 | solution.py:142
  55.4 3.5 %multiply_bitcast_fusion.2 = f32[1024,512]{0,1:T(8,128)} fusion(bf16[1024,576]{1,0:T(8,128)(2,1)S(1)} %get-tuple-element.272, bf16[2048,576]{1,0:T(8,128)(2,1)} %get-tuple-element.271, s32[]{:T(128)S(6)} %select_n.70), kind=kOutput, calls=%fused_computation.4.clone.1 | convolution fusion | flops 604504064 | bytes 3932164 | tf_op jit(solution)/shard_map/while/body/eval_jaxpr/rd,kd->rk/dot_general | solution.py:133
  58.9 1.9 copy.53
  61.6 0.8 select_dynamic-update-slice_fusion.2
  62.5 3.5 %multiply_bitcast_fusion.2 = f32[1024,512]{0,1:T(8,128)} fusion(bf16[1024,576]{1,0:T(8,128)(2,1)S(1)} %get-tuple-element.272, bf16[2048,576]{1,0:T(8,128)(2,1)} %get-tuple-element.271, s32[]{:T(128)S(6)} %select_n.70), kind=kOutput, calls=%fused_computation.4.clone.1 | convolution fusion | flops 604504064 | bytes 3932164 | tf_op jit(solution)/shard_map/while/body/eval_jaxpr/rd,kd->rk/dot_general | solution.py:133
  66.0 1.9 copy.53
  68.7 0.8 select_dynamic-update-slice_fusion.2
  69.5 3.5 %multiply_bitcast_fusion.2 = f32[1024,512]{0,1:T(8,128)} fusion(bf16[1024,576]{1,0:T(8,128)(2,1)S(1)} %get-tuple-element.272, bf16[2048,576]{1,0:T(8,128)(2,1)} %get-tuple-element.271, s32[]{:T(128)S(6)} %select_n.70), kind=kOutput, calls=%fused_computation.4.clone.1 | convolution fusion | flops 604504064 | bytes 3932164 | tf_op jit(solution)/shard_map/while/body/eval_jaxpr/rd,kd->rk/dot_general | solution.py:133
  73.0 1.9 copy.53
  76.5 3.5 %multiply_bitcast_fusion.2 = f32[1024,512]{0,1:T(8,128)} fusion(bf16[1024,576]{1,0:T(8,128)(2,1)S(1)} %get-tuple-element.272, bf16[2048,576]{1,0:T(8,128)(2,1)} %get-tuple-element.271, s32[]{:T(128)S(6)} %select_n.70), kind=kOutput, calls=%fused_computation.4.clone.1 | convolution fusion | flops 604504064 | bytes 3932164 | tf_op jit(solution)/shard_map/while/body/eval_jaxpr/rd,kd->rk/dot_general | solution.py:133
  80.0 1.9 copy.53
  82.7 0.8 select_dynamic-update-slice_fusion.2
  83.6 33.4 %shard_map.95 = f32[16,8,2048]{2,1,0:T(8,128)} custom-call(f32[16,8,2048]{2,1,0:T(8,128)} %bitcast.60), custom_call_target="tpu_custom_call" | custom-call | bytes 2097152 | tf_op jit(solution)/shard_map/pallas_call | solution.py:77
  117.0 1.6 fusion.12
  118.8 3.2 %multiply_reduce_fusion = (f32[8,64]{1,0:T(8,128)S(1)}, bf16[8,64,2048]{2,1,0:T(8,128)(2,1)S(1)}) fusion(f32[8,64,2048]{2,1,0:T(8,128)} %get-tuple-element.202, f32[8,2048]{1,0:T(8,128)S(1)} %subtract_select_fusion, f32[8,64]{1,0:T(8,128)S(1)} %copy.41), kind=kLoop, calls=%fused_computation.10 | loop fusion | flops 7339520 | bytes 6361088 | tf_op jit(solution)/shard_map/reduce_sum | solution.py:159
  124.2 14.0 %shard_map.96 = (bf16[16,32,128]{2,1,0:T(8,128)(2,1)}, f32[16,1,32]{2,1,0:T(1,128)}) custom-call(bf16[16,32,128]{2,1,0:T(8,128)(2,1)} %bitcast.63, f32[16,1,32]{2,1,0:T(1,128)} %copy.48.refs_1_), custom_call_target="tpu_custom_call" | custom-call | bytes 266240 | tf_op jit(solution)/shard_map/pallas_call | solution.py:77
  138.8 1.4 reduce.4
  140.9 2.5 %copy.49 = bf16[2048,512]{1,0:T(8,128)(2,1)} copy(bf16[2048,512]{0,1:T(8,128)(2,1)S(1)} %bitcast.58) | data formatting | bytes 4194304 | tf_op jit(solution)/shard_map/rk,rd->kd/dot_general | solution.py:165
  143.4 3.3 %fusion.13.refs_0_ = f32[16,128,128]{2,1,0:T(8,128)} fusion(bf16[16,128,512]{2,1,0:T(8,128)(2,1)} %bitcast.59, bf16[512,128,1]{1,0,2:T(8,128)(2,1)S(1)} %bitcast.62), kind=kOutput, calls=%fused_computation.27 | convolution fusion | flops 268435456 | bytes 3276800 | tf_op jit(solution)/shard_map/rk,rd->kd/dot_general | solution.py:165
  146.7 22.1 %shard_map.97 = f32[16,128,128]{2,1,0:T(8,128)} custom-call(f32[16,128,128]{2,1,0:T(8,128)} %fusion.13.refs_0_), custom_call_target="tpu_custom_call" | custom-call | bytes 2097152 | tf_op jit(solution)/shard_map/pallas_call | solution.py:77
  168.8 1.9 reduce_sum.81
  170.7 12.0 %shard_map.98 = f32[16,8,128]{2,1,0:T(8,128)} custom-call(f32[16,8,128]{2,1,0:T(8,128)} %bitcast.65), custom_call_target="tpu_custom_call" | custom-call | bytes 131072 | tf_op jit(solution)/shard_map/pallas_call | solution.py:77
  182.7 1.5 reduce_sum.82.refs_0_
  184.2 12.1 %shard_map.99 = f32[16,8,128]{2,1,0:T(8,128)} custom-call(f32[8,128]{1,0:T(8,128)} %reduce_sum.82.refs_0_), custom_call_target="tpu_custom_call" | custom-call | bytes 131072 | tf_op jit(solution)/shard_map/pallas_call | solution.py:77
  196.3 1.5 convert_bitcast_fusion
  (64 shorter events, 12.5 us)
Async XLA Ops:
  7.2 24.4 %copy-start.6 = (s32[128]{0:T(128)S(1)}, s32[128]{0:T(128)}, u32[]{:S(2)}) copy-start(s32[128]{0:T(128)} %param.12) | copy-start | bytes 1540
  7.2 24.5 %copy-start.5 = (bf16[128,128]{1,0:T(8,128)(2,1)S(1)}, bf16[128,128]{1,0:T(8,128)(2,1)}, u32[]{:S(2)}) copy-start(bf16[128,128]{1,0:T(8,128)(2,1)} %param.14) | copy-start | bytes 98308
  7.2 47.1 %all-gather.2.cloned.1.call-start = ((), (), s32[]{:S(2)}) async-start(), calls=%async_computation | async-start | bytes 2785280 | tf_op jit(solution)/shard_map/all_gather | solution.py:101
  28.4 24.9 %copy-start.2 = (bf16[8,16,4,128]{3,2,1,0:T(4,128)(2,1)}, bf16[8,16,4,128]{3,2,1,0:T(4,128)(2,1)S(1)}, u32[]{:S(2)}) copy-start(bf16[8,16,4,128]{3,2,1,0:T(4,128)(2,1)S(1)} %copy.38) | copy-start | bytes 393220
  31.7 21.9 %copy-start.7 = (s32[8]{0:T(128)}, s32[8]{0:T(128)S(1)}, u32[]{:S(2)}) copy-start(s32[8]{0:T(128)S(1)} %dynamic_slice.10) | copy-start | bytes 100
  31.7 21.9 %copy-start.9 = (s32[8]{0:T(128)}, s32[8]{0:T(128)S(1)}, u32[]{:S(2)}) copy-start(s32[8]{0:T(128)S(1)} %iota_add_fusion.2) | copy-start | bytes 100
  50.7 2.7 %copy-start = (bf16[2048,128]{1,0:T(8,128)(2,1)}, bf16[2048,128]{1,0:T(8,128)(2,1)S(1)}, u32[]{:S(2)}) copy-start(bf16[2048,128]{1,0:T(8,128)(2,1)S(1)} %all_gather.6) | copy-start | bytes 1572868
  53.5 1.9 copy-start.11
  83.6 35.0 %copy-start.8 = (s32[8]{0:T(128)S(1)}, s32[8]{0:T(128)}, u32[]{:S(2)}) copy-start(s32[8]{0:T(128)} %copy-done.7) | copy-start | bytes 100
  83.6 35.0 %copy-start.10 = (s32[8]{0:T(128)S(1)}, s32[8]{0:T(128)}, u32[]{:S(2)}) copy-start(s32[8]{0:T(128)} %copy-done.9) | copy-start | bytes 100
  83.6 35.1 %copy-start.12 = (f32[8]{0:T(128)S(1)}, f32[8]{0:T(128)}, u32[]{:S(2)}) copy-start(f32[8]{0:T(128)} %copy-done.11) | copy-start | bytes 100
  83.6 35.1 %copy-start.13 = (f32[8]{0:T(128)S(1)}, f32[8]{0:T(128)}, u32[]{:S(2)}) copy-start(f32[8]{0:T(128)} %fusion.9) | copy-start | bytes 100
  118.8 3.2 %copy-start.1 = (bf16[2048,128]{1,0:T(8,128)(2,1)S(1)}, bf16[2048,128]{1,0:T(8,128)(2,1)}, u32[]{:S(2)}) copy-start(bf16[2048,128]{1,0:T(8,128)(2,1)} %copy-done) | copy-start | bytes 1572868
  140.9 2.5 %copy-start.3 = (bf16[8,16,4,128]{3,2,1,0:T(4,128)(2,1)S(1)}, bf16[8,16,4,128]{3,2,1,0:T(4,128)(2,1)}, u32[]{:S(2)}) copy-start(bf16[8,16,4,128]{3,2,1,0:T(4,128)(2,1)} %copy-done.2) | copy-start | bytes 393220
  146.7 51.1 %copy-start.4 = (bf16[16,32,128]{2,1,0:T(8,128)(2,1)S(1)}, bf16[16,32,128]{2,1,0:T(8,128)(2,1)}, u32[]{:S(2)}) copy-start(bf16[16,32,128]{2,1,0:T(8,128)(2,1)} %get-tuple-element.134) | copy-start | bytes 393220
Sparse Core Ops, SparseCore 0:
  9.9 41.9 all-gather.1

commit v3 on v2

--- a/solution.py
+++ b/solution.py
@@ -23,7 +23,7 @@
     return tuple(peer if name == axis else lax.axis_index(name) for name in AXES)
 
 
-def exchange_kernel(axis, count, gather, *refs):
+def exchange_kernel(axis, count, gathers, *refs):
     x_refs, y_refs = refs[:count], refs[count : 2 * count]
     send_sem, recv_sem = refs[2 * count], refs[2 * count + 1]
     n = lax.axis_size(axis)
@@ -39,7 +39,7 @@
     for step in range(1, n):
         peer = lax.rem(me + step, n)
         for i in range(count):
-            source = x_refs[i] if gather else x_refs[i].at[peer]
+            source = x_refs[i] if gathers[i] else x_refs[i].at[peer]
             copy = pltpu.make_async_remote_copy(
                 src_ref=source,
                 dst_ref=y_refs[i].at[me],
@@ -51,7 +51,7 @@
             copy.start()
             copies.append(copy)
     for i in range(count):
-        y_refs[i][me] = x_refs[i][...] if gather else x_refs[i][me]
+        y_refs[i][me] = x_refs[i][...] if gathers[i] else x_refs[i][me]
     for step in range(1, n):
         source_device = lax.rem(me + n - step, n)
         for i in range(count):
@@ -67,15 +67,16 @@
             incoming.wait_recv()
 
 
-def exchange(arrays, axis, collective_id, gather=False):
+def exchange(arrays, axis, collective_id, gathers=None):
     n = lax.axis_size(axis)
     count = len(arrays)
+    gathers = tuple(gathers or (False,) * count)
     out_shapes = [
-        jax.ShapeDtypeStruct(((n,) + a.shape) if gather else a.shape, a.dtype) for a in arrays
+        jax.ShapeDtypeStruct(((n,) + a.shape) if g else a.shape, a.dtype) for a, g in zip(arrays, gathers)
     ]
-    moved = sum(a.size * a.dtype.itemsize for a in arrays) * (n if gather else 1)
+    moved = sum(a.size * a.dtype.itemsize * (n if g else 1) for a, g in zip(arrays, gathers))
     return pl.pallas_call(
-        functools.partial(exchange_kernel, axis, count, gather),
+        functools.partial(exchange_kernel, axis, count, gathers),
         out_shape=out_shapes,
         in_specs=[pl.BlockSpec(memory_space=pltpu.VMEM)] * count,
         out_specs=[pl.BlockSpec(memory_space=pltpu.VMEM)] * count,
@@ -86,6 +87,43 @@
         compiler_params=pltpu.CompilerParams(collective_id=collective_id, has_side_effects=True),
         cost_estimate=pl.CostEstimate(flops=0, transcendentals=0, bytes_accessed=2 * moved),
     )(*arrays)
+
+
+def head_mass_kernel(query_ref, latent_ref, sums_ref, start_ref, position_ref, out_ref):
+    rows, width = out_ref.shape
+    scores = lax.dot_general(
+        query_ref[...], latent_ref[...], (((1,), (1,)), ((), ())), preferred_element_type=jnp.float32
+    )
+    mass = jnp.exp(scores * main_scale - sums_ref[...])
+    mass = jnp.sum(mass.reshape(rows, mass.shape[0] // rows, width), axis=1)
+    columns = pl.program_id(0) * width + lax.broadcasted_iota(jnp.int32, (rows, width), 1)
+    seen = (columns >= start_ref[...]) & (columns <= position_ref[...])
+    out_ref[...] = jnp.where(seen, mass, 0.0)
+
+
+def head_mass(flat_query, latent_piece, flat_sums, window_start, positions):
+    query_rows = window_start.shape[0]
+    tokens, latent_width = latent_piece.shape
+    width = math.gcd(tokens, 256)
+    flat_rows = flat_query.shape[0]
+    return pl.pallas_call(
+        head_mass_kernel,
+        out_shape=jax.ShapeDtypeStruct((query_rows, tokens), jnp.float32),
+        grid=(tokens // width,),
+        in_specs=[
+            pl.BlockSpec((flat_rows, latent_width), lambda k: (0, 0)),
+            pl.BlockSpec((width, latent_width), lambda k: (k, 0)),
+            pl.BlockSpec((flat_rows, 1), lambda k: (0, 0)),
+            pl.BlockSpec((query_rows, 1), lambda k: (0, 0)),
+            pl.BlockSpec((query_rows, 1), lambda k: (0, 0)),
+        ],
+        out_specs=pl.BlockSpec((query_rows, width), lambda k: (0, k)),
+        cost_estimate=pl.CostEstimate(
+            flops=2 * flat_rows * tokens * latent_width,
+            transcendentals=flat_rows * tokens,
+            bytes_accessed=flat_query.size * 2 + latent_piece.size * 2 + query_rows * tokens * 4,
+        ),
+    )(flat_query, latent_piece, flat_sums, window_start[:, None], positions[:, None])
 
 
 def on_device(main_query, latent, log_sums, window_start, index_query, index_key, index_weight):
@@ -96,20 +134,27 @@
     blocks = lax.axis_size("pb")
     tokens = query_rows * blocks
     own_rows = query_rows // groups
+    index_heads = part_heads * groups
     block_first = lax.axis_index("pb") * query_rows
     flat_query = main_query.reshape(query_rows * head_count, latent_width)
     latent_piece = lax.all_gather(latent, "pb", axis=0, tiled=True)
     keys_all = lax.all_gather(index_key, "pb", axis=0, tiled=True)
 
-    index_parts, weight_parts = exchange(
+    positions = block_first + jnp.arange(query_rows, dtype=jnp.int32)
+    probs_part = head_mass(
+        flat_query, latent_piece, log_sums.reshape(query_rows * head_count, 1), window_start, positions
+    )
+
+    probs_parts, index_parts, weight_parts = exchange(
         [
+            probs_part.reshape(groups, own_rows, tokens),
             index_query.reshape(groups, own_rows * part_heads, index_width),
             index_weight.reshape(groups, 1, own_rows * part_heads),
         ],
         "ha",
         0,
     )
-    index_heads = part_heads * groups
+    probs_all = jnp.sum(probs_parts, axis=0)
     local_index = (
         index_parts.reshape(groups, own_rows, part_heads, index_width)
         .transpose(1, 0, 2, 3)
@@ -121,27 +166,6 @@
     row_first = block_first + lax.axis_index("ha") * own_rows
     own_positions = row_first + jnp.arange(own_rows, dtype=jnp.int32)
     own_start = lax.dynamic_slice_in_dim(window_start, lax.axis_index("ha") * own_rows, own_rows, 0)
-
-    positions = block_first + jnp.arange(query_rows, dtype=jnp.int32)
-    probs_part = jnp.zeros((query_rows, tokens), jnp.float32)
-    block_size = math.gcd(tokens, 512)
-
-    def one_block(block_index, probs_inner):
-        offset = block_index * block_size
-        latent_block = lax.dynamic_slice_in_dim(latent_piece, offset, block_size, 0)
-        visible_mask = visible(window_start, positions, offset, block_size)
-        scores = jnp.einsum(
-            "rd,kd->rk", flat_query, latent_block, preferred_element_type=jnp.float32
-        )
-        scores = scores.reshape(query_rows, head_count, block_size) * main_scale
-        head_mass = jnp.where(
-            visible_mask, jnp.sum(jnp.exp(scores - log_sums[:, :, None]), axis=1), 0.0
-        )
-        return lax.dynamic_update_slice_in_dim(probs_inner, head_mass, offset, 1)
-
-    probs_part = lax.fori_loop(0, tokens // block_size, one_block, probs_part)
-    probs_parts = exchange([probs_part.reshape(groups, own_rows, tokens)], "ha", 1)[0]
-    probs_all = jnp.sum(probs_parts, axis=0)
 
     flat_index = local_index.reshape(own_rows * index_heads, index_width)
     active = jnp.einsum("rd,kd->rk", flat_index, keys_all, preferred_element_type=jnp.float32)
@@ -164,24 +188,25 @@
     query_grad = jnp.dot(coeffs, keys_all, preferred_element_type=jnp.float32)
     key_grad = jnp.einsum("rk,rd->kd", coeffs, flat_index, preferred_element_type=jnp.float32)
 
+    key_parts = exchange([key_grad.reshape(blocks, query_rows, index_width)], "pb", 1)[0]
+    key_share = jnp.sum(key_parts, axis=0).reshape(groups, own_rows, index_width)
+
     query_grad = query_grad.astype(jnp.bfloat16).reshape(own_rows, groups, part_heads, index_width)
-    query_back, weight_back = exchange(
+    query_back, weight_back, key_rows = exchange(
         [
             query_grad.transpose(1, 0, 2, 3).reshape(groups, own_rows * part_heads, index_width),
             weight_grad.reshape(own_rows, groups, part_heads)
             .transpose(1, 0, 2)
             .reshape(groups, 1, own_rows * part_heads),
+            key_share,
         ],
         "ha",
         2,
     )
     query_output = query_back.reshape(query_rows, part_heads, index_width)
     weight_output = weight_back.reshape(query_rows, part_heads)
-
-    key_parts = exchange([key_grad.reshape(blocks, query_rows, index_width)], "pb", 3)[0]
-    key_share = jnp.sum(key_parts, axis=0).reshape(groups, own_rows, index_width)
-    key_rows = jnp.sum(exchange([key_share], "ha", 4)[0], axis=0)
-    key_output = exchange([key_rows], "ha", 5, gather=True)[0]
+    key_rows = jnp.sum(key_rows, axis=0)
+    key_output = exchange([key_rows], "ha", 3, gathers=(True,))[0]
     key_output = key_output.reshape(query_rows, index_width).astype(jnp.bfloat16)
     return (query_output, key_output, weight_output)
 

time: 207 us -> 177 us (0.86)
  matrix products: 20.6 us -> 4.72 us
  Pallas kernels: 110 us -> 95.6 us
  waiting for transfers between devices: 0.02 us -> 13.9 us
  other arithmetic: 18.4 us -> 8.69 us
  local copies, waits for them, and re-layouts: 23 us -> 18.8 us
    pallas_call x6 -> x5, Pallas kernels: 110 us -> 95.6 us  [the longest x4 86.2 us: exchange(): pl.pallas_call(functools.partial(exchange_kernel, axis, count, gathers),...]
    dot_general x4 -> x0, matrix products: 14 us -> none  [one_block(): jnp.einsum('rd,kd->rk', flat_query, latent_block, preferred_element_type=...]
    all_gather x1, waiting for transfers between devices: 0.01 us -> 13.9 us  [on_device(): latent_piece = lax.all_gather(latent, 'pb', axis=0, tiled=True)]
    mul x4 -> x0, local copies, waits for them, and re-layouts: 7.68 us -> none  [one_block(): scores = scores.reshape(query_rows, head_count, block_size) * main_scale]
    dynamic_update_slice x4 -> x0, other arithmetic: 3.29 us -> none  [one_block(): return lax.dynamic_update_slice_in_dim(probs_inner, head_mass, offset, 1)]
    reduce_sum x5 -> x1, other arithmetic: 4.52 us -> 1.45 us  [on_device(): key_rows = jnp.sum(key_rows, axis=0)]
    reduce_sum x1, other arithmetic: 3.22 us -> 0.97 us  [on_device(): weight_grad = jnp.sum(logit_grad[:, None, :] * relu_act, axis=2)]
    unnamed x34 -> x8, local copies, waits for them, and re-layouts: 6.87 us -> 8.42 us
  transfers between devices with their start and end apart: 1 -> 1, of which waited for: 0 -> 1; matrix products, arithmetic and copies ran while one was open for 5% -> 5% of each run, Pallas kernels for 8% -> 0%
where the time goes in v3:
time: 177 us; the launch traced here: 176 us
  Pallas kernels  95.6 us (54%)
  blocking collectives  19.8 us (11%)
  local copies, waits for them, and re-layouts  18.8 us (11%)
  between operations  14.1 us (8%)
  waiting for transfers between devices  13.9 us (8%)
  other arithmetic  8.69 us (5%)
  matrix products  4.72 us (3%)
    pallas_call x4, Pallas kernels, exchange(): pl.pallas_call(functools.partial(exchange_kernel, axis, count, gathers),...  86.2 us
    all_gather x1, blocking collectives, on_device(): keys_all = lax.all_gather(index_key, 'pb', axis=0, tiled=True)  19.8 us
    all_gather x1, waiting for transfers between devices, on_device(): latent_piece = lax.all_gather(latent, 'pb', axis=0, tiled=True)  13.9 us
    pallas_call x1, Pallas kernels, head_mass(): pl.pallas_call(head_mass_kernel, out_shape=jax.ShapeDtypeStruct((query_ro...  9.4 us
    unnamed x8, local copies, waits for them, and re-layouts  8.42 us
  transfers between devices with their start and end apart: 1, of which 1 were waited for; matrix products, arithmetic and copies ran while one was open for 5% of the time, Pallas kernels for 0%

profile of v3, /device:TPU:8, one launch (start us, length us, event | category | flops | bytes accessed | tf_op | source)
XLA Modules:
  0.0 175.6 jit_solution(11166249512607426074)
XLA Ops:
  7.2 1.7 copy.38
  8.9 2.9 %copy.37 = bf16[128,8,576]{2,1,0:T(8,128)(2,1)} copy(bf16[128,8,576]{0,2,1:T(8,128)(2,1)} %param.7) | data formatting | bytes 2359296 | tf_op args[0]
  11.8 0.8 copy.39
  12.6 1.0 reshape.167.sums_ref
  13.6 1.4 copy.41.start_ref
  15.0 0.8 copy.42
  15.8 0.7 reshape.154
  16.5 0.7 dynamic_slice.3
  17.2 0.6 iota_add_fusion.position_ref
  17.8 19.8 %all_gather.7 = bf16[2048,128]{1,0:T(8,128)(2,1)S(1)} all-gather(bf16[128,128]{1,0:T(8,128)(2,1)} %param.12), channel_id=1, replica_groups=mesh['pb'=16,'ha'=16] {'pb'}, dimensions={0}, use_global_device_ids=true | all-gather | bytes 557056 | tf_op jit(solution)/shard_map/all_gather | solution.py:141
  37.6 13.9 %all-gather.2.cloned.1.call-done.latent_ref = bf16[2048,576]{1,0:T(8,128)(2,1)} async-done(((bf16[128,576]{1,0:T(8,128)(2,1)}), bf16[2048,576]{1,0:T(8,128)(2,1)}) %all-gather.2.cloned.1.call-update) | async-done | bytes 2359312 | tf_op jit(solution)/shard_map/all_gather | solution.py:140
  51.5 9.4 %shard_map.94 = f32[128,2048]{1,0:T(8,128)} custom-call(bf16[1024,576]{1,0:T(8,128)(2,1)} %bitcast.45, bf16[2048,576]{1,0:T(8,128)(2,1)} %all-gather.2.cloned.1.call-done.latent_ref, f32[1024,1]{1,0:T(8,128)} %reshape.167.sums_ref, s32[128,1]{1,0:T(8,128)} %copy.41.start_ref, s32[128,1]{1,0:T(8,128)} %iota_add_fusion.position_ref), custom_call_target="tpu_custom_call" | custom-call | flops 2415919104 | bytes 4587520 | tf_op jit(solution)/shard_map/pallas_call | solution.py:109
  60.9 37.0 %shard_map.95 = (f32[16,8,2048]{2,1,0:T(8,128)}, bf16[16,32,128]{2,1,0:T(8,128)(2,1)}, f32[16,1,32]{2,1,0:T(1,128)}) custom-call(f32[16,8,2048]{2,1,0:T(8,128)} %bitcast.48, bf16[16,32,128]{2,1,0:T(8,128)(2,1)} %bitcast.52, f32[16,1,32]{2,1,0:T(1,128)} %bitcast.59), custom_call_target="tpu_custom_call" | custom-call | bytes 2363392 | tf_op jit(solution)/shard_map/pallas_call | solution.py:78
  97.9 1.0 copy.44
  98.9 0.8 copy.45
  99.8 0.7 multiply_reduce_fusion.1
  101.5 1.0 multiply_reduce_fusion
  102.5 2.5 %copy.51 = bf16[2048,512]{1,0:T(8,128)(2,1)} copy(bf16[2048,512]{0,1:T(8,128)(2,1)S(1)} %bitcast.42) | data formatting | bytes 4194304 | tf_op jit(solution)/shard_map/rk,rd->kd/dot_general | solution.py:189
  105.0 3.3 %fusion.7.refs_0_ = f32[16,128,128]{2,1,0:T(8,128)} fusion(bf16[16,128,512]{2,1,0:T(8,128)(2,1)} %bitcast.44, bf16[512,128,1]{1,0,2:T(8,128)(2,1)S(1)} %bitcast.47), kind=kOutput, calls=%fused_computation.18 | convolution fusion | flops 268435456 | bytes 3276800 | tf_op jit(solution)/shard_map/rk,rd->kd/dot_general | solution.py:189
  108.2 21.4 %shard_map.96 = f32[16,128,128]{2,1,0:T(8,128)} custom-call(f32[16,128,128]{2,1,0:T(8,128)} %fusion.7.refs_0_), custom_call_target="tpu_custom_call" | custom-call | bytes 2097152 | tf_op jit(solution)/shard_map/pallas_call | solution.py:78
  129.6 0.7 convolution_convert_fusion
  130.3 0.7 copy.48
  131.2 0.7 copy.53.refs_1_
  131.9 1.9 %reduce_sum.68 = f32[128,128]{1,0:T(8,128)} reduce(f32[16,128,128]{2,1,0:T(8,128)} %shard_map.96, f32[]{:T(128)} %constant.5.clone.1), dimensions={0}, to_apply=%region_6.7 | reduce | flops 245760 | bytes 1114116 | tf_op jit(solution)/shard_map/reduce_sum | solution.py:192
  133.8 15.7 %shard_map.97 = (bf16[16,32,128]{2,1,0:T(8,128)(2,1)}, f32[16,1,32]{2,1,0:T(1,128)}, f32[16,8,128]{2,1,0:T(8,128)}) custom-call(bf16[16,32,128]{2,1,0:T(8,128)(2,1)} %bitcast.49, f32[16,1,32]{2,1,0:T(1,128)} %copy.53.refs_1_, f32[16,8,128]{2,1,0:T(8,128)} %bitcast.51), custom_call_target="tpu_custom_call" | custom-call | bytes 397312 | tf_op jit(solution)/shard_map/pallas_call | solution.py:78
  149.5 1.5 reduce_sum.69.refs_0_
  150.9 12.1 %shard_map.98 = f32[16,8,128]{2,1,0:T(8,128)} custom-call(f32[8,128]{1,0:T(8,128)} %reduce_sum.69.refs_0_), custom_call_target="tpu_custom_call" | custom-call | bytes 131072 | tf_op jit(solution)/shard_map/pallas_call | solution.py:78
  163.1 1.5 convert_bitcast_fusion
  164.6 0.5 broadcast.73
  165.1 1.4 reduce.4
  166.5 0.7 copy.54
  167.2 1.6 copy.56
  (14 shorter events, 1.4 us)
Async XLA Ops:
  7.2 44.3 %all-gather.2.cloned.1.call-start = ((), (), s32[]{:S(2)}) async-start(), calls=%async_computation | async-start | bytes 2785280 | tf_op jit(solution)/shard_map/all_gather | solution.py:140
  97.9 3.1 %copy-start = (f32[16,8,2048]{2,1,0:T(8,128)S(1)}, f32[16,8,2048]{2,1,0:T(8,128)}, u32[]{:S(2)}) copy-start(f32[16,8,2048]{2,1,0:T(8,128)} %get-tuple-element.11) | copy-start | bytes 3145732
Sparse Core Ops, SparseCore 0:
  9.8 41.5 all-gather.1

commit v4 on v3

--- a/solution.py
+++ b/solution.py
@@ -23,68 +23,83 @@
     return tuple(peer if name == axis else lax.axis_index(name) for name in AXES)
 
 
-def exchange_kernel(axis, count, gathers, *refs):
+def exchange_kernel(items, *refs):
+    count = len(items)
     x_refs, y_refs = refs[:count], refs[count : 2 * count]
     send_sem, recv_sem = refs[2 * count], refs[2 * count + 1]
-    n = lax.axis_size(axis)
-    me = lax.axis_index(axis)
+    axes = sorted({axis for axis, _ in items})
+    stride = max(lax.axis_size(axis) for axis in axes)
 
     barrier = pltpu.get_barrier_semaphore()
-    for step in range(1, n):
-        peer = lax.rem(me + step, n)
-        pl.semaphore_signal(barrier, inc=1, device_id=device_of(axis, peer), device_id_type=MESH)
-    pl.semaphore_wait(barrier, n - 1)
-
-    copies = []
-    for step in range(1, n):
-        peer = lax.rem(me + step, n)
-        for i in range(count):
-            source = x_refs[i] if gathers[i] else x_refs[i].at[peer]
+    for axis in axes:
+        n = lax.axis_size(axis)
+        me = lax.axis_index(axis)
+        for step in range(1, n):
+            peer = lax.rem(me + step, n)
+            pl.semaphore_signal(barrier, inc=1, device_id=device_of(axis, peer), device_id_type=MESH)
+    pl.semaphore_wait(barrier, sum(lax.axis_size(axis) - 1 for axis in axes))
+
+    copies = {}
+    for step in range(1, max(lax.axis_size(axis) for axis in axes)):
+        for i, (axis, gather) in enumerate(items):
+            n = lax.axis_size(axis)
+            if step >= n:
+                continue
+            me = lax.axis_index(axis)
+            peer = lax.rem(me + step, n)
+            source = x_refs[i] if gather else x_refs[i].at[peer]
             copy = pltpu.make_async_remote_copy(
                 src_ref=source,
                 dst_ref=y_refs[i].at[me],
-                send_sem=send_sem.at[i * n + peer],
-                recv_sem=recv_sem.at[i * n + me],
+                send_sem=send_sem.at[i * stride + peer],
+                recv_sem=recv_sem.at[i * stride + me],
                 device_id=device_of(axis, peer),
                 device_id_type=MESH,
             )
             copy.start()
-            copies.append(copy)
-    for i in range(count):
-        y_refs[i][me] = x_refs[i][...] if gathers[i] else x_refs[i][me]
-    for step in range(1, n):
-        source_device = lax.rem(me + n - step, n)
-        for i in range(count):
-            copies[(step - 1) * count + i].wait_send()
+            copies[(i, step)] = copy
+    for i, (axis, gather) in enumerate(items):
+        me = lax.axis_index(axis)
+        y_refs[i][me] = x_refs[i][...] if gather else x_refs[i][me]
+    for step in range(1, max(lax.axis_size(axis) for axis in axes)):
+        for i, (axis, gather) in enumerate(items):
+            n = lax.axis_size(axis)
+            if step >= n:
+                continue
+            me = lax.axis_index(axis)
+            source_device = lax.rem(me + n - step, n)
+            copies[(i, step)].wait_send()
             incoming = pltpu.make_async_remote_copy(
                 src_ref=y_refs[i].at[source_device],
                 dst_ref=y_refs[i].at[source_device],
-                send_sem=send_sem.at[i * n + source_device],
-                recv_sem=recv_sem.at[i * n + source_device],
+                send_sem=send_sem.at[i * stride + source_device],
+                recv_sem=recv_sem.at[i * stride + source_device],
                 device_id=device_of(axis, source_device),
                 device_id_type=MESH,
             )
             incoming.wait_recv()
 
 
-def exchange(arrays, axis, collective_id, gathers=None):
-    n = lax.axis_size(axis)
+def exchange(arrays, items, collective_id):
     count = len(arrays)
-    gathers = tuple(gathers or (False,) * count)
+    items = tuple(items)
     out_shapes = [
-        jax.ShapeDtypeStruct(((n,) + a.shape) if g else a.shape, a.dtype) for a, g in zip(arrays, gathers)
+        jax.ShapeDtypeStruct(((lax.axis_size(axis),) + a.shape) if g else a.shape, a.dtype)
+        for a, (axis, g) in zip(arrays, items)
     ]
-    moved = sum(a.size * a.dtype.itemsize * (n if g else 1) for a, g in zip(arrays, gathers))
+    moved = sum(
+        a.size * a.dtype.itemsize * (lax.axis_size(axis) if g else 1) for a, (axis, g) in zip(arrays, items)
+    )
+    slots = count * max(lax.axis_size(axis) for axis, _ in items)
     return pl.pallas_call(
-        functools.partial(exchange_kernel, axis, count, gathers),
+        functools.partial(exchange_kernel, items),
         out_shape=out_shapes,
         in_specs=[pl.BlockSpec(memory_space=pltpu.VMEM)] * count,
         out_specs=[pl.BlockSpec(memory_space=pltpu.VMEM)] * count,
-        scratch_shapes=[
-            pltpu.SemaphoreType.DMA((count * n,)),
-            pltpu.SemaphoreType.DMA((count * n,)),
-        ],
-        compiler_params=pltpu.CompilerParams(collective_id=collective_id, has_side_effects=True),
+        scratch_shapes=[pltpu.SemaphoreType.DMA((slots,)), pltpu.SemaphoreType.DMA((slots,))],
+        compiler_params=pltpu.CompilerParams(
+            collective_id=collective_id, has_side_effects=True, vmem_limit_bytes=48 * 1024 * 1024
+        ),
         cost_estimate=pl.CostEstimate(flops=0, transcendentals=0, bytes_accessed=2 * moved),
     )(*arrays)
 
@@ -135,26 +150,31 @@
     tokens = query_rows * blocks
     own_rows = query_rows // groups
     index_heads = part_heads * groups
+    all_heads = head_count * groups
     block_first = lax.axis_index("pb") * query_rows
-    flat_query = main_query.reshape(query_rows * head_count, latent_width)
-    latent_piece = lax.all_gather(latent, "pb", axis=0, tiled=True)
-    keys_all = lax.all_gather(index_key, "pb", axis=0, tiled=True)
-
-    positions = block_first + jnp.arange(query_rows, dtype=jnp.int32)
-    probs_part = head_mass(
-        flat_query, latent_piece, log_sums.reshape(query_rows * head_count, 1), window_start, positions
-    )
-
-    probs_parts, index_parts, weight_parts = exchange(
+
+    latent_parts, key_parts, query_parts, sums_parts, index_parts, weight_parts = exchange(
         [
-            probs_part.reshape(groups, own_rows, tokens),
+            latent,
+            index_key,
+            main_query.reshape(groups, own_rows * head_count, latent_width),
+            log_sums.reshape(groups, 1, own_rows * head_count),
             index_query.reshape(groups, own_rows * part_heads, index_width),
             index_weight.reshape(groups, 1, own_rows * part_heads),
         ],
-        "ha",
+        [("pb", True), ("pb", True), ("ha", False), ("ha", False), ("ha", False), ("ha", False)],
         0,
     )
-    probs_all = jnp.sum(probs_parts, axis=0)
+    latent_piece = latent_parts.reshape(tokens, latent_width)
+    keys_all = key_parts.reshape(tokens, index_width)
+    local_query = (
+        query_parts.reshape(groups, own_rows, head_count, latent_width)
+        .transpose(1, 0, 2, 3)
+        .reshape(own_rows * all_heads, latent_width)
+    )
+    local_sums = (
+        sums_parts.reshape(groups, own_rows, head_count).transpose(1, 0, 2).reshape(own_rows * all_heads, 1)
+    )
     local_index = (
         index_parts.reshape(groups, own_rows, part_heads, index_width)
         .transpose(1, 0, 2, 3)
@@ -166,6 +186,8 @@
     row_first = block_first + lax.axis_index("ha") * own_rows
     own_positions = row_first + jnp.arange(own_rows, dtype=jnp.int32)
     own_start = lax.dynamic_slice_in_dim(window_start, lax.axis_index("ha") * own_rows, own_rows, 0)
+
+    probs_all = head_mass(local_query, latent_piece, local_sums, own_start, own_positions)
 
     flat_index = local_index.reshape(own_rows * index_heads, index_width)
     active = jnp.einsum("rd,kd->rk", flat_index, keys_all, preferred_element_type=jnp.float32)
@@ -188,25 +210,23 @@
     query_grad = jnp.dot(coeffs, keys_all, preferred_element_type=jnp.float32)
     key_grad = jnp.einsum("rk,rd->kd", coeffs, flat_index, preferred_element_type=jnp.float32)
 
-    key_parts = exchange([key_grad.reshape(blocks, query_rows, index_width)], "pb", 1)[0]
-    key_share = jnp.sum(key_parts, axis=0).reshape(groups, own_rows, index_width)
-
     query_grad = query_grad.astype(jnp.bfloat16).reshape(own_rows, groups, part_heads, index_width)
-    query_back, weight_back, key_rows = exchange(
+    key_parts, query_back, weight_back = exchange(
         [
+            key_grad.reshape(blocks, query_rows, index_width),
             query_grad.transpose(1, 0, 2, 3).reshape(groups, own_rows * part_heads, index_width),
             weight_grad.reshape(own_rows, groups, part_heads)
             .transpose(1, 0, 2)
             .reshape(groups, 1, own_rows * part_heads),
-            key_share,
         ],
-        "ha",
-        2,
+        [("pb", False), ("ha", False), ("ha", False)],
+        1,
     )
     query_output = query_back.reshape(query_rows, part_heads, index_width)
     weight_output = weight_back.reshape(query_rows, part_heads)
-    key_rows = jnp.sum(key_rows, axis=0)
-    key_output = exchange([key_rows], "ha", 3, gathers=(True,))[0]
+    key_share = jnp.sum(key_parts, axis=0).reshape(groups, own_rows, index_width)
+    key_rows = jnp.sum(exchange([key_share], [("ha", False)], 2)[0], axis=0)
+    key_output = exchange([key_rows], [("ha", True)], 3)[0]
     key_output = key_output.reshape(query_rows, index_width).astype(jnp.bfloat16)
     return (query_output, key_output, weight_output)
 

time: 177 us -> 153 us (0.86)
  Pallas kernels: 95.6 us -> 127 us
  blocking collectives: 19.8 us -> 0 us
  waiting for transfers between devices: 13.9 us -> 0 us
  between operations: 14.1 us -> 0.76 us
  other arithmetic: 8.69 us -> 4.49 us
  local copies, waits for them, and re-layouts: 18.8 us -> 16.2 us
    pallas_call x4, Pallas kernels: 86.2 us -> 119 us  [exchange(): pl.pallas_call(functools.partial(exchange_kernel, items), out_shape=out_s...]
    all_gather x1 -> x0, blocking collectives: 19.8 us -> none  [on_device(): keys_all = lax.all_gather(index_key, 'pb', axis=0, tiled=True)]
    all_gather x1 -> x0, waiting for transfers between devices: 13.9 us -> none  [on_device(): latent_piece = lax.all_gather(latent, 'pb', axis=0, tiled=True)]
    reduce_sum x1, other arithmetic: 1.9 us -> 0.06 us  [on_device(): jnp.sum(key_parts, axis=0).reshape(groups, own_rows, index_width)]
    unnamed x8 -> x12, local copies, waits for them, and re-layouts: 8.42 us -> 7.83 us
  transfers between devices with their start and end apart: 1 -> 0, of which waited for: 1 -> 0; matrix products, arithmetic and copies ran while one was open for 5% -> 0% of each run, Pallas kernels for 0% -> 0%
where the time goes in v4:
time: 153 us; the launch traced here: 152 us
  Pallas kernels  127 us (83%)
  local copies, waits for them, and re-layouts  16.2 us (11%)
  other arithmetic  4.49 us (3%)
  matrix products  3.72 us (2%)
    pallas_call x4, Pallas kernels, exchange(): pl.pallas_call(functools.partial(exchange_kernel, items), out_shape=out_s...  119 us
    pallas_call x1, Pallas kernels, head_mass(): pl.pallas_call(head_mass_kernel, out_shape=jax.ShapeDtypeStruct((query_ro...  8.43 us
    unnamed x12, local copies, waits for them, and re-layouts  7.83 us

profile of v4, /device:TPU:8, one launch (start us, length us, event | category | flops | bytes accessed | tf_op | source)
XLA Modules:
  0.0 152.3 jit_solution(7336775795200507283)
XLA Ops:
  0.6 0.7 dynamic_slice.3
  1.4 0.7 dynamic-slice_bitcast_fusion
  2.1 0.6 iota_add_fusion.position_ref
  2.7 0.7 copy.57.start_ref
  3.4 0.8 copy.44
  4.2 0.8 copy.45
  5.1 1.1 copy.46.refs_0_
  6.2 2.2 %copy.43 = bf16[128,8,576]{2,1,0:T(8,128)(2,1)S(1)} copy(bf16[128,8,576]{0,2,1:T(8,128)(2,1)} %param.7) | data formatting | bytes 2359296 | tf_op args[0]
  8.4 0.9 copy-done
  9.3 0.8 copy-done.1
  10.1 77.9 %shard_map.94 = (bf16[16,128,576]{2,1,0:T(8,128)(2,1)}, bf16[16,128,128]{2,1,0:T(8,128)(2,1)S(1)}, bf16[16,64,576]{2,1,0:T(8,128)(2,1)S(1)}, f32[16,1,64]{2,1,0:...) custom-call(bf16[128,576]{1,0:T(8,128)(2,1)S(1)} %copy.46.refs_0_, ...), custom_call_target="tpu_custom_call" | custom-call | bytes 8400896 | tf_op jit(solution)/shard_map/pallas_call | solution.py:94
  88.1 0.1 copy.51
  88.4 1.0 reshape.109.sums_ref
  89.4 1.2 copy.53
  90.6 8.4 %shard_map.95 = f32[8,2048]{1,0:T(8,128)} custom-call(bf16[1024,576]{1,0:T(8,128)(2,1)} %bitcast.64, bf16[2048,576]{1,0:T(8,128)(2,1)} %bitcast.73, f32[1024,1]{1,0:T(8,128)} %reshape.109.sums_ref, s32[8,1]{1,0:T(8,128)} %copy.57.start_ref, s32[8,1]{1,0:T(8,128)} %iota_add_fusion.position_ref), custom_call_target="tpu_custom_call" | custom-call | flops 2415919104 | bytes 3604480 | tf_op jit(solution)/shard_map/pallas_call | solution.py:124
  99.0 1.0 reduce_sum.56
  100.1 0.7 multiply_reduce_fusion.1
  100.8 0.2 fusion.3
  101.0 0.2 fusion.1
  101.2 0.1 subtract_select_fusion
  101.3 1.0 multiply_reduce_fusion
  102.3 0.7 convolution_convert_fusion
  103.3 2.5 %copy.58 = bf16[2048,512]{1,0:T(8,128)(2,1)} copy(bf16[2048,512]{0,1:T(8,128)(2,1)S(1)} %bitcast.62) | data formatting | bytes 4194304 | tf_op jit(solution)/shard_map/rk,rd->kd/dot_general | solution.py:211
  105.8 2.3 %fusion.4.refs_0_ = f32[16,128,128]{2,1,0:T(8,128)S(1)} fusion(bf16[16,128,512]{2,1,0:T(8,128)(2,1)} %bitcast.63, bf16[512,128,1]{1,0,2:T(8,128)(2,1)S(1)} %bitcast.66), kind=kOutput, calls=%fused_computation.15 | convolution fusion | flops 268435456 | bytes 3276800 | tf_op jit(solution)/shard_map/rk,rd->kd/dot_general | solution.py:211
  108.1 19.1 %shard_map.96 = (f32[16,128,128]{2,1,0:T(8,128)S(1)}, bf16[16,32,128]{2,1,0:T(8,128)(2,1)S(1)}, f32[16,1,32]{2,1,0:T(1,128)S(1)}) custom-call(f32[16,128,128]{2,1,0:T(8,128)S(1)} %fusion.4.refs_0_, bf16[16,32,128]{2,1,0:T(8,128)(2,1)S(1)} %bitcast.54, f32[16,1,32]{2,1,0:T(1,128)S(1)} %copy.63.refs_2_), custom_call_target="tpu_custom_call" | custom-call | bytes 2363392 | tf_op jit(solution)/shard_map/pallas_call | solution.py:94
  127.3 0.5 broadcast.23
  127.8 0.7 reduce.3
  128.5 0.7 copy.64
  129.3 10.9 %shard_map.97 = f32[16,8,128]{2,1,0:T(8,128)S(1)} custom-call(f32[16,8,128]{2,1,0:T(8,128)S(1)} %bitcast.55), custom_call_target="tpu_custom_call" | custom-call | bytes 131072 | tf_op jit(solution)/shard_map/pallas_call | solution.py:94
  140.2 10.8 %shard_map.98 = f32[16,8,128]{2,1,0:T(8,128)S(1)} custom-call(f32[8,128]{1,0:T(8,128)S(1)} %reduce_sum.59.refs_0_), custom_call_target="tpu_custom_call" | custom-call | bytes 131072 | tf_op jit(solution)/shard_map/pallas_call | solution.py:94
  151.1 0.6 convert_bitcast_fusion
  151.7 0.7 copy.66
  (19 shorter events, 1.0 us)
Async XLA Ops:
  8.4 0.9 copy-start
  9.3 0.8 copy-start.1
  99.0 2.2 %copy-start.2 = (f32[8,2048]{1,0:T(8,128)S(1)}, f32[8,2048]{1,0:T(8,128)}, u32[]{:S(2)}) copy-start(f32[8,2048]{1,0:T(8,128)} %shard_map.95) | copy-start | bytes 196612

commit v5 on v4

--- a/solution.py
+++ b/solution.py
@@ -23,72 +23,108 @@
     return tuple(peer if name == axis else lax.axis_index(name) for name in AXES)
 
 
+def pair_peers(axis):
+    n = lax.axis_size(axis)
+    me = lax.axis_index(axis)
+    sibling = me + 1 - 2 * lax.rem(me, 2)
+    return sibling, [lax.rem(me + 2 * step, n) for step in range(1, n // 2)]
+
+
+def barrier_peers(items):
+    peers = []
+    for axis in sorted({axis for axis, _ in items}):
+        n = lax.axis_size(axis)
+        me = lax.axis_index(axis)
+        modes = {mode for item_axis, mode in items if item_axis == axis}
+        if modes == {"pair"}:
+            sibling, others = pair_peers(axis)
+            peers += [(axis, sibling)] + [(axis, peer) for peer in others]
+        else:
+            peers += [(axis, lax.rem(me + step, n)) for step in range(1, n)]
+    return peers
+
+
 def exchange_kernel(items, *refs):
     count = len(items)
     x_refs, y_refs = refs[:count], refs[count : 2 * count]
     send_sem, recv_sem = refs[2 * count], refs[2 * count + 1]
-    axes = sorted({axis for axis, _ in items})
-    stride = max(lax.axis_size(axis) for axis in axes)
+    stride = max(lax.axis_size(axis) for axis, _ in items)
+    forward_base = count * stride
+
+    def remote(i, axis, source, slot, target, send_slot, recv_slot):
+        return pltpu.make_async_remote_copy(
+            src_ref=source,
+            dst_ref=y_refs[i].at[slot],
+            send_sem=send_sem.at[send_slot],
+            recv_sem=recv_sem.at[recv_slot],
+            device_id=device_of(axis, target),
+            device_id_type=MESH,
+        )
 
     barrier = pltpu.get_barrier_semaphore()
-    for axis in axes:
+    peers = barrier_peers(items)
+    for axis, peer in peers:
+        pl.semaphore_signal(barrier, inc=1, device_id=device_of(axis, peer), device_id_type=MESH)
+    pl.semaphore_wait(barrier, len(peers))
+
+    sends = []
+    for i, (axis, mode) in enumerate(items):
         n = lax.axis_size(axis)
         me = lax.axis_index(axis)
-        for step in range(1, n):
-            peer = lax.rem(me + step, n)
-            pl.semaphore_signal(barrier, inc=1, device_id=device_of(axis, peer), device_id_type=MESH)
-    pl.semaphore_wait(barrier, sum(lax.axis_size(axis) - 1 for axis in axes))
-
-    copies = {}
-    for step in range(1, max(lax.axis_size(axis) for axis in axes)):
-        for i, (axis, gather) in enumerate(items):
-            n = lax.axis_size(axis)
-            if step >= n:
-                continue
-            me = lax.axis_index(axis)
-            peer = lax.rem(me + step, n)
-            source = x_refs[i] if gather else x_refs[i].at[peer]
-            copy = pltpu.make_async_remote_copy(
-                src_ref=source,
-                dst_ref=y_refs[i].at[me],
-                send_sem=send_sem.at[i * stride + peer],
-                recv_sem=recv_sem.at[i * stride + me],
-                device_id=device_of(axis, peer),
-                device_id_type=MESH,
+        if mode == "pair":
+            sibling, others = pair_peers(axis)
+            targets = [sibling] + others
+        else:
+            targets = [lax.rem(me + step, n) for step in range(1, n)]
+        for peer in targets:
+            source = x_refs[i].at[peer] if mode == "a2a" else x_refs[i]
+            copy = remote(i, axis, source, me, peer, i * stride + peer, i * stride + me)
+            copy.start()
+            sends.append(copy)
+    for i, (axis, mode) in enumerate(items):
+        me = lax.axis_index(axis)
+        y_refs[i][me] = x_refs[i][me] if mode == "a2a" else x_refs[i][...]
+
+    forwards = []
+    for i, (axis, mode) in enumerate(items):
+        if mode != "pair":
+            continue
+        sibling, others = pair_peers(axis)
+        for block in others:
+            arrived = remote(i, axis, y_refs[i].at[block], block, block, i * stride + block, i * stride + block)
+            arrived.wait_recv()
+            copy = remote(
+                i, axis, y_refs[i].at[block], block, sibling, forward_base + i * stride + block,
+                i * stride + block,
             )
             copy.start()
-            copies[(i, step)] = copy
-    for i, (axis, gather) in enumerate(items):
-        me = lax.axis_index(axis)
-        y_refs[i][me] = x_refs[i][...] if gather else x_refs[i][me]
-    for step in range(1, max(lax.axis_size(axis) for axis in axes)):
-        for i, (axis, gather) in enumerate(items):
-            n = lax.axis_size(axis)
-            if step >= n:
-                continue
-            me = lax.axis_index(axis)
-            source_device = lax.rem(me + n - step, n)
-            copies[(i, step)].wait_send()
-            incoming = pltpu.make_async_remote_copy(
-                src_ref=y_refs[i].at[source_device],
-                dst_ref=y_refs[i].at[source_device],
-                send_sem=send_sem.at[i * stride + source_device],
-                recv_sem=recv_sem.at[i * stride + source_device],
-                device_id=device_of(axis, source_device),
-                device_id_type=MESH,
-            )
+            forwards.append(copy)
+
+    for i, (axis, mode) in enumerate(items):
+        n = lax.axis_size(axis)
+        me = lax.axis_index(axis)
+        if mode == "pair":
+            sibling, _ = pair_peers(axis)
+            blocks = [sibling] + [lax.rem(sibling + 2 * step, n) for step in range(1, n // 2)]
+        else:
+            blocks = [lax.rem(me + n - step, n) for step in range(1, n)]
+        for block in blocks:
+            incoming = remote(i, axis, y_refs[i].at[block], block, block, i * stride + block, i * stride + block)
             incoming.wait_recv()
+    for copy in sends + forwards:
+        copy.wait_send()
 
 
 def exchange(arrays, items, collective_id):
     count = len(arrays)
     items = tuple(items)
     out_shapes = [
-        jax.ShapeDtypeStruct(((lax.axis_size(axis),) + a.shape) if g else a.shape, a.dtype)
-        for a, (axis, g) in zip(arrays, items)
+        jax.ShapeDtypeStruct(a.shape if mode == "a2a" else ((lax.axis_size(axis),) + a.shape), a.dtype)
+        for a, (axis, mode) in zip(arrays, items)
     ]
     moved = sum(
-        a.size * a.dtype.itemsize * (lax.axis_size(axis) if g else 1) for a, (axis, g) in zip(arrays, items)
+        a.size * a.dtype.itemsize * (1 if mode == "a2a" else lax.axis_size(axis))
+        for a, (axis, mode) in zip(arrays, items)
     )
     slots = count * max(lax.axis_size(axis) for axis, _ in items)
     return pl.pallas_call(
@@ -96,7 +132,7 @@
         out_shape=out_shapes,
         in_specs=[pl.BlockSpec(memory_space=pltpu.VMEM)] * count,
         out_specs=[pl.BlockSpec(memory_space=pltpu.VMEM)] * count,
-        scratch_shapes=[pltpu.SemaphoreType.DMA((slots,)), pltpu.SemaphoreType.DMA((slots,))],
+        scratch_shapes=[pltpu.SemaphoreType.DMA((2 * slots,)), pltpu.SemaphoreType.DMA((slots,))],
         compiler_params=pltpu.CompilerParams(
             collective_id=collective_id, has_side_effects=True, vmem_limit_bytes=48 * 1024 * 1024
         ),
@@ -162,7 +198,7 @@
             index_query.reshape(groups, own_rows * part_heads, index_width),
             index_weight.reshape(groups, 1, own_rows * part_heads),
         ],
-        [("pb", True), ("pb", True), ("ha", False), ("ha", False), ("ha", False), ("ha", False)],
+        [("pb", "pair"), ("pb", "pair"), ("ha", "a2a"), ("ha", "a2a"), ("ha", "a2a"), ("ha", "a2a")],
         0,
     )
     latent_piece = latent_parts.reshape(tokens, latent_width)
@@ -219,14 +255,14 @@
             .transpose(1, 0, 2)
             .reshape(groups, 1, own_rows * part_heads),
         ],
-        [("pb", False), ("ha", False), ("ha", False)],
+        [("pb", "a2a"), ("ha", "a2a"), ("ha", "a2a")],
         1,
     )
     query_output = query_back.reshape(query_rows, part_heads, index_width)
     weight_output = weight_back.reshape(query_rows, part_heads)
     key_share = jnp.sum(key_parts, axis=0).reshape(groups, own_rows, index_width)
-    key_rows = jnp.sum(exchange([key_share], [("ha", False)], 2)[0], axis=0)
-    key_output = exchange([key_rows], [("ha", True)], 3)[0]
+    key_rows = jnp.sum(exchange([key_share], [("ha", "a2a")], 2)[0], axis=0)
+    key_output = exchange([key_rows], [("ha", "gather")], 3)[0]
     key_output = key_output.reshape(query_rows, index_width).astype(jnp.bfloat16)
     return (query_output, key_output, weight_output)
 

time: 153 us -> 136 us (0.89)
  Pallas kernels: 127 us -> 111 us
    pallas_call x4, Pallas kernels: 119 us -> 102 us  [exchange(): pl.pallas_call(functools.partial(exchange_kernel, items), out_shape=out_s...]
where the time goes in v5:
time: 136 us
  Pallas kernels  111 us (82%)
  local copies, waits for them, and re-layouts  16.2 us (12%)
  other arithmetic  4.49 us (3%)
  matrix products  3.72 us (3%)
    pallas_call x4, Pallas kernels, exchange(): pl.pallas_call(functools.partial(exchange_kernel, items), out_shape=out_s...  102 us
    pallas_call x1, Pallas kernels, head_mass(): pl.pallas_call(head_mass_kernel, out_shape=jax.ShapeDtypeStruct((query_ro...  8.42 us
    unnamed x12, local copies, waits for them, and re-layouts  7.83 us

profile of v5, /device:TPU:8, one launch (start us, length us, event | category | flops | bytes accessed | tf_op | source)
XLA Modules:
  0.0 135.9 jit_solution(2970700157769814934)
XLA Ops:
  0.6 0.7 dynamic_slice.3
  1.4 0.7 dynamic-slice_bitcast_fusion
  2.1 0.6 iota_add_fusion.position_ref
  2.7 0.7 copy.57.start_ref
  3.4 0.8 copy.44
  4.2 0.8 copy.45
  5.1 1.1 copy.46.refs_0_
  6.2 2.2 %copy.43 = bf16[128,8,576]{2,1,0:T(8,128)(2,1)S(1)} copy(bf16[128,8,576]{0,2,1:T(8,128)(2,1)} %param.7) | data formatting | bytes 2359296 | tf_op args[0]
  8.4 0.9 copy-done
  9.3 0.8 copy-done.1
  10.1 52.2 %shard_map.94 = (bf16[16,128,576]{2,1,0:T(8,128)(2,1)}, bf16[16,128,128]{2,1,0:T(8,128)(2,1)S(1)}, bf16[16,64,576]{2,1,0:T(8,128)(2,1)S(1)}, f32[16,1,64]{2,1,0:...) custom-call(bf16[128,576]{1,0:T(8,128)(2,1)S(1)} %copy.46.refs_0_, ...), custom_call_target="tpu_custom_call" | custom-call | bytes 8400896 | tf_op jit(solution)/shard_map/pallas_call | solution.py:130
  62.4 0.1 copy.51
  62.8 1.0 reshape.109.sums_ref
  63.8 1.2 copy.53
  65.0 8.4 %shard_map.95 = f32[8,2048]{1,0:T(8,128)} custom-call(bf16[1024,576]{1,0:T(8,128)(2,1)} %bitcast.64, bf16[2048,576]{1,0:T(8,128)(2,1)} %bitcast.73, f32[1024,1]{1,0:T(8,128)} %reshape.109.sums_ref, s32[8,1]{1,0:T(8,128)} %copy.57.start_ref, s32[8,1]{1,0:T(8,128)} %iota_add_fusion.position_ref), custom_call_target="tpu_custom_call" | custom-call | flops 2415919104 | bytes 3604480 | tf_op jit(solution)/shard_map/pallas_call | solution.py:160
  73.4 1.0 reduce_sum.56
  74.4 0.7 multiply_reduce_fusion.1
  75.2 0.2 fusion.3
  75.4 0.2 fusion.1
  75.6 0.1 subtract_select_fusion
  75.7 1.0 multiply_reduce_fusion
  76.7 0.7 convolution_convert_fusion
  77.7 2.5 %copy.58 = bf16[2048,512]{1,0:T(8,128)(2,1)} copy(bf16[2048,512]{0,1:T(8,128)(2,1)S(1)} %bitcast.62) | data formatting | bytes 4194304 | tf_op jit(solution)/shard_map/rk,rd->kd/dot_general | solution.py:247
  80.2 2.3 %fusion.4.refs_0_ = f32[16,128,128]{2,1,0:T(8,128)S(1)} fusion(bf16[16,128,512]{2,1,0:T(8,128)(2,1)} %bitcast.63, bf16[512,128,1]{1,0,2:T(8,128)(2,1)S(1)} %bitcast.66), kind=kOutput, calls=%fused_computation.15 | convolution fusion | flops 268435456 | bytes 3276800 | tf_op jit(solution)/shard_map/rk,rd->kd/dot_general | solution.py:247
  82.5 26.1 %shard_map.96 = (f32[16,128,128]{2,1,0:T(8,128)S(1)}, bf16[16,32,128]{2,1,0:T(8,128)(2,1)S(1)}, f32[16,1,32]{2,1,0:T(1,128)S(1)}) custom-call(f32[16,128,128]{2,1,0:T(8,128)S(1)} %fusion.4.refs_0_, bf16[16,32,128]{2,1,0:T(8,128)(2,1)S(1)} %bitcast.54, f32[16,1,32]{2,1,0:T(1,128)S(1)} %copy.63.refs_2_), custom_call_target="tpu_custom_call" | custom-call | bytes 2363392 | tf_op jit(solution)/shard_map/pallas_call | solution.py:130
  108.6 0.5 broadcast.23
  109.1 0.7 reduce.3
  109.9 0.7 copy.64
  110.6 13.1 %shard_map.97 = f32[16,8,128]{2,1,0:T(8,128)S(1)} custom-call(f32[16,8,128]{2,1,0:T(8,128)S(1)} %bitcast.55), custom_call_target="tpu_custom_call" | custom-call | bytes 131072 | tf_op jit(solution)/shard_map/pallas_call | solution.py:130
  123.7 10.9 %shard_map.98 = f32[16,8,128]{2,1,0:T(8,128)S(1)} custom-call(f32[8,128]{1,0:T(8,128)S(1)} %reduce_sum.59.refs_0_), custom_call_target="tpu_custom_call" | custom-call | bytes 131072 | tf_op jit(solution)/shard_map/pallas_call | solution.py:130
  134.6 0.6 convert_bitcast_fusion
  135.2 0.7 copy.66
  (19 shorter events, 1.0 us)
Async XLA Ops:
  8.4 0.9 copy-start
  9.3 0.8 copy-start.1
  73.4 2.2 %copy-start.2 = (f32[8,2048]{1,0:T(8,128)S(1)}, f32[8,2048]{1,0:T(8,128)}, u32[]{:S(2)}) copy-start(f32[8,2048]{1,0:T(8,128)} %shard_map.95) | copy-start | bytes 196612

commit v6 on v5

--- a/solution.py
+++ b/solution.py
@@ -32,23 +32,58 @@
 
 def barrier_peers(items):
     peers = []
-    for axis in sorted({axis for axis, _ in items}):
+    for axis in sorted({axis for axis, _, _ in items}):
         n = lax.axis_size(axis)
         me = lax.axis_index(axis)
-        modes = {mode for item_axis, mode in items if item_axis == axis}
-        if modes == {"pair"}:
-            sibling, others = pair_peers(axis)
+        modes = {mode for item_axis, mode, _ in items if item_axis == axis}
+        sibling, others = pair_peers(axis)
+        if modes == {"sib"}:
+            peers += [(axis, sibling)]
+        elif modes == {"same"}:
+            peers += [(axis, peer) for peer in others]
+        elif modes == {"pair"}:
             peers += [(axis, sibling)] + [(axis, peer) for peer in others]
         else:
             peers += [(axis, lax.rem(me + step, n)) for step in range(1, n)]
     return peers
 
 
+def plan(axis, mode):
+    n = lax.axis_size(axis)
+    me = lax.axis_index(axis)
+    sibling, others = pair_peers(axis)
+    if mode == "a2a":
+        return (
+            [(lax.rem(me + s, n), lax.rem(me + s, n), me) for s in range(1, n)],
+            [(lax.rem(me + n - s, n), lax.rem(me + n - s, n)) for s in range(1, n)],
+        )
+    if mode == "gather":
+        return (
+            [(lax.rem(me + s, n), None, me) for s in range(1, n)],
+            [(lax.rem(me + n - s, n), lax.rem(me + n - s, n)) for s in range(1, n)],
+        )
+    if mode == "sib":
+        parity = lax.rem(sibling, 2)
+        return (
+            [(sibling, 2 * j + parity, j) for j in range(n // 2)],
+            [(sibling, j) for j in range(n // 2)],
+        )
+    if mode == "same":
+        return (
+            [(peer, peer // 2, me // 2) for peer in others],
+            [(lax.rem(me + n - 2 * s, n), lax.rem(me + n - 2 * s, n) // 2) for s in range(1, n // 2)],
+        )
+    return (
+        [(peer, None, me) for peer in [sibling] + others],
+        [(sibling, sibling)] + [(lax.rem(sibling + 2 * s, n),) * 2 for s in range(1, n // 2)],
+    )
+
+
 def exchange_kernel(items, *refs):
     count = len(items)
     x_refs, y_refs = refs[:count], refs[count : 2 * count]
-    send_sem, recv_sem = refs[2 * count], refs[2 * count + 1]
-    stride = max(lax.axis_size(axis) for axis, _ in items)
+    send_sem, recv_sem, local_sem = refs[2 * count : 2 * count + 3]
+    stride = max(lax.axis_size(axis) for axis, _, _ in items)
     forward_base = count * stride
 
     def remote(i, axis, source, slot, target, send_slot, recv_slot):
@@ -68,25 +103,30 @@
     pl.semaphore_wait(barrier, len(peers))
 
     sends = []
-    for i, (axis, mode) in enumerate(items):
-        n = lax.axis_size(axis)
-        me = lax.axis_index(axis)
-        if mode == "pair":
-            sibling, others = pair_peers(axis)
-            targets = [sibling] + others
-        else:
-            targets = [lax.rem(me + step, n) for step in range(1, n)]
-        for peer in targets:
-            source = x_refs[i].at[peer] if mode == "a2a" else x_refs[i]
-            copy = remote(i, axis, source, me, peer, i * stride + peer, i * stride + me)
+    for i, (axis, mode, _) in enumerate(items):
+        for peer, chunk, slot in plan(axis, mode)[0]:
+            source = x_refs[i] if chunk is None else x_refs[i].at[chunk]
+            send_slot = i * stride + (chunk if mode == "sib" else peer)
+            copy = remote(i, axis, source, slot, peer, send_slot, i * stride + slot)
             copy.start()
             sends.append(copy)
-    for i, (axis, mode) in enumerate(items):
+    locals_ = []
+    for i, (axis, mode, _) in enumerate(items):
         me = lax.axis_index(axis)
-        y_refs[i][me] = x_refs[i][me] if mode == "a2a" else x_refs[i][...]
+        if mode == "sib":
+            continue
+        if mode == "same":
+            own = (x_refs[i].at[me // 2], y_refs[i].at[me // 2])
+        elif mode == "a2a":
+            own = (x_refs[i].at[me], y_refs[i].at[me])
+        else:
+            own = (x_refs[i], y_refs[i].at[me])
+        copy = pltpu.make_async_copy(own[0], own[1], local_sem.at[i])
+        copy.start()
+        locals_.append(copy)
 
     forwards = []
-    for i, (axis, mode) in enumerate(items):
+    for i, (axis, mode, _) in enumerate(items):
         if mode != "pair":
             continue
         sibling, others = pair_peers(axis)
@@ -100,39 +140,42 @@
             copy.start()
             forwards.append(copy)
 
-    for i, (axis, mode) in enumerate(items):
-        n = lax.axis_size(axis)
-        me = lax.axis_index(axis)
-        if mode == "pair":
-            sibling, _ = pair_peers(axis)
-            blocks = [sibling] + [lax.rem(sibling + 2 * step, n) for step in range(1, n // 2)]
-        else:
-            blocks = [lax.rem(me + n - step, n) for step in range(1, n)]
-        for block in blocks:
-            incoming = remote(i, axis, y_refs[i].at[block], block, block, i * stride + block, i * stride + block)
+    for i, (axis, mode, _) in enumerate(items):
+        for peer, slot in plan(axis, mode)[1]:
+            incoming = remote(i, axis, y_refs[i].at[slot], slot, peer, i * stride + slot, i * stride + slot)
             incoming.wait_recv()
     for copy in sends + forwards:
         copy.wait_send()
+    for copy in locals_:
+        copy.wait()
 
 
 def exchange(arrays, items, collective_id):
     count = len(arrays)
     items = tuple(items)
-    out_shapes = [
-        jax.ShapeDtypeStruct(a.shape if mode == "a2a" else ((lax.axis_size(axis),) + a.shape), a.dtype)
-        for a, (axis, mode) in zip(arrays, items)
-    ]
-    moved = sum(
-        a.size * a.dtype.itemsize * (1 if mode == "a2a" else lax.axis_size(axis))
-        for a, (axis, mode) in zip(arrays, items)
-    )
-    slots = count * max(lax.axis_size(axis) for axis, _ in items)
+
+    def out_shape(a, axis, mode):
+        n = lax.axis_size(axis)
+        if mode == "a2a":
+            return a.shape
+        if mode in ("sib", "same"):
+            return (n // 2,) + a.shape[1:]
+        return (n,) + a.shape
+
+    out_shapes = [jax.ShapeDtypeStruct(out_shape(a, axis, mode), a.dtype) for a, (axis, mode, _) in zip(arrays, items)]
+    moved = sum(math.prod(o.shape) * a.dtype.itemsize for a, o in zip(arrays, out_shapes))
+    slots = count * max(lax.axis_size(axis) for axis, _, _ in items)
+    space = [pl.BlockSpec(memory_space=pl.ANY if hbm else pltpu.VMEM) for _, _, hbm in items]
     return pl.pallas_call(
         functools.partial(exchange_kernel, items),
         out_shape=out_shapes,
-        in_specs=[pl.BlockSpec(memory_space=pltpu.VMEM)] * count,
+        in_specs=space,
         out_specs=[pl.BlockSpec(memory_space=pltpu.VMEM)] * count,
-        scratch_shapes=[pltpu.SemaphoreType.DMA((2 * slots,)), pltpu.SemaphoreType.DMA((slots,))],
+        scratch_shapes=[
+            pltpu.SemaphoreType.DMA((2 * slots,)),
+            pltpu.SemaphoreType.DMA((slots,)),
+            pltpu.SemaphoreType.DMA((count,)),
+        ],
         compiler_params=pltpu.CompilerParams(
             collective_id=collective_id, has_side_effects=True, vmem_limit_bytes=48 * 1024 * 1024
         ),
@@ -198,7 +241,14 @@
             index_query.reshape(groups, own_rows * part_heads, index_width),
             index_weight.reshape(groups, 1, own_rows * part_heads),
         ],
-        [("pb", "pair"), ("pb", "pair"), ("ha", "a2a"), ("ha", "a2a"), ("ha", "a2a"), ("ha", "a2a")],
+        [
+            ("pb", "pair", False),
+            ("pb", "pair", False),
+            ("ha", "a2a", True),
+            ("ha", "a2a", False),
+            ("ha", "a2a", False),
+            ("ha", "a2a", False),
+        ],
         0,
     )
     latent_piece = latent_parts.reshape(tokens, latent_width)
@@ -247,22 +297,28 @@
     key_grad = jnp.einsum("rk,rd->kd", coeffs, flat_index, preferred_element_type=jnp.float32)
 
     query_grad = query_grad.astype(jnp.bfloat16).reshape(own_rows, groups, part_heads, index_width)
+    key_grad = key_grad.reshape(blocks, query_rows, index_width)
+    sibling_part = exchange([key_grad], [("pb", "sib", False)], 1)[0]
+    parity = lax.rem(lax.axis_index("pb"), 2)
+    own_part = lax.dynamic_index_in_dim(
+        key_grad.reshape(blocks // 2, 2, query_rows, index_width), parity, axis=1, keepdims=False
+    )
     key_parts, query_back, weight_back = exchange(
         [
-            key_grad.reshape(blocks, query_rows, index_width),
+            own_part + sibling_part,
             query_grad.transpose(1, 0, 2, 3).reshape(groups, own_rows * part_heads, index_width),
             weight_grad.reshape(own_rows, groups, part_heads)
             .transpose(1, 0, 2)
             .reshape(groups, 1, own_rows * part_heads),
         ],
-        [("pb", "a2a"), ("ha", "a2a"), ("ha", "a2a")],
-        1,
+        [("pb", "same", False), ("ha", "a2a", False), ("ha", "a2a", False)],
+        4,
     )
     query_output = query_back.reshape(query_rows, part_heads, index_width)
     weight_output = weight_back.reshape(query_rows, part_heads)
     key_share = jnp.sum(key_parts, axis=0).reshape(groups, own_rows, index_width)
-    key_rows = jnp.sum(exchange([key_share], [("ha", "a2a")], 2)[0], axis=0)
-    key_output = exchange([key_rows], [("ha", "gather")], 3)[0]
+    key_rows = jnp.sum(exchange([key_share], [("ha", "a2a", False)], 2)[0], axis=0)
+    key_output = exchange([key_rows], [("ha", "gather", False)], 3)[0]
     key_output = key_output.reshape(query_rows, index_width).astype(jnp.bfloat16)
     return (query_output, key_output, weight_output)
 

time: 136 us -> 128 us (0.941)
  Pallas kernels: 111 us -> 106 us
  local copies, waits for them, and re-layouts: 16.2 us -> 13.6 us
  matrix products: 3.72 us -> 2.17 us
    pallas_call x4 -> x5, Pallas kernels: 102 us -> 97.6 us  [exchange(): pl.pallas_call(functools.partial(exchange_kernel, items), out_shape=out_s...]
    dot_general x1 -> x0, local copies, waits for them, and re-layouts: 2.51 us -> none  [on_device(): jnp.einsum('rk,rd->kd', coeffs, flat_index, preferred_element_type=jnp.fl...]
    dot_general x1, matrix products: 2.29 us -> 0.74 us  [on_device(): jnp.einsum('rk,rd->kd', coeffs, flat_index, preferred_element_type=jnp.fl...]
where the time goes in v6:
time: 128 us; the launch traced here: 127 us
  Pallas kernels  106 us (83%)
  local copies, waits for them, and re-layouts  13.6 us (11%)
  other arithmetic  4.52 us (4%)
  matrix products  2.17 us (2%)
    pallas_call x5, Pallas kernels, exchange(): pl.pallas_call(functools.partial(exchange_kernel, items), out_shape=out_s...  97.6 us
    pallas_call x1, Pallas kernels, head_mass(): pl.pallas_call(head_mass_kernel, out_shape=jax.ShapeDtypeStruct((query_ro...  8.42 us
    unnamed x12, local copies, waits for them, and re-layouts  7.83 us

profile of v6, /device:TPU:8, one launch (start us, length us, event | category | flops | bytes accessed | tf_op | source)
XLA Modules:
  0.0 127.1 jit_solution(2128226486134602297)
XLA Ops:
  0.6 0.7 dynamic_slice.7
  1.4 0.7 dynamic-slice_bitcast_fusion
  2.1 0.6 iota_add_fusion.position_ref
  2.7 0.7 copy.55.start_ref
  3.4 0.8 copy.42
  4.2 0.8 copy.43
  5.1 1.1 copy.44.refs_0_
  6.2 2.2 %copy.41 = bf16[128,8,576]{2,1,0:T(8,128)(2,1)S(1)} copy(bf16[128,8,576]{0,2,1:T(8,128)(2,1)} %param.7) | data formatting | bytes 2359296 | tf_op args[0]
  8.4 0.9 copy-done
  9.3 0.8 copy-done.1
  10.1 52.3 %shard_map.94 = (bf16[16,128,576]{2,1,0:T(8,128)(2,1)}, bf16[16,128,128]{2,1,0:T(8,128)(2,1)S(1)}, bf16[16,64,576]{2,1,0:T(8,128)(2,1)S(1)}, f32[16,1,64]{2,1,0:...) custom-call(bf16[128,576]{1,0:T(8,128)(2,1)S(1)} %copy.44.refs_0_, ...), custom_call_target="tpu_custom_call" | custom-call | bytes 8400896 | tf_op jit(solution)/shard_map/pallas_call | solution.py:169
  62.5 0.1 copy.49
  62.8 1.0 reshape.110.sums_ref
  63.8 1.2 copy.51
  65.0 8.4 %shard_map.95 = f32[8,2048]{1,0:T(8,128)} custom-call(bf16[1024,576]{1,0:T(8,128)(2,1)} %bitcast.67, bf16[2048,576]{1,0:T(8,128)(2,1)} %bitcast.76, f32[1024,1]{1,0:T(8,128)} %reshape.110.sums_ref, s32[8,1]{1,0:T(8,128)} %copy.55.start_ref, s32[8,1]{1,0:T(8,128)} %iota_add_fusion.position_ref), custom_call_target="tpu_custom_call" | custom-call | flops 2415919104 | bytes 3604480 | tf_op jit(solution)/shard_map/pallas_call | solution.py:203
  73.5 1.0 reduce_sum.56
  74.5 0.7 multiply_reduce_fusion.1
  75.2 0.2 fusion.3
  75.4 0.2 fusion.1
  75.7 0.1 subtract_select_fusion
  75.8 1.0 multiply_reduce_fusion
  76.7 0.7 convolution_convert_fusion
  77.5 0.7 fusion.4
  78.5 2.4 %shard_map.96 = f32[8,128,128]{2,1,0:T(8,128)S(1)} custom-call(f32[16,128,128]{2,1,0:T(8,128)S(1)} %bitcast.52), custom_call_target="tpu_custom_call" | custom-call | bytes 1048576 | tf_op jit(solution)/shard_map/pallas_call | solution.py:169
  81.0 21.1 %shard_map.97 = (f32[8,128,128]{2,1,0:T(8,128)S(1)}, bf16[16,32,128]{2,1,0:T(8,128)(2,1)S(1)}, f32[16,1,32]{2,1,0:T(1,128)S(1)}) custom-call(f32[8,128,128]{2,1,0:T(8,128)S(1)} %bitcast_add_fusion.refs_0_, bf16[16,32,128]{2,1,0:T(8,128)(2,1)S(1)} %bitcast.58, f32[16,1,32]{2,1,0:T(1,128)S(1)} %copy.60.refs_2_), custom_call_target="tpu_custom_call" | custom-call | bytes 1314816 | tf_op jit(solution)/shard_map/pallas_call | solution.py:169
  102.1 0.5 broadcast.24
  102.6 0.7 reduce.3
  103.4 0.7 copy.61
  104.1 10.9 %shard_map.98 = f32[16,8,128]{2,1,0:T(8,128)S(1)} custom-call(f32[16,8,128]{2,1,0:T(8,128)S(1)} %bitcast.59), custom_call_target="tpu_custom_call" | custom-call | bytes 131072 | tf_op jit(solution)/shard_map/pallas_call | solution.py:169
  115.0 10.8 %shard_map.99 = f32[16,8,128]{2,1,0:T(8,128)S(1)} custom-call(f32[8,128]{1,0:T(8,128)S(1)} %reduce_sum.59.refs_0_), custom_call_target="tpu_custom_call" | custom-call | bytes 131072 | tf_op jit(solution)/shard_map/pallas_call | solution.py:169
  125.9 0.6 convert_bitcast_fusion
  126.5 0.7 copy.64
  (20 shorter events, 1.0 us)
Async XLA Ops:
  8.4 0.9 copy-start
  9.3 0.8 copy-start.1
  73.5 2.2 %copy-start.2 = (f32[8,2048]{1,0:T(8,128)S(1)}, f32[8,2048]{1,0:T(8,128)}, u32[]{:S(2)}) copy-start(f32[8,2048]{1,0:T(8,128)} %shard_map.95) | copy-start | bytes 196612

commit v7 on v6

--- a/solution.py
+++ b/solution.py
@@ -303,22 +303,22 @@
     own_part = lax.dynamic_index_in_dim(
         key_grad.reshape(blocks // 2, 2, query_rows, index_width), parity, axis=1, keepdims=False
     )
-    key_parts, query_back, weight_back = exchange(
+    key_parts = exchange([own_part + sibling_part], [("pb", "same", False)], 4)[0]
+    key_share = jnp.sum(key_parts, axis=0).reshape(groups, own_rows, index_width)
+    key_rows, query_back, weight_back = exchange(
         [
-            own_part + sibling_part,
+            key_share,
             query_grad.transpose(1, 0, 2, 3).reshape(groups, own_rows * part_heads, index_width),
             weight_grad.reshape(own_rows, groups, part_heads)
             .transpose(1, 0, 2)
             .reshape(groups, 1, own_rows * part_heads),
         ],
-        [("pb", "same", False), ("ha", "a2a", False), ("ha", "a2a", False)],
-        4,
+        [("ha", "a2a", False), ("ha", "a2a", False), ("ha", "a2a", False)],
+        2,
     )
     query_output = query_back.reshape(query_rows, part_heads, index_width)
     weight_output = weight_back.reshape(query_rows, part_heads)
-    key_share = jnp.sum(key_parts, axis=0).reshape(groups, own_rows, index_width)
-    key_rows = jnp.sum(exchange([key_share], [("ha", "a2a", False)], 2)[0], axis=0)
-    key_output = exchange([key_rows], [("ha", "gather", False)], 3)[0]
+    key_output = exchange([jnp.sum(key_rows, axis=0)], [("ha", "gather", False)], 3)[0]
     key_output = key_output.reshape(query_rows, index_width).astype(jnp.bfloat16)
     return (query_output, key_output, weight_output)
 

time: 128 us -> 127 us (level)
  no operation moved by 1% of the time
where the time goes in v7:
time: 127 us
  Pallas kernels  106 us (83%)
  local copies, waits for them, and re-layouts  13.6 us (11%)
  other arithmetic  4.52 us (4%)
  matrix products  2.17 us (2%)
    pallas_call x5, Pallas kernels, exchange(): pl.pallas_call(functools.partial(exchange_kernel, items), out_shape=out_s...  97.3 us
    pallas_call x1, Pallas kernels, head_mass(): pl.pallas_call(head_mass_kernel, out_shape=jax.ShapeDtypeStruct((query_ro...  8.42 us
    unnamed x12, local copies, waits for them, and re-layouts  7.83 us

profile of v7, /device:TPU:8, one launch (start us, length us, event | category | flops | bytes accessed | tf_op | source)
XLA Modules:
  0.0 126.9 jit_solution(10485834580910314664)
XLA Ops:
  0.6 0.7 dynamic_slice.7
  1.4 0.7 dynamic-slice_bitcast_fusion
  2.1 0.6 iota_add_fusion.position_ref
  2.7 0.7 copy.55.start_ref
  3.4 0.8 copy.42
  4.2 0.8 copy.43
  5.1 1.1 copy.44.refs_0_
  6.2 2.2 %copy.41 = bf16[128,8,576]{2,1,0:T(8,128)(2,1)S(1)} copy(bf16[128,8,576]{0,2,1:T(8,128)(2,1)} %param.7) | data formatting | bytes 2359296 | tf_op args[0]
  8.4 0.9 copy-done
  9.3 0.8 copy-done.1
  10.1 52.3 %shard_map.94 = (bf16[16,128,576]{2,1,0:T(8,128)(2,1)}, bf16[16,128,128]{2,1,0:T(8,128)(2,1)S(1)}, bf16[16,64,576]{2,1,0:T(8,128)(2,1)S(1)}, f32[16,1,64]{2,1,0:...) custom-call(bf16[128,576]{1,0:T(8,128)(2,1)S(1)} %copy.44.refs_0_, ...), custom_call_target="tpu_custom_call" | custom-call | bytes 8400896 | tf_op jit(solution)/shard_map/pallas_call | solution.py:169
  62.5 0.1 copy.49
  62.8 1.0 reshape.110.sums_ref
  63.8 1.2 copy.51
  65.0 8.4 %shard_map.95 = f32[8,2048]{1,0:T(8,128)} custom-call(bf16[1024,576]{1,0:T(8,128)(2,1)} %bitcast.67, bf16[2048,576]{1,0:T(8,128)(2,1)} %bitcast.76, f32[1024,1]{1,0:T(8,128)} %reshape.110.sums_ref, s32[8,1]{1,0:T(8,128)} %copy.55.start_ref, s32[8,1]{1,0:T(8,128)} %iota_add_fusion.position_ref), custom_call_target="tpu_custom_call" | custom-call | flops 2415919104 | bytes 3604480 | tf_op jit(solution)/shard_map/pallas_call | solution.py:203
  73.5 1.0 reduce_sum.56
  74.5 0.7 multiply_reduce_fusion.1
  75.2 0.2 fusion.3
  75.4 0.2 fusion.1
  75.7 0.1 subtract_select_fusion
  75.8 1.0 multiply_reduce_fusion
  76.7 0.7 convolution_convert_fusion
  77.5 0.7 fusion.4
  78.5 2.4 %shard_map.96 = f32[8,128,128]{2,1,0:T(8,128)S(1)} custom-call(f32[16,128,128]{2,1,0:T(8,128)S(1)} %bitcast.52), custom_call_target="tpu_custom_call" | custom-call | bytes 1048576 | tf_op jit(solution)/shard_map/pallas_call | solution.py:169
  81.0 15.8 %shard_map.97 = f32[8,128,128]{2,1,0:T(8,128)S(1)} custom-call(f32[8,128,128]{2,1,0:T(8,128)S(1)} %bitcast_add_fusion.refs_0_), custom_call_target="tpu_custom_call" | custom-call | bytes 1048576 | tf_op jit(solution)/shard_map/pallas_call | solution.py:169
  96.8 16.1 %shard_map.98 = (f32[16,8,128]{2,1,0:T(8,128)S(1)}, bf16[16,32,128]{2,1,0:T(8,128)(2,1)S(1)}, f32[16,1,32]{2,1,0:T(1,128)S(1)}) custom-call(f32[16,8,128]{2,1,0:T(8,128)S(1)} %bitcast.59, bf16[16,32,128]{2,1,0:T(8,128)(2,1)S(1)} %bitcast.58, f32[16,1,32]{2,1,0:T(1,128)S(1)} %copy.60.refs_2_), custom_call_target="tpu_custom_call" | custom-call | bytes 397312 | tf_op jit(solution)/shard_map/pallas_call | solution.py:169
  112.9 0.5 broadcast.24
  113.4 0.7 reduce.3
  114.2 0.7 copy.61
  114.9 10.7 %shard_map.99 = f32[16,8,128]{2,1,0:T(8,128)S(1)} custom-call(f32[8,128]{1,0:T(8,128)S(1)} %reduce_sum.59.refs_0_), custom_call_target="tpu_custom_call" | custom-call | bytes 131072 | tf_op jit(solution)/shard_map/pallas_call | solution.py:169
  125.6 0.6 convert_bitcast_fusion
  126.2 0.7 copy.64
  (20 shorter events, 1.0 us)
Async XLA Ops:
  8.4 0.9 copy-start
  9.3 0.8 copy-start.1
  73.5 2.2 %copy-start.2 = (f32[8,2048]{1,0:T(8,128)S(1)}, f32[8,2048]{1,0:T(8,128)}, u32[]{:S(2)}) copy-start(f32[8,2048]{1,0:T(8,128)} %shard_map.95) | copy-start | bytes 196612

commit v8 on v7

--- a/solution.py
+++ b/solution.py
@@ -52,31 +52,41 @@
     n = lax.axis_size(axis)
     me = lax.axis_index(axis)
     sibling, others = pair_peers(axis)
+    always = None
     if mode == "a2a":
         return (
-            [(lax.rem(me + s, n), lax.rem(me + s, n), me) for s in range(1, n)],
-            [(lax.rem(me + n - s, n), lax.rem(me + n - s, n)) for s in range(1, n)],
+            [(lax.rem(me + s, n), lax.rem(me + s, n), me, always) for s in range(1, n)],
+            [(lax.rem(me + n - s, n), lax.rem(me + n - s, n), always) for s in range(1, n)],
         )
     if mode == "gather":
         return (
-            [(lax.rem(me + s, n), None, me) for s in range(1, n)],
-            [(lax.rem(me + n - s, n), lax.rem(me + n - s, n)) for s in range(1, n)],
+            [(lax.rem(me + s, n), None, me, always) for s in range(1, n)],
+            [(lax.rem(me + n - s, n), lax.rem(me + n - s, n), always) for s in range(1, n)],
         )
     if mode == "sib":
         parity = lax.rem(sibling, 2)
         return (
-            [(sibling, 2 * j + parity, j) for j in range(n // 2)],
-            [(sibling, j) for j in range(n // 2)],
+            [(sibling, 2 * j + parity, j, always) for j in range(n // 2)],
+            [(sibling, j, always) for j in range(n // 2)],
         )
     if mode == "same":
+        sources = [lax.rem(me + n - 2 * s, n) for s in range(1, n // 2)]
         return (
-            [(peer, peer // 2, me // 2) for peer in others],
-            [(lax.rem(me + n - 2 * s, n), lax.rem(me + n - 2 * s, n) // 2) for s in range(1, n // 2)],
-        )
+            [(peer, peer // 2, me // 2, peer // 2 < me // 2) for peer in others],
+            [(peer, peer // 2, peer // 2 > me // 2) for peer in sources],
+        )
+    sources = [lax.rem(sibling + 2 * s, n) for s in range(1, n // 2)]
     return (
-        [(peer, None, me) for peer in [sibling] + others],
-        [(sibling, sibling)] + [(lax.rem(sibling + 2 * s, n),) * 2 for s in range(1, n // 2)],
-    )
+        [(sibling, None, me, always)] + [(peer, None, me, peer // 2 > me // 2) for peer in others],
+        [(sibling, sibling, always)] + [(peer, peer, peer // 2 < me // 2) for peer in sources],
+    )
+
+
+def when(condition, body):
+    if condition is None:
+        body()
+    else:
+        pl.when(condition)(body)
 
 
 def exchange_kernel(items, *refs):
@@ -104,23 +114,33 @@
 
     sends = []
     for i, (axis, mode, _) in enumerate(items):
-        for peer, chunk, slot in plan(axis, mode)[0]:
+        for peer, chunk, slot, condition in plan(axis, mode)[0]:
             source = x_refs[i] if chunk is None else x_refs[i].at[chunk]
             send_slot = i * stride + (chunk if mode == "sib" else peer)
             copy = remote(i, axis, source, slot, peer, send_slot, i * stride + slot)
-            copy.start()
-            sends.append(copy)
+            when(condition, copy.start)
+            sends.append((copy, condition))
     locals_ = []
     for i, (axis, mode, _) in enumerate(items):
         me = lax.axis_index(axis)
+        n = lax.axis_size(axis)
         if mode == "sib":
             continue
         if mode == "same":
             own = (x_refs[i].at[me // 2], y_refs[i].at[me // 2])
+            for j in range(n // 2):
+                def clear(j=j):
+                    y_refs[i][j] = jnp.zeros(y_refs[i].shape[1:], y_refs[i].dtype)
+                when(j < me // 2, clear)
         elif mode == "a2a":
             own = (x_refs[i].at[me], y_refs[i].at[me])
         else:
             own = (x_refs[i], y_refs[i].at[me])
+            if mode == "pair":
+                for block in range(n):
+                    def clear(block=block):
+                        y_refs[i][block] = jnp.zeros(y_refs[i].shape[1:], y_refs[i].dtype)
+                    when(block // 2 > me // 2, clear)
         copy = pltpu.make_async_copy(own[0], own[1], local_sem.at[i])
         copy.start()
         locals_.append(copy)
@@ -129,23 +149,28 @@
     for i, (axis, mode, _) in enumerate(items):
         if mode != "pair":
             continue
+        me = lax.axis_index(axis)
         sibling, others = pair_peers(axis)
         for block in others:
             arrived = remote(i, axis, y_refs[i].at[block], block, block, i * stride + block, i * stride + block)
-            arrived.wait_recv()
             copy = remote(
                 i, axis, y_refs[i].at[block], block, sibling, forward_base + i * stride + block,
                 i * stride + block,
             )
-            copy.start()
-            forwards.append(copy)
+
+            def relay(arrived=arrived, copy=copy):
+                arrived.wait_recv()
+                copy.start()
+
+            when(block // 2 < me // 2, relay)
+            forwards.append((copy, block // 2 < me // 2))
 
     for i, (axis, mode, _) in enumerate(items):
-        for peer, slot in plan(axis, mode)[1]:
+        for peer, slot, condition in plan(axis, mode)[1]:
             incoming = remote(i, axis, y_refs[i].at[slot], slot, peer, i * stride + slot, i * stride + slot)
-            incoming.wait_recv()
-    for copy in sends + forwards:
-        copy.wait_send()
+            when(condition, incoming.wait_recv)
+    for copy, condition in sends + forwards:
+        when(condition, copy.wait_send)
     for copy in locals_:
         copy.wait()
 

time: 127 us -> 125 us (0.984)
  Pallas kernels: 106 us -> 103 us
    pallas_call x5, Pallas kernels: 97.3 us -> 94.4 us  [exchange(): pl.pallas_call(functools.partial(exchange_kernel, items), out_shape=out_s...]
where the time goes in v8:
time: 125 us; the launch traced here: 124 us
  Pallas kernels  103 us (82%)
  local copies, waits for them, and re-layouts  13.6 us (11%)
  other arithmetic  4.52 us (4%)
  matrix products  2.17 us (2%)
    pallas_call x5, Pallas kernels, exchange(): pl.pallas_call(functools.partial(exchange_kernel, items), out_shape=out_s...  94.4 us
    pallas_call x1, Pallas kernels, head_mass(): pl.pallas_call(head_mass_kernel, out_shape=jax.ShapeDtypeStruct((query_ro...  8.42 us
    unnamed x12, local copies, waits for them, and re-layouts  7.83 us

profile of v8, /device:TPU:8, one launch (start us, length us, event | category | flops | bytes accessed | tf_op | source)
XLA Modules:
  0.0 124.0 jit_solution(2816294043784550594)
XLA Ops:
  0.6 0.7 dynamic_slice.7
  1.4 0.7 dynamic-slice_bitcast_fusion
  2.1 0.6 iota_add_fusion.position_ref
  2.7 0.7 copy.55.start_ref
  3.4 0.8 copy.42
  4.2 0.8 copy.43
  5.1 1.1 copy.44.refs_0_
  6.2 2.2 %copy.41 = bf16[128,8,576]{2,1,0:T(8,128)(2,1)S(1)} copy(bf16[128,8,576]{0,2,1:T(8,128)(2,1)} %param.7) | data formatting | bytes 2359296 | tf_op args[0]
  8.4 0.9 copy-done
  9.3 0.8 copy-done.1
  10.1 47.4 %shard_map.94 = (bf16[16,128,576]{2,1,0:T(8,128)(2,1)}, bf16[16,128,128]{2,1,0:T(8,128)(2,1)S(1)}, bf16[16,64,576]{2,1,0:T(8,128)(2,1)S(1)}, f32[16,1,64]{2,1,0:...) custom-call(bf16[128,576]{1,0:T(8,128)(2,1)S(1)} %copy.44.refs_0_, ...), custom_call_target="tpu_custom_call" | custom-call | bytes 8400896 | tf_op jit(solution)/shard_map/pallas_call | solution.py:194
  57.6 0.1 copy.49
  57.9 1.0 reshape.110.sums_ref
  58.9 1.2 copy.51
  60.1 8.4 %shard_map.95 = f32[8,2048]{1,0:T(8,128)} custom-call(bf16[1024,576]{1,0:T(8,128)(2,1)} %bitcast.67, bf16[2048,576]{1,0:T(8,128)(2,1)} %bitcast.76, f32[1024,1]{1,0:T(8,128)} %reshape.110.sums_ref, s32[8,1]{1,0:T(8,128)} %copy.55.start_ref, s32[8,1]{1,0:T(8,128)} %iota_add_fusion.position_ref), custom_call_target="tpu_custom_call" | custom-call | flops 2415919104 | bytes 3604480 | tf_op jit(solution)/shard_map/pallas_call | solution.py:228
  68.5 1.0 reduce_sum.56
  69.6 0.7 multiply_reduce_fusion.1
  70.3 0.2 fusion.3
  70.5 0.2 fusion.1
  70.7 0.1 subtract_select_fusion
  70.8 1.0 multiply_reduce_fusion
  71.8 0.7 convolution_convert_fusion
  72.5 0.7 fusion.4
  73.5 2.4 %shard_map.96 = f32[8,128,128]{2,1,0:T(8,128)S(1)} custom-call(f32[16,128,128]{2,1,0:T(8,128)S(1)} %bitcast.52), custom_call_target="tpu_custom_call" | custom-call | bytes 1048576 | tf_op jit(solution)/shard_map/pallas_call | solution.py:194
  76.1 20.1 %shard_map.97 = f32[8,128,128]{2,1,0:T(8,128)S(1)} custom-call(f32[8,128,128]{2,1,0:T(8,128)S(1)} %bitcast_add_fusion.refs_0_), custom_call_target="tpu_custom_call" | custom-call | bytes 1048576 | tf_op jit(solution)/shard_map/pallas_call | solution.py:194
  96.2 13.8 %shard_map.98 = (f32[16,8,128]{2,1,0:T(8,128)S(1)}, bf16[16,32,128]{2,1,0:T(8,128)(2,1)S(1)}, f32[16,1,32]{2,1,0:T(1,128)S(1)}) custom-call(f32[16,8,128]{2,1,0:T(8,128)S(1)} %bitcast.59, bf16[16,32,128]{2,1,0:T(8,128)(2,1)S(1)} %bitcast.58, f32[16,1,32]{2,1,0:T(1,128)S(1)} %copy.60.refs_2_), custom_call_target="tpu_custom_call" | custom-call | bytes 397312 | tf_op jit(solution)/shard_map/pallas_call | solution.py:194
  110.1 0.5 broadcast.24
  110.6 0.7 reduce.3
  111.4 0.7 copy.61
  112.0 10.7 %shard_map.99 = f32[16,8,128]{2,1,0:T(8,128)S(1)} custom-call(f32[8,128]{1,0:T(8,128)S(1)} %reduce_sum.59.refs_0_), custom_call_target="tpu_custom_call" | custom-call | bytes 131072 | tf_op jit(solution)/shard_map/pallas_call | solution.py:194
  122.7 0.6 convert_bitcast_fusion
  123.3 0.7 copy.64
  (20 shorter events, 1.0 us)
Async XLA Ops:
  8.4 0.9 copy-start
  9.3 0.8 copy-start.1
  68.5 2.2 %copy-start.2 = (f32[8,2048]{1,0:T(8,128)S(1)}, f32[8,2048]{1,0:T(8,128)}, u32[]{:S(2)}) copy-start(f32[8,2048]{1,0:T(8,128)} %shard_map.95) | copy-start | bytes 196612

commit v9 on v8

--- a/solution.py
+++ b/solution.py
@@ -113,7 +113,9 @@
     pl.semaphore_wait(barrier, len(peers))
 
     sends = []
-    for i, (axis, mode, _) in enumerate(items):
+    order = sorted(range(count), key=lambda i: items[i][0] != "ha")
+    for i in order:
+        axis, mode, _ = items[i]
         for peer, chunk, slot, condition in plan(axis, mode)[0]:
             source = x_refs[i] if chunk is None else x_refs[i].at[chunk]
             send_slot = i * stride + (chunk if mode == "sib" else peer)
@@ -223,7 +225,7 @@
 def head_mass(flat_query, latent_piece, flat_sums, window_start, positions):
     query_rows = window_start.shape[0]
     tokens, latent_width = latent_piece.shape
-    width = math.gcd(tokens, 256)
+    width = math.gcd(tokens, 512)
     flat_rows = flat_query.shape[0]
     return pl.pallas_call(
         head_mass_kernel,

time: 125 us -> 124 us (level)
  Pallas kernels: 103 us -> 101 us
    pallas_call x1, Pallas kernels: 8.42 us -> 6.87 us  [head_mass(): pl.pallas_call(head_mass_kernel, out_shape=jax.ShapeDtypeStruct((query_ro...]
where the time goes in v9:
time: 124 us; the launch traced here: 123 us
  Pallas kernels  101 us (81%)
  local copies, waits for them, and re-layouts  13.6 us (11%)
  other arithmetic  4.52 us (4%)
  matrix products  2.17 us (2%)
    pallas_call x5, Pallas kernels, exchange(): pl.pallas_call(functools.partial(exchange_kernel, items), out_shape=out_s...  94.5 us
    unnamed x12, local copies, waits for them, and re-layouts  7.83 us
    pallas_call x1, Pallas kernels, head_mass(): pl.pallas_call(head_mass_kernel, out_shape=jax.ShapeDtypeStruct((query_ro...  6.87 us

profile of v9, /device:TPU:8, one launch (start us, length us, event | category | flops | bytes accessed | tf_op | source)
XLA Modules:
  0.0 122.5 jit_solution(17034289732710150575)
XLA Ops:
  0.6 0.7 dynamic_slice.7
  1.4 0.7 dynamic-slice_bitcast_fusion
  2.1 0.6 iota_add_fusion.position_ref
  2.7 0.7 copy.55.start_ref
  3.4 0.8 copy.42
  4.2 0.8 copy.43
  5.1 1.1 copy.44.refs_0_
  6.2 2.2 %copy.41 = bf16[128,8,576]{2,1,0:T(8,128)(2,1)S(1)} copy(bf16[128,8,576]{0,2,1:T(8,128)(2,1)} %param.7) | data formatting | bytes 2359296 | tf_op args[0]
  8.4 0.9 copy-done
  9.3 0.8 copy-done.1
  10.1 47.3 %shard_map.94 = (bf16[16,128,576]{2,1,0:T(8,128)(2,1)}, bf16[16,128,128]{2,1,0:T(8,128)(2,1)S(1)}, bf16[16,64,576]{2,1,0:T(8,128)(2,1)S(1)}, f32[16,1,64]{2,1,0:...) custom-call(bf16[128,576]{1,0:T(8,128)(2,1)S(1)} %copy.44.refs_0_, ...), custom_call_target="tpu_custom_call" | custom-call | bytes 8400896 | tf_op jit(solution)/shard_map/pallas_call | solution.py:196
  57.6 0.1 copy.49
  57.9 1.0 reshape.110.sums_ref
  58.9 1.2 copy.51
  60.1 6.9 %shard_map.95 = f32[8,2048]{1,0:T(8,128)} custom-call(bf16[1024,576]{1,0:T(8,128)(2,1)} %bitcast.67, bf16[2048,576]{1,0:T(8,128)(2,1)} %bitcast.76, f32[1024,1]{1,0:T(8,128)} %reshape.110.sums_ref, s32[8,1]{1,0:T(8,128)} %copy.55.start_ref, s32[8,1]{1,0:T(8,128)} %iota_add_fusion.position_ref), custom_call_target="tpu_custom_call" | custom-call | flops 2415919104 | bytes 3604480 | tf_op jit(solution)/shard_map/pallas_call | solution.py:230
  67.0 1.0 reduce_sum.56
  68.0 0.7 multiply_reduce_fusion.1
  68.7 0.2 fusion.3
  68.9 0.2 fusion.1
  69.2 0.1 subtract_select_fusion
  69.3 1.0 multiply_reduce_fusion
  70.2 0.7 convolution_convert_fusion
  70.9 0.7 fusion.4
  72.0 2.4 %shard_map.96 = f32[8,128,128]{2,1,0:T(8,128)S(1)} custom-call(f32[16,128,128]{2,1,0:T(8,128)S(1)} %bitcast.52), custom_call_target="tpu_custom_call" | custom-call | bytes 1048576 | tf_op jit(solution)/shard_map/pallas_call | solution.py:196
  74.5 20.2 %shard_map.97 = f32[8,128,128]{2,1,0:T(8,128)S(1)} custom-call(f32[8,128,128]{2,1,0:T(8,128)S(1)} %bitcast_add_fusion.refs_0_), custom_call_target="tpu_custom_call" | custom-call | bytes 1048576 | tf_op jit(solution)/shard_map/pallas_call | solution.py:196
  94.8 13.9 %shard_map.98 = (f32[16,8,128]{2,1,0:T(8,128)S(1)}, bf16[16,32,128]{2,1,0:T(8,128)(2,1)S(1)}, f32[16,1,32]{2,1,0:T(1,128)S(1)}) custom-call(f32[16,8,128]{2,1,0:T(8,128)S(1)} %bitcast.59, bf16[16,32,128]{2,1,0:T(8,128)(2,1)S(1)} %bitcast.58, f32[16,1,32]{2,1,0:T(1,128)S(1)} %copy.60.refs_2_), custom_call_target="tpu_custom_call" | custom-call | bytes 397312 | tf_op jit(solution)/shard_map/pallas_call | solution.py:196
  108.6 0.5 broadcast.24
  109.2 0.7 reduce.3
  109.9 0.7 copy.61
  110.6 10.7 %shard_map.99 = f32[16,8,128]{2,1,0:T(8,128)S(1)} custom-call(f32[8,128]{1,0:T(8,128)S(1)} %reduce_sum.59.refs_0_), custom_call_target="tpu_custom_call" | custom-call | bytes 131072 | tf_op jit(solution)/shard_map/pallas_call | solution.py:196
  121.3 0.6 convert_bitcast_fusion
  121.9 0.7 copy.64
  (20 shorter events, 1.0 us)
Async XLA Ops:
  8.4 0.9 copy-start
  9.3 0.8 copy-start.1
  67.0 2.2 %copy-start.2 = (f32[8,2048]{1,0:T(8,128)S(1)}, f32[8,2048]{1,0:T(8,128)}, u32[]{:S(2)}) copy-start(f32[8,2048]{1,0:T(8,128)} %shard_map.95) | copy-start | bytes 196612

commit v10 on v9

--- a/solution.py
+++ b/solution.py
@@ -110,7 +110,8 @@
     peers = barrier_peers(items)
     for axis, peer in peers:
         pl.semaphore_signal(barrier, inc=1, device_id=device_of(axis, peer), device_id_type=MESH)
-    pl.semaphore_wait(barrier, len(peers))
+    if peers:
+        pl.semaphore_wait(barrier, len(peers))
 
     sends = []
     order = sorted(range(count), key=lambda i: items[i][0] != "ha")
@@ -210,41 +211,48 @@
     )(*arrays)
 
 
-def head_mass_kernel(query_ref, latent_ref, sums_ref, start_ref, position_ref, out_ref):
+def head_mass_kernel(query_rows, starts_ref, query_ref, latent_ref, sums_ref, out_ref):
     rows, width = out_ref.shape
     scores = lax.dot_general(
         query_ref[...], latent_ref[...], (((1,), (1,)), ((), ())), preferred_element_type=jnp.float32
     )
     mass = jnp.exp(scores * main_scale - sums_ref[...])
     mass = jnp.sum(mass.reshape(rows, mass.shape[0] // rows, width), axis=1)
+    own_first = lax.axis_index("ha") * rows
+    row_ids = lax.broadcasted_iota(jnp.int32, (rows, width), 0)
+    starts = jnp.zeros((rows, width), jnp.int32)
+    for row in range(rows):
+        starts = jnp.where(row_ids == row, starts_ref[own_first + row], starts)
+    positions = lax.axis_index("pb") * query_rows + own_first + row_ids
     columns = pl.program_id(0) * width + lax.broadcasted_iota(jnp.int32, (rows, width), 1)
-    seen = (columns >= start_ref[...]) & (columns <= position_ref[...])
+    seen = (columns >= starts) & (columns <= positions)
     out_ref[...] = jnp.where(seen, mass, 0.0)
 
 
-def head_mass(flat_query, latent_piece, flat_sums, window_start, positions):
+def head_mass(flat_query, latent_piece, flat_sums, window_start, rows):
     query_rows = window_start.shape[0]
     tokens, latent_width = latent_piece.shape
     width = math.gcd(tokens, 512)
     flat_rows = flat_query.shape[0]
     return pl.pallas_call(
-        head_mass_kernel,
-        out_shape=jax.ShapeDtypeStruct((query_rows, tokens), jnp.float32),
-        grid=(tokens // width,),
-        in_specs=[
-            pl.BlockSpec((flat_rows, latent_width), lambda k: (0, 0)),
-            pl.BlockSpec((width, latent_width), lambda k: (k, 0)),
-            pl.BlockSpec((flat_rows, 1), lambda k: (0, 0)),
-            pl.BlockSpec((query_rows, 1), lambda k: (0, 0)),
-            pl.BlockSpec((query_rows, 1), lambda k: (0, 0)),
-        ],
-        out_specs=pl.BlockSpec((query_rows, width), lambda k: (0, k)),
+        functools.partial(head_mass_kernel, query_rows),
+        out_shape=jax.ShapeDtypeStruct((rows, tokens), jnp.float32),
+        grid_spec=pltpu.PrefetchScalarGridSpec(
+            num_scalar_prefetch=1,
+            grid=(tokens // width,),
+            in_specs=[
+                pl.BlockSpec((flat_rows, latent_width), lambda k, starts: (0, 0)),
+                pl.BlockSpec((width, latent_width), lambda k, starts: (k, 0)),
+                pl.BlockSpec((flat_rows, 1), lambda k, starts: (0, 0)),
+            ],
+            out_specs=pl.BlockSpec((rows, width), lambda k, starts: (0, k)),
+        ),
         cost_estimate=pl.CostEstimate(
             flops=2 * flat_rows * tokens * latent_width,
             transcendentals=flat_rows * tokens,
-            bytes_accessed=flat_query.size * 2 + latent_piece.size * 2 + query_rows * tokens * 4,
+            bytes_accessed=flat_query.size * 2 + latent_piece.size * 2 + rows * tokens * 4,
         ),
-    )(flat_query, latent_piece, flat_sums, window_start[:, None], positions[:, None])
+    )(window_start, flat_query, latent_piece, flat_sums)
 
 
 def on_device(main_query, latent, log_sums, window_start, index_query, index_key, index_weight):
@@ -300,7 +308,7 @@
     own_positions = row_first + jnp.arange(own_rows, dtype=jnp.int32)
     own_start = lax.dynamic_slice_in_dim(window_start, lax.axis_index("ha") * own_rows, own_rows, 0)
 
-    probs_all = head_mass(local_query, latent_piece, local_sums, own_start, own_positions)
+    probs_all = head_mass(local_query, latent_piece, local_sums, window_start, own_rows)
 
     flat_index = local_index.reshape(own_rows * index_heads, index_width)
     active = jnp.einsum("rd,kd->rk", flat_index, keys_all, preferred_element_type=jnp.float32)

time: 124 us -> 122 us (0.984)
  local copies, waits for them, and re-layouts: 13.6 us -> 12.2 us
    broadcast_in_dim x2 -> x0, local copies, waits for them, and re-layouts: 1.4 us -> none  [visible(): window_start[:, None]]
where the time goes in v10:
time: 122 us; the launch traced here: 121 us
  Pallas kernels  102 us (84%)
  local copies, waits for them, and re-layouts  12.2 us (10%)
  other arithmetic  3.93 us (3%)
  matrix products  2.17 us (2%)
    pallas_call x5, Pallas kernels, exchange(): pl.pallas_call(functools.partial(exchange_kernel, items), out_shape=out_s...  94.5 us
    unnamed x12, local copies, waits for them, and re-layouts  7.83 us
    pallas_call x1, Pallas kernels, head_mass(): pl.pallas_call(functools.partial(head_mass_kernel, query_rows), out_shape...  7.46 us

profile of v10, /device:TPU:8, one launch (start us, length us, event | category | flops | bytes accessed | tf_op | source)
XLA Modules:
  0.0 121.1 jit_solution(5779865124399852697)
XLA Ops:
  0.7 0.7 dynamic_slice.7
  1.4 0.8 copy.40
  2.3 0.8 copy.41
  3.1 1.1 copy.42.refs_0_
  4.2 2.2 %copy.39 = bf16[128,8,576]{2,1,0:T(8,128)(2,1)S(1)} copy(bf16[128,8,576]{0,2,1:T(8,128)(2,1)} %param.7) | data formatting | bytes 2359296 | tf_op args[0]
  6.4 0.9 copy-done
  7.3 0.8 copy-done.1
  8.1 47.3 %shard_map.94 = (bf16[16,128,576]{2,1,0:T(8,128)(2,1)}, bf16[16,128,128]{2,1,0:T(8,128)(2,1)S(1)}, bf16[16,64,576]{2,1,0:T(8,128)(2,1)S(1)}, f32[16,1,64]{2,1,0:...) custom-call(bf16[128,576]{1,0:T(8,128)(2,1)S(1)} %copy.42.refs_0_, ...), custom_call_target="tpu_custom_call" | custom-call | bytes 8400896 | tf_op jit(solution)/shard_map/pallas_call | solution.py:197
  55.6 0.1 copy.47
  55.7 0.1 copy.50
  55.9 1.0 reshape.106.sums_ref
  56.9 1.2 copy.49
  58.1 7.5 %shard_map.95 = f32[8,2048]{1,0:T(8,128)} custom-call(s32[128]{0:T(128)} %starts_ref.1, bf16[1024,576]{1,0:T(8,128)(2,1)} %bitcast.65, bf16[2048,576]{1,0:T(8,128)(2,1)} %bitcast.74, f32[1024,1]{1,0:T(8,128)} %reshape.106.sums_ref), custom_call_target="tpu_custom_call" | custom-call | flops 2415919104 | bytes 3604480 | tf_op jit(solution)/shard_map/pallas_call | solution.py:237
  65.6 1.0 reduce_sum.56
  66.6 0.7 multiply_reduce_fusion.1
  67.3 0.2 fusion.3
  67.5 0.2 fusion.1
  67.8 0.1 subtract_select_fusion
  67.9 1.0 multiply_reduce_fusion
  68.8 0.7 convolution_convert_fusion
  69.5 0.7 fusion.4
  70.3 0.1 copy.55
  70.4 0.1 copy.56
  70.6 2.4 %shard_map.96 = f32[8,128,128]{2,1,0:T(8,128)S(1)} custom-call(f32[16,128,128]{2,1,0:T(8,128)S(1)} %bitcast.50), custom_call_target="tpu_custom_call" | custom-call | bytes 1048576 | tf_op jit(solution)/shard_map/pallas_call | solution.py:197
  73.1 20.2 %shard_map.97 = f32[8,128,128]{2,1,0:T(8,128)S(1)} custom-call(f32[8,128,128]{2,1,0:T(8,128)S(1)} %bitcast_add_fusion.refs_0_), custom_call_target="tpu_custom_call" | custom-call | bytes 1048576 | tf_op jit(solution)/shard_map/pallas_call | solution.py:197
  93.4 13.9 %shard_map.98 = (f32[16,8,128]{2,1,0:T(8,128)S(1)}, bf16[16,32,128]{2,1,0:T(8,128)(2,1)S(1)}, f32[16,1,32]{2,1,0:T(1,128)S(1)}) custom-call(f32[16,8,128]{2,1,0:T(8,128)S(1)} %bitcast.57, bf16[16,32,128]{2,1,0:T(8,128)(2,1)S(1)} %bitcast.56, f32[16,1,32]{2,1,0:T(1,128)S(1)} %copy.57.refs_2_), custom_call_target="tpu_custom_call" | custom-call | bytes 397312 | tf_op jit(solution)/shard_map/pallas_call | solution.py:197
  107.3 0.5 broadcast.20
  107.8 0.7 reduce.3
  108.5 0.7 copy.58
  109.2 10.7 %shard_map.99 = f32[16,8,128]{2,1,0:T(8,128)S(1)} custom-call(f32[8,128]{1,0:T(8,128)S(1)} %reduce_sum.59.refs_0_), custom_call_target="tpu_custom_call" | custom-call | bytes 131072 | tf_op jit(solution)/shard_map/pallas_call | solution.py:197
  119.9 0.6 convert_bitcast_fusion
  120.5 0.7 copy.61
  (17 shorter events, 0.7 us)
Async XLA Ops:
  6.4 0.9 copy-start
  7.3 0.8 copy-start.1
  65.6 2.2 %copy-start.2 = (f32[8,2048]{1,0:T(8,128)S(1)}, f32[8,2048]{1,0:T(8,128)}, u32[]{:S(2)}) copy-start(f32[8,2048]{1,0:T(8,128)} %shard_map.95) | copy-start | bytes 196612

commit v11 on v10

--- a/solution.py
+++ b/solution.py
@@ -211,13 +211,14 @@
     )(*arrays)
 
 
-def head_mass_kernel(query_rows, starts_ref, query_ref, latent_ref, sums_ref, out_ref):
+def head_mass_kernel(query_rows, sources, starts_ref, query_ref, latent_ref, sums_ref, out_ref):
     rows, width = out_ref.shape
     scores = lax.dot_general(
         query_ref[...], latent_ref[...], (((1,), (1,)), ((), ())), preferred_element_type=jnp.float32
     )
     mass = jnp.exp(scores * main_scale - sums_ref[...])
-    mass = jnp.sum(mass.reshape(rows, mass.shape[0] // rows, width), axis=1)
+    heads = mass.shape[0] // (rows * sources)
+    mass = jnp.sum(mass.reshape(sources, rows, heads, width), axis=(0, 2))
     own_first = lax.axis_index("ha") * rows
     row_ids = lax.broadcasted_iota(jnp.int32, (rows, width), 0)
     starts = jnp.zeros((rows, width), jnp.int32)
@@ -229,13 +230,13 @@
     out_ref[...] = jnp.where(seen, mass, 0.0)
 
 
-def head_mass(flat_query, latent_piece, flat_sums, window_start, rows):
+def head_mass(flat_query, latent_piece, flat_sums, window_start, rows, sources):
     query_rows = window_start.shape[0]
     tokens, latent_width = latent_piece.shape
     width = math.gcd(tokens, 512)
     flat_rows = flat_query.shape[0]
     return pl.pallas_call(
-        functools.partial(head_mass_kernel, query_rows),
+        functools.partial(head_mass_kernel, query_rows, sources),
         out_shape=jax.ShapeDtypeStruct((rows, tokens), jnp.float32),
         grid_spec=pltpu.PrefetchScalarGridSpec(
             num_scalar_prefetch=1,
@@ -288,14 +289,8 @@
     )
     latent_piece = latent_parts.reshape(tokens, latent_width)
     keys_all = key_parts.reshape(tokens, index_width)
-    local_query = (
-        query_parts.reshape(groups, own_rows, head_count, latent_width)
-        .transpose(1, 0, 2, 3)
-        .reshape(own_rows * all_heads, latent_width)
-    )
-    local_sums = (
-        sums_parts.reshape(groups, own_rows, head_count).transpose(1, 0, 2).reshape(own_rows * all_heads, 1)
-    )
+    local_query = query_parts.reshape(own_rows * all_heads, latent_width)
+    local_sums = sums_parts.reshape(own_rows * all_heads, 1)
     local_index = (
         index_parts.reshape(groups, own_rows, part_heads, index_width)
         .transpose(1, 0, 2, 3)
@@ -308,7 +303,7 @@
     own_positions = row_first + jnp.arange(own_rows, dtype=jnp.int32)
     own_start = lax.dynamic_slice_in_dim(window_start, lax.axis_index("ha") * own_rows, own_rows, 0)
 
-    probs_all = head_mass(local_query, latent_piece, local_sums, window_start, own_rows)
+    probs_all = head_mass(local_query, latent_piece, local_sums, window_start, own_rows, groups)
 
     flat_index = local_index.reshape(own_rows * index_heads, index_width)
     active = jnp.einsum("rd,kd->rk", flat_index, keys_all, preferred_element_type=jnp.float32)

time: 122 us -> 123 us (level)
    unnamed x12 -> x14, local copies, waits for them, and re-layouts: 7.83 us -> 8.9 us
where the time goes in v11:
time: 123 us; the launch traced here: 122 us
  Pallas kernels  102 us (83%)
  local copies, waits for them, and re-layouts  12.2 us (10%)
  other arithmetic  4.61 us (4%)
  matrix products  2.17 us (2%)
    pallas_call x5, Pallas kernels, exchange(): pl.pallas_call(functools.partial(exchange_kernel, items), out_shape=out_s...  94.5 us
    unnamed x14, local copies, waits for them, and re-layouts  8.9 us
    pallas_call x1, Pallas kernels, head_mass(): pl.pallas_call(functools.partial(head_mass_kernel, query_rows, sources),...  7.49 us

profile of v11, /device:TPU:8, one launch (start us, length us, event | category | flops | bytes accessed | tf_op | source)
XLA Modules:
  0.0 121.8 jit_solution(3282153835407190355)
XLA Ops:
  0.7 0.7 dynamic_slice.7
  1.4 0.8 copy.35
  2.3 0.8 copy.36
  3.1 1.1 copy.37.refs_0_
  4.2 2.2 %copy.34 = bf16[128,8,576]{2,1,0:T(8,128)(2,1)S(1)} copy(bf16[128,8,576]{0,2,1:T(8,128)(2,1)} %param.7) | data formatting | bytes 2359296 | tf_op args[0]
  6.4 0.9 copy-done
  7.3 0.8 copy-done.1
  8.1 47.3 %shard_map.94 = (bf16[16,128,576]{2,1,0:T(8,128)(2,1)}, bf16[16,128,128]{2,1,0:T(8,128)(2,1)S(1)}, bf16[16,64,576]{2,1,0:T(8,128)(2,1)S(1)}, f32[16,1,64]{2,1,0:...) custom-call(bf16[128,576]{1,0:T(8,128)(2,1)S(1)} %copy.37.refs_0_, ...), custom_call_target="tpu_custom_call" | custom-call | bytes 8400896 | tf_op jit(solution)/shard_map/pallas_call | solution.py:197
  55.4 1.1 copy-done.2
  56.6 0.5 broadcast.23
  57.1 0.7 reduce.6
  57.8 0.1 copy.42
  58.0 1.3 %reshape.98.sums_ref = f32[1024,1]{1,0:T(8,128)} reshape(f32[16,64]{1,0:T(8,128)S(1)} %reduce.6) | data formatting | bytes 8192 | tf_op jit(solution)/shard_map/reshape | solution.py:293
  59.3 7.5 %shard_map.95 = f32[8,2048]{1,0:T(8,128)} custom-call(s32[128]{0:T(128)} %starts_ref.1, bf16[1024,576]{1,0:T(8,128)(2,1)} %bitcast.56, bf16[2048,576]{1,0:T(8,128)(2,1)} %bitcast.66, f32[1024,1]{1,0:T(8,128)} %reshape.98.sums_ref), custom_call_target="tpu_custom_call" | custom-call | flops 2415919104 | bytes 3604480 | tf_op jit(solution)/shard_map/pallas_call | solution.py:238
  66.8 1.0 reduce_sum.56
  67.8 0.7 multiply_reduce_fusion.1
  68.5 0.2 fusion.3
  68.7 0.2 fusion.1
  69.0 0.1 subtract_select_fusion
  69.1 1.0 multiply_reduce_fusion
  70.0 0.7 convolution_convert_fusion
  70.8 0.7 fusion.4
  71.5 0.1 copy.47
  71.6 0.1 copy.48
  71.8 2.4 %shard_map.96 = f32[8,128,128]{2,1,0:T(8,128)S(1)} custom-call(f32[16,128,128]{2,1,0:T(8,128)S(1)} %bitcast.44), custom_call_target="tpu_custom_call" | custom-call | bytes 1048576 | tf_op jit(solution)/shard_map/pallas_call | solution.py:197
  74.3 20.2 %shard_map.97 = f32[8,128,128]{2,1,0:T(8,128)S(1)} custom-call(f32[8,128,128]{2,1,0:T(8,128)S(1)} %bitcast_add_fusion.refs_0_), custom_call_target="tpu_custom_call" | custom-call | bytes 1048576 | tf_op jit(solution)/shard_map/pallas_call | solution.py:197
  94.6 13.9 %shard_map.98 = (f32[16,8,128]{2,1,0:T(8,128)S(1)}, bf16[16,32,128]{2,1,0:T(8,128)(2,1)S(1)}, f32[16,1,32]{2,1,0:T(1,128)S(1)}) custom-call(f32[16,8,128]{2,1,0:T(8,128)S(1)} %bitcast.50, bf16[16,32,128]{2,1,0:T(8,128)(2,1)S(1)} %bitcast.49, f32[16,1,32]{2,1,0:T(1,128)S(1)} %copy.49.refs_2_), custom_call_target="tpu_custom_call" | custom-call | bytes 397312 | tf_op jit(solution)/shard_map/pallas_call | solution.py:197
  108.5 0.7 reduce.7
  109.2 0.7 copy.50
  109.9 10.7 %shard_map.99 = f32[16,8,128]{2,1,0:T(8,128)S(1)} custom-call(f32[8,128]{1,0:T(8,128)S(1)} %reduce_sum.59.refs_0_), custom_call_target="tpu_custom_call" | custom-call | bytes 131072 | tf_op jit(solution)/shard_map/pallas_call | solution.py:197
  120.6 0.6 convert_bitcast_fusion
  121.2 0.7 copy.53
  (17 shorter events, 0.7 us)
Async XLA Ops:
  6.4 0.9 copy-start
  7.3 0.8 copy-start.1
  55.4 1.1 copy-start.2
  66.8 2.2 %copy-start.3 = (f32[8,2048]{1,0:T(8,128)S(1)}, f32[8,2048]{1,0:T(8,128)}, u32[]{:S(2)}) copy-start(f32[8,2048]{1,0:T(8,128)} %shard_map.95) | copy-start | bytes 196612

commit v12 on v10

--- a/solution.py
+++ b/solution.py
@@ -255,6 +255,64 @@
     )(window_start, flat_query, latent_piece, flat_sums)
 
 
+def indexer_kernel(query_rows, starts_ref, index_ref, keys_ref, weight_ref, probs_ref, qgrad_ref, wgrad_ref,
+                   kgrad_ref):
+    rows, tokens = probs_ref.shape
+    flat = index_ref.shape[0]
+    heads = flat // rows
+    index = index_ref[...]
+    keys = keys_ref[...]
+    weight = weight_ref[...]
+    active = lax.dot_general(index, keys, (((1,), (1,)), ((), ())), preferred_element_type=jnp.float32)
+    relu_act = jnp.maximum(active, 0.0)
+    logits = jnp.sum((weight * relu_act).reshape(rows, heads, tokens), axis=1)
+
+    own_first = lax.axis_index("ha") * rows
+    row_ids = lax.broadcasted_iota(jnp.int32, (rows, tokens), 0)
+    starts = jnp.zeros((rows, tokens), jnp.int32)
+    for row in range(rows):
+        starts = jnp.where(row_ids == row, starts_ref[own_first + row], starts)
+    positions = lax.axis_index("pb") * query_rows + own_first + row_ids
+    columns = lax.broadcasted_iota(jnp.int32, (rows, tokens), 1)
+    seen = (columns >= starts) & (columns <= positions)
+
+    probs = probs_ref[...]
+    target = probs / jnp.sum(probs, axis=1, keepdims=True)
+    masked = jnp.where(seen, logits, very_low)
+    row_top = jnp.max(masked, axis=1, keepdims=True)
+    expo = jnp.where(seen, jnp.exp(masked - row_top), 0.0)
+    grad = jnp.where(seen, expo / jnp.sum(expo, axis=1, keepdims=True) - target, 0.0)
+    grad = jnp.broadcast_to(grad[:, None, :], (rows, heads, tokens)).reshape(flat, tokens)
+
+    wgrad_ref[...] = jnp.sum(grad * relu_act, axis=1, keepdims=True)
+    coeffs = jnp.where(active > 0.0, grad * weight, 0.0).astype(jnp.bfloat16)
+    qgrad_ref[...] = jnp.dot(coeffs, keys, preferred_element_type=jnp.float32).astype(qgrad_ref.dtype)
+    kgrad_ref[...] = lax.dot_general(
+        coeffs, index, (((0,), (0,)), ((), ())), preferred_element_type=jnp.float32
+    )
+
+
+def indexer_grads(flat_index, keys_all, flat_weight, probs_all, window_start):
+    flat, width = flat_index.shape
+    rows, tokens = probs_all.shape
+    vmem = pltpu.MemorySpace.VMEM
+    return pl.pallas_call(
+        functools.partial(indexer_kernel, window_start.shape[0]),
+        out_shape=(
+            jax.ShapeDtypeStruct((flat, width), jnp.bfloat16),
+            jax.ShapeDtypeStruct((flat, 1), jnp.float32),
+            jax.ShapeDtypeStruct((tokens, width), jnp.float32),
+        ),
+        in_specs=[pl.BlockSpec(memory_space=pltpu.SMEM)] + [pl.BlockSpec(memory_space=vmem)] * 4,
+        out_specs=[pl.BlockSpec(memory_space=vmem)] * 3,
+        compiler_params=pltpu.CompilerParams(vmem_limit_bytes=56 * 1024 * 1024),
+        cost_estimate=pl.CostEstimate(
+            flops=6 * flat * tokens * width, transcendentals=rows * tokens,
+            bytes_accessed=(flat + tokens) * width * 2 + tokens * width * 4,
+        ),
+    )(window_start, flat_index, keys_all, flat_weight, probs_all)
+
+
 def on_device(main_query, latent, log_sums, window_start, index_query, index_key, index_weight):
     query_rows, head_count, latent_width = main_query.shape
     index_width = index_query.shape[2]
@@ -311,25 +369,10 @@
     probs_all = head_mass(local_query, latent_piece, local_sums, window_start, own_rows)
 
     flat_index = local_index.reshape(own_rows * index_heads, index_width)
-    active = jnp.einsum("rd,kd->rk", flat_index, keys_all, preferred_element_type=jnp.float32)
-    active = active.reshape(own_rows, index_heads, tokens)
-    relu_act = jnp.maximum(active, 0.0)
-    logit_all = jnp.sum(local_weight[:, :, None] * relu_act, axis=1)
-
-    visible_all = visible(own_start, own_positions, 0, tokens)
-    target = probs_all / jnp.sum(probs_all, axis=1, keepdims=True)
-    masked = jnp.where(visible_all, logit_all, very_low)
-    row_top = jnp.max(masked, axis=1, keepdims=True)
-    expo = jnp.where(visible_all, jnp.exp(masked - row_top), 0.0)
-    logit_grad = jnp.where(visible_all, expo / jnp.sum(expo, axis=1, keepdims=True) - target, 0.0)
-
-    weight_grad = jnp.sum(logit_grad[:, None, :] * relu_act, axis=2)
-    coeffs = jnp.where(
-        active > 0.0, logit_grad[:, None, :] * local_weight[:, :, None], 0.0
-    ).astype(jnp.bfloat16)
-    coeffs = coeffs.reshape(own_rows * index_heads, tokens)
-    query_grad = jnp.dot(coeffs, keys_all, preferred_element_type=jnp.float32)
-    key_grad = jnp.einsum("rk,rd->kd", coeffs, flat_index, preferred_element_type=jnp.float32)
+    query_grad, weight_grad, key_grad = indexer_grads(
+        flat_index, keys_all, local_weight.reshape(own_rows * index_heads, 1), probs_all, window_start
+    )
+    weight_grad = weight_grad.reshape(own_rows, index_heads)
 
     query_grad = query_grad.astype(jnp.bfloat16).reshape(own_rows, groups, part_heads, index_width)
     key_grad = key_grad.reshape(blocks, query_rows, index_width)

time: 122 us -> 122 us (level)
  Pallas kernels: 102 us -> 107 us
  other arithmetic: 3.93 us -> 1.54 us
  matrix products: 2.17 us -> 0 us
  local copies, waits for them, and re-layouts: 12.2 us -> 10.5 us
    pallas_call x0 -> x1, Pallas kernels: none -> 5.06 us  [indexer_grads(): pl.pallas_call(functools.partial(indexer_kernel, window_start.shape[0]),...]
    unnamed x12 -> x24, local copies, waits for them, and re-layouts: 7.83 us -> 5.27 us
    reduce_sum x3 -> x0, other arithmetic: 2.23 us -> none  [the longest x1 1.04 us: on_device(): target = probs_all / jnp.sum(probs_all, axis=1, keepdims=True)]
    dot_general x3 -> x0, matrix products: 2.17 us -> none  [the longest x1 0.74 us: on_device(): jnp.einsum('rk,rd->kd', coeffs, flat_index, preferred_element_type=jnp.fl...]
where the time goes in v12:
time: 122 us; the launch traced here: 120 us
  Pallas kernels  107 us (88%)
  local copies, waits for them, and re-layouts  10.5 us (9%)
  other arithmetic  1.54 us (1%)
    pallas_call x5, Pallas kernels, exchange(): pl.pallas_call(functools.partial(exchange_kernel, items), out_shape=out_s...  94.8 us
    pallas_call x1, Pallas kernels, head_mass(): pl.pallas_call(functools.partial(head_mass_kernel, query_rows), out_shape...  7.45 us
    unnamed x24, local copies, waits for them, and re-layouts  5.27 us
    pallas_call x1, Pallas kernels, indexer_grads(): pl.pallas_call(functools.partial(indexer_kernel, window_start.shape[0]),...  5.06 us

profile of v12, /device:TPU:8, one launch (start us, length us, event | category | flops | bytes accessed | tf_op | source)
XLA Modules:
  0.0 120.2 jit_solution(13426008157357905569)
XLA Ops:
  0.7 2.3 %copy.22 = bf16[128,8,576]{2,1,0:T(8,128)(2,1)S(1)} copy(bf16[128,8,576]{0,2,1:T(8,128)(2,1)} %param.7) | data formatting | bytes 2359296 | tf_op args[0]
  3.0 0.2 copy.25.refs_0_
  3.2 0.1 copy.23
  3.3 0.1 reshape.66
  3.4 0.1 copy.24
  3.5 0.1 reshape.68
  3.6 47.5 %shard_map.94 = (bf16[16,128,576]{2,1,0:T(8,128)(2,1)}, bf16[16,128,128]{2,1,0:T(8,128)(2,1)S(1)}, bf16[16,64,576]{2,1,0:T(8,128)(2,1)S(1)}, f32[16,1,64]{2,1,0:...) custom-call(bf16[128,576]{1,0:T(8,128)(2,1)S(1)} %copy.25.refs_0_, ...), custom_call_target="tpu_custom_call" | custom-call | bytes 8400896 | tf_op jit(solution)/shard_map/pallas_call | solution.py:197
  51.2 1.2 %copy.31 = bf16[16,8,8,576]{3,2,0,1:T(8,128)(2,1)} copy(bf16[16,8,8,576]{3,2,1,0:T(8,128)(2,1)S(1)} %bitcast.39) | data formatting | bytes 2359296 | tf_op jit(solution)/shard_map/reshape | solution.py:350
  52.4 0.1 copy.32
  52.5 0.1 copy.33
  52.5 1.0 reshape.84.sums_ref
  53.6 7.5 %shard_map.95.probs_ref = f32[8,2048]{1,0:T(8,128)} custom-call(s32[128]{0:T(128)} %starts_ref.3, bf16[1024,576]{1,0:T(8,128)(2,1)} %bitcast.48, bf16[2048,576]{1,0:T(8,128)(2,1)} %bitcast.55, f32[1024,1]{1,0:T(8,128)} %reshape.84.sums_ref), custom_call_target="tpu_custom_call" | custom-call | flops 2415919104 | bytes 3604480 | tf_op jit(solution)/shard_map/pallas_call | solution.py:237
  61.0 0.1 copy.29
  61.1 0.1 copy.30
  61.2 0.8 reshape_reshape.16.weight_ref
  62.0 0.7 copy.28
  62.7 5.1 %shard_map.96 = (bf16[512,128]{1,0:T(8,128)(2,1)}, f32[512,1]{1,0:T(8,128)}, f32[2048,128]{1,0:T(8,128)}) custom-call(s32[128]{0:T(128)} %starts_ref.3, bf16[512,128]{1,0:T(8,128)(2,1)} %bitcast.52, bf16[2048,128]{1,0:T(8,128)(2,1)} %bitcast.47, f32[512,1]{1,0:T(8,128)} %reshape_reshape.16.weight_ref, f32[8,2048]{1,0:T(8,128)} %shard_map.95.probs_ref), custom_call_target="tpu_custom_call" | custom-call | flops 805306368 | bytes 1703936 | tf_op jit(solution)/shard_map/pallas_call | solution.py:299
  67.8 1.2 %copy-done = f32[2048,128]{1,0:T(8,128)S(1)} copy-done((f32[2048,128]{1,0:T(8,128)S(1)}, f32[2048,128]{1,0:T(8,128)}, u32[]{:S(2)}) %copy-start) | copy-done | bytes 1048600
  69.0 2.4 %shard_map.97 = f32[8,128,128]{2,1,0:T(8,128)S(1)} custom-call(f32[16,128,128]{2,1,0:T(8,128)S(1)} %bitcast.37), custom_call_target="tpu_custom_call" | custom-call | bytes 1048576 | tf_op jit(solution)/shard_map/pallas_call | solution.py:197
  71.5 20.2 %shard_map.98 = f32[8,128,128]{2,1,0:T(8,128)S(1)} custom-call(f32[8,128,128]{2,1,0:T(8,128)S(1)} %bitcast_add_fusion.refs_0_), custom_call_target="tpu_custom_call" | custom-call | bytes 1048576 | tf_op jit(solution)/shard_map/pallas_call | solution.py:197
  91.8 0.1 reduce
  92.0 0.1 reshape_reshape.15
  92.1 0.1 copy.38
  92.2 0.1 copy.39.refs_2_
  92.3 13.8 %shard_map.99 = (f32[16,8,128]{2,1,0:T(8,128)S(1)}, bf16[16,32,128]{2,1,0:T(8,128)(2,1)S(1)}, f32[16,1,32]{2,1,0:T(1,128)S(1)}) custom-call(f32[16,8,128]{2,1,0:T(8,128)S(1)} %bitcast.41, bf16[16,32,128]{2,1,0:T(8,128)(2,1)S(1)} %bitcast.40, f32[16,1,32]{2,1,0:T(1,128)S(1)} %copy.39.refs_2_), custom_call_target="tpu_custom_call" | custom-call | bytes 397312 | tf_op jit(solution)/shard_map/pallas_call | solution.py:197
  106.1 10.9 %shard_map.100 = f32[16,8,128]{2,1,0:T(8,128)S(1)} custom-call(f32[8,128]{1,0:T(8,128)S(1)} %reduce_sum.19.refs_0_), custom_call_target="tpu_custom_call" | custom-call | bytes 131072 | tf_op jit(solution)/shard_map/pallas_call | solution.py:197
  117.0 0.6 convert_bitcast_fusion
  117.6 0.5 broadcast.5
  118.1 0.7 reduce.4
  118.8 0.1 reshape.83
  118.9 0.7 copy.40
  119.6 0.7 copy.43
  (21 shorter events, 0.2 us)
Async XLA Ops:
  0.6 2.4 %copy-start.5 = (bf16[128,576]{0,1:T(8,128)(2,1)S(1)}, bf16[128,576]{0,1:T(8,128)(2,1)}, u32[]{:S(2)}) copy-start(bf16[128,576]{0,1:T(8,128)(2,1)} %param.8) | copy-start | bytes 442372
  0.7 2.5 %copy-start.7 = (f32[128,8]{0,1:T(8,128)S(1)}, f32[128,8]{0,1:T(8,128)}, u32[]{:S(2)}) copy-start(f32[128,8]{0,1:T(8,128)} %param.9) | copy-start | bytes 12292
  0.7 2.7 %copy-start.8 = (f32[128,4]{0,1:T(4,128)S(1)}, f32[128,4]{0,1:T(4,128)}, u32[]{:S(2)}) copy-start(f32[128,4]{0,1:T(4,128)} %param.13) | copy-start | bytes 6148
  0.7 2.9 %copy-start.1 = (bf16[128,4,128]{2,1,0:T(4,128)(2,1)S(1)}, bf16[128,4,128]{2,1,0:T(4,128)(2,1)}, u32[]{:S(2)}) copy-start(bf16[128,4,128]{2,1,0:T(4,128)(2,1)} %param.11) | copy-start | bytes 393220
  0.7 2.9 %copy-start.2 = (bf16[128,128]{1,0:T(8,128)(2,1)S(1)}, bf16[128,128]{1,0:T(8,128)(2,1)}, u32[]{:S(2)}) copy-start(bf16[128,128]{1,0:T(8,128)(2,1)} %refs_1_.1) | copy-start | bytes 98308
  51.1 1.2 %copy-start.3 = (bf16[16,128,128]{2,1,0:T(8,128)(2,1)}, bf16[16,128,128]{2,1,0:T(8,128)(2,1)S(1)}, u32[]{:S(2)}) copy-start(bf16[16,128,128]{2,1,0:T(8,128)(2,1)S(1)} %get-tuple-element.16) | copy-start | bytes 1572868
  67.8 1.2 %copy-start = (f32[2048,128]{1,0:T(8,128)S(1)}, f32[2048,128]{1,0:T(8,128)}, u32[]{:S(2)}) copy-start(f32[2048,128]{1,0:T(8,128)} %get-tuple-element.21) | copy-start | bytes 3145732
  71.4 20.4 %copy-start.6 = (bf16[512,128]{1,0:T(8,128)(2,1)S(1)}, bf16[512,128]{1,0:T(8,128)(2,1)}, u32[]{:S(2)}) copy-start(bf16[512,128]{1,0:T(8,128)(2,1)} %get-tuple-element.22) | copy-start | bytes 393220
  71.5 20.4 %copy-start.4 = (f32[512,1]{1,0:T(8,128)S(1)}, f32[512,1]{1,0:T(8,128)}, u32[]{:S(2)}) copy-start(f32[512,1]{1,0:T(8,128)} %get-tuple-element.23) | copy-start | bytes 6148

commit v13 on v12

--- a/solution.py
+++ b/solution.py
@@ -211,13 +211,14 @@
     )(*arrays)
 
 
-def head_mass_kernel(query_rows, starts_ref, query_ref, latent_ref, sums_ref, out_ref):
+def head_mass_kernel(query_rows, sources, starts_ref, query_ref, latent_ref, sums_ref, out_ref):
     rows, width = out_ref.shape
     scores = lax.dot_general(
         query_ref[...], latent_ref[...], (((1,), (1,)), ((), ())), preferred_element_type=jnp.float32
     )
     mass = jnp.exp(scores * main_scale - sums_ref[...])
-    mass = jnp.sum(mass.reshape(rows, mass.shape[0] // rows, width), axis=1)
+    heads = mass.shape[0] // (rows * sources)
+    mass = jnp.sum(mass.reshape(sources, rows, heads, width), axis=(0, 2))
     own_first = lax.axis_index("ha") * rows
     row_ids = lax.broadcasted_iota(jnp.int32, (rows, width), 0)
     starts = jnp.zeros((rows, width), jnp.int32)
@@ -229,13 +230,13 @@
     out_ref[...] = jnp.where(seen, mass, 0.0)
 
 
-def head_mass(flat_query, latent_piece, flat_sums, window_start, rows):
+def head_mass(flat_query, latent_piece, flat_sums, window_start, rows, sources):
     query_rows = window_start.shape[0]
     tokens, latent_width = latent_piece.shape
     width = math.gcd(tokens, 512)
     flat_rows = flat_query.shape[0]
     return pl.pallas_call(
-        functools.partial(head_mass_kernel, query_rows),
+        functools.partial(head_mass_kernel, query_rows, sources),
         out_shape=jax.ShapeDtypeStruct((rows, tokens), jnp.float32),
         grid_spec=pltpu.PrefetchScalarGridSpec(
             num_scalar_prefetch=1,
@@ -346,14 +347,8 @@
     )
     latent_piece = latent_parts.reshape(tokens, latent_width)
     keys_all = key_parts.reshape(tokens, index_width)
-    local_query = (
-        query_parts.reshape(groups, own_rows, head_count, latent_width)
-        .transpose(1, 0, 2, 3)
-        .reshape(own_rows * all_heads, latent_width)
-    )
-    local_sums = (
-        sums_parts.reshape(groups, own_rows, head_count).transpose(1, 0, 2).reshape(own_rows * all_heads, 1)
-    )
+    local_query = query_parts.reshape(own_rows * all_heads, latent_width)
+    local_sums = sums_parts.reshape(own_rows * all_heads, 1)
     local_index = (
         index_parts.reshape(groups, own_rows, part_heads, index_width)
         .transpose(1, 0, 2, 3)
@@ -366,7 +361,7 @@
     own_positions = row_first + jnp.arange(own_rows, dtype=jnp.int32)
     own_start = lax.dynamic_slice_in_dim(window_start, lax.axis_index("ha") * own_rows, own_rows, 0)
 
-    probs_all = head_mass(local_query, latent_piece, local_sums, window_start, own_rows)
+    probs_all = head_mass(local_query, latent_piece, local_sums, window_start, own_rows, groups)
 
     flat_index = local_index.reshape(own_rows * index_heads, index_width)
     query_grad, weight_grad, key_grad = indexer_grads(

time: 122 us -> 124 us (1.016)
  local copies, waits for them, and re-layouts: 10.5 us -> 12.1 us
    unnamed x24 -> x26, local copies, waits for them, and re-layouts: 5.27 us -> 7.99 us
where the time goes in v13:
time: 124 us; the launch traced here: 123 us
  Pallas kernels  107 us (86%)
  local copies, waits for them, and re-layouts  12.1 us (10%)
  other arithmetic  2.21 us (2%)
    pallas_call x5, Pallas kernels, exchange(): pl.pallas_call(functools.partial(exchange_kernel, items), out_shape=out_s...  94.8 us
    unnamed x26, local copies, waits for them, and re-layouts  7.99 us
    pallas_call x1, Pallas kernels, head_mass(): pl.pallas_call(functools.partial(head_mass_kernel, query_rows, sources),...  7.49 us
    pallas_call x1, Pallas kernels, indexer_grads(): pl.pallas_call(functools.partial(indexer_kernel, window_start.shape[0]),...  5.04 us

profile of v13, /device:TPU:8, one launch (start us, length us, event | category | flops | bytes accessed | tf_op | source)
XLA Modules:
  0.0 122.5 jit_solution(17664400578462073679)
XLA Ops:
  0.6 1.1 copy.23.refs_0_
  1.7 2.3 %copy.20 = bf16[128,8,576]{2,1,0:T(8,128)(2,1)S(1)} copy(bf16[128,8,576]{0,2,1:T(8,128)(2,1)} %param.7) | data formatting | bytes 2359296 | tf_op args[0]
  4.0 0.1 copy.21
  4.1 0.1 reshape.60
  4.2 0.1 copy.22
  4.3 0.1 reshape.62
  4.4 47.5 %shard_map.94 = (bf16[16,128,576]{2,1,0:T(8,128)(2,1)}, bf16[16,128,128]{2,1,0:T(8,128)(2,1)S(1)}, bf16[16,64,576]{2,1,0:T(8,128)(2,1)S(1)}, f32[16,1,64]{2,1,0:...) custom-call(bf16[128,576]{1,0:T(8,128)(2,1)S(1)} %copy.23.refs_0_, ...), custom_call_target="tpu_custom_call" | custom-call | bytes 8400896 | tf_op jit(solution)/shard_map/pallas_call | solution.py:197
  52.0 1.1 copy-done.4
  53.0 0.8 copy-done.5
  53.8 0.7 copy.26
  54.5 0.1 copy.27
  54.6 0.1 copy.28
  54.7 0.8 reshape_reshape.16.weight_ref
  55.6 0.5 broadcast.8
  56.1 0.7 reduce.7
  56.8 1.3 %reshape.76.sums_ref = f32[1024,1]{1,0:T(8,128)} reshape(f32[16,64]{1,0:T(8,128)S(1)} %reduce.7) | data formatting | bytes 8192 | tf_op jit(solution)/shard_map/reshape | solution.py:351
  58.0 7.5 %shard_map.95.probs_ref = f32[8,2048]{1,0:T(8,128)} custom-call(s32[128]{0:T(128)} %starts_ref.3, bf16[1024,576]{1,0:T(8,128)(2,1)} %bitcast.40, bf16[2048,576]{1,0:T(8,128)(2,1)} %bitcast.47, f32[1024,1]{1,0:T(8,128)} %reshape.76.sums_ref), custom_call_target="tpu_custom_call" | custom-call | flops 2415919104 | bytes 3604480 | tf_op jit(solution)/shard_map/pallas_call | solution.py:238
  65.5 5.0 %shard_map.96 = (bf16[512,128]{1,0:T(8,128)(2,1)}, f32[512,1]{1,0:T(8,128)}, f32[2048,128]{1,0:T(8,128)}) custom-call(s32[128]{0:T(128)} %starts_ref.3, bf16[512,128]{1,0:T(8,128)(2,1)} %bitcast.44, bf16[2048,128]{1,0:T(8,128)(2,1)} %bitcast.41, f32[512,1]{1,0:T(8,128)} %reshape_reshape.16.weight_ref, f32[8,2048]{1,0:T(8,128)} %shard_map.95.probs_ref), custom_call_target="tpu_custom_call" | custom-call | flops 805306368 | bytes 1703936 | tf_op jit(solution)/shard_map/pallas_call | solution.py:300
  70.6 1.2 copy-done
  71.8 2.4 %shard_map.97 = f32[8,128,128]{2,1,0:T(8,128)S(1)} custom-call(f32[16,128,128]{2,1,0:T(8,128)S(1)} %bitcast.31), custom_call_target="tpu_custom_call" | custom-call | bytes 1048576 | tf_op jit(solution)/shard_map/pallas_call | solution.py:197
  74.3 20.2 %shard_map.98 = f32[8,128,128]{2,1,0:T(8,128)S(1)} custom-call(f32[8,128,128]{2,1,0:T(8,128)S(1)} %bitcast_add_fusion.refs_0_), custom_call_target="tpu_custom_call" | custom-call | bytes 1048576 | tf_op jit(solution)/shard_map/pallas_call | solution.py:197
  94.6 0.1 reduce.1
  94.8 0.1 reshape_reshape.15
  94.9 0.1 copy.33
  95.0 0.1 copy.34.refs_2_
  95.1 13.8 %shard_map.99 = (f32[16,8,128]{2,1,0:T(8,128)S(1)}, bf16[16,32,128]{2,1,0:T(8,128)(2,1)S(1)}, f32[16,1,32]{2,1,0:T(1,128)S(1)}) custom-call(f32[16,8,128]{2,1,0:T(8,128)S(1)} %bitcast.34, bf16[16,32,128]{2,1,0:T(8,128)(2,1)S(1)} %bitcast.33, f32[16,1,32]{2,1,0:T(1,128)S(1)} %copy.34.refs_2_), custom_call_target="tpu_custom_call" | custom-call | bytes 397312 | tf_op jit(solution)/shard_map/pallas_call | solution.py:197
  108.9 10.9 %shard_map.100 = f32[16,8,128]{2,1,0:T(8,128)S(1)} custom-call(f32[8,128]{1,0:T(8,128)S(1)} %reduce_sum.19.refs_0_), custom_call_target="tpu_custom_call" | custom-call | bytes 131072 | tf_op jit(solution)/shard_map/pallas_call | solution.py:197
  119.8 0.6 convert_bitcast_fusion
  120.4 0.7 reduce.8
  121.1 0.1 reshape.75
  121.2 0.7 copy.35
  121.9 0.7 copy.38
  (21 shorter events, 0.2 us)
Async XLA Ops:
  1.7 2.3 %copy-start.8 = (f32[128,8]{0,1:T(8,128)S(1)}, f32[128,8]{0,1:T(8,128)}, u32[]{:S(2)}) copy-start(f32[128,8]{0,1:T(8,128)} %param.9) | copy-start | bytes 12292
  1.7 2.5 %copy-start.9 = (f32[128,4]{0,1:T(4,128)S(1)}, f32[128,4]{0,1:T(4,128)}, u32[]{:S(2)}) copy-start(f32[128,4]{0,1:T(4,128)} %param.13) | copy-start | bytes 6148
  1.7 2.7 %copy-start.2 = (bf16[128,4,128]{2,1,0:T(4,128)(2,1)S(1)}, bf16[128,4,128]{2,1,0:T(4,128)(2,1)}, u32[]{:S(2)}) copy-start(bf16[128,4,128]{2,1,0:T(4,128)(2,1)} %param.11) | copy-start | bytes 393220
  1.7 2.7 %copy-start.3 = (bf16[128,128]{1,0:T(8,128)(2,1)S(1)}, bf16[128,128]{1,0:T(8,128)(2,1)}, u32[]{:S(2)}) copy-start(bf16[128,128]{1,0:T(8,128)(2,1)} %refs_1_.1) | copy-start | bytes 98308
  52.0 1.1 copy-start.4
  53.0 0.8 copy-start.5
  70.6 1.2 %copy-start = (f32[2048,128]{1,0:T(8,128)S(1)}, f32[2048,128]{1,0:T(8,128)}, u32[]{:S(2)}) copy-start(f32[2048,128]{1,0:T(8,128)} %get-tuple-element.21) | copy-start | bytes 3145732
  71.8 2.4 %copy-start.1 = (f32[2048,128]{1,0:T(8,128)S(1)}, f32[2048,128]{1,0:T(8,128)}, u32[]{:S(2)}) copy-start(f32[2048,128]{1,0:T(8,128)} %get-tuple-element.21) | copy-start | bytes 3145732
  74.2 20.4 %copy-start.7 = (bf16[512,128]{1,0:T(8,128)(2,1)S(1)}, bf16[512,128]{1,0:T(8,128)(2,1)}, u32[]{:S(2)}) copy-start(bf16[512,128]{1,0:T(8,128)(2,1)} %get-tuple-element.22) | copy-start | bytes 393220
  74.3 20.4 %copy-start.6 = (f32[512,1]{1,0:T(8,128)S(1)}, f32[512,1]{1,0:T(8,128)}, u32[]{:S(2)}) copy-start(f32[512,1]{1,0:T(8,128)} %get-tuple-element.23) | copy-start | bytes 6148

commit v14 on v12

--- a/solution.py
+++ b/solution.py
@@ -232,7 +232,7 @@
 def head_mass(flat_query, latent_piece, flat_sums, window_start, rows):
     query_rows = window_start.shape[0]
     tokens, latent_width = latent_piece.shape
-    width = math.gcd(tokens, 512)
+    width = math.gcd(tokens, 1024)
     flat_rows = flat_query.shape[0]
     return pl.pallas_call(
         functools.partial(head_mass_kernel, query_rows),
@@ -396,8 +396,9 @@
     )
     query_output = query_back.reshape(query_rows, part_heads, index_width)
     weight_output = weight_back.reshape(query_rows, part_heads)
-    key_output = exchange([jnp.sum(key_rows, axis=0)], [("ha", "gather", False)], 3)[0]
-    key_output = key_output.reshape(query_rows, index_width).astype(jnp.bfloat16)
+    key_rows = jnp.sum(key_rows, axis=0).astype(jnp.bfloat16)
+    key_output = exchange([key_rows], [("ha", "gather", False)], 3)[0]
+    key_output = key_output.reshape(query_rows, index_width)
     return (query_output, key_output, weight_output)
 
 

time: 122 us -> 121 us (level)
    unnamed x24 -> x25, local copies, waits for them, and re-layouts: 5.27 us -> 5.89 us
where the time goes in v14:
time: 121 us; the launch traced here: 120 us
  Pallas kernels  107 us (88%)
  local copies, waits for them, and re-layouts  11.1 us (9%)
    pallas_call x5, Pallas kernels, exchange(): pl.pallas_call(functools.partial(exchange_kernel, items), out_shape=out_s...  94.7 us
    pallas_call x1, Pallas kernels, head_mass(): pl.pallas_call(functools.partial(head_mass_kernel, query_rows), out_shape...  7.04 us
    unnamed x25, local copies, waits for them, and re-layouts  5.89 us
    pallas_call x1, Pallas kernels, indexer_grads(): pl.pallas_call(functools.partial(indexer_kernel, window_start.shape[0]),...  5.06 us

profile of v14, /device:TPU:8, one launch (start us, length us, event | category | flops | bytes accessed | tf_op | source)
XLA Modules:
  0.0 119.7 jit_solution(12992975262270382790)
XLA Ops:
  0.7 2.3 %copy.22 = bf16[128,8,576]{2,1,0:T(8,128)(2,1)S(1)} copy(bf16[128,8,576]{0,2,1:T(8,128)(2,1)} %param.7) | data formatting | bytes 2359296 | tf_op args[0]
  3.0 0.2 copy.25.refs_0_
  3.2 0.1 copy.23
  3.3 0.1 reshape.67
  3.4 0.1 copy.24
  3.5 0.1 reshape.69
  3.6 47.5 %shard_map.94 = (bf16[16,128,576]{2,1,0:T(8,128)(2,1)}, bf16[16,128,128]{2,1,0:T(8,128)(2,1)S(1)}, bf16[16,64,576]{2,1,0:T(8,128)(2,1)S(1)}, f32[16,1,64]{2,1,0:...) custom-call(bf16[128,576]{1,0:T(8,128)(2,1)S(1)} %copy.25.refs_0_, ...), custom_call_target="tpu_custom_call" | custom-call | bytes 8400896 | tf_op jit(solution)/shard_map/pallas_call | solution.py:197
  51.2 1.2 %copy.31 = bf16[16,8,8,576]{3,2,0,1:T(8,128)(2,1)} copy(bf16[16,8,8,576]{3,2,1,0:T(8,128)(2,1)S(1)} %bitcast.38) | data formatting | bytes 2359296 | tf_op jit(solution)/shard_map/reshape | solution.py:350
  52.4 0.1 copy.32
  52.5 0.1 copy.33
  52.5 1.0 reshape.86.sums_ref
  53.6 7.0 %shard_map.95.probs_ref = f32[8,2048]{1,0:T(8,128)} custom-call(s32[128]{0:T(128)} %starts_ref.3, bf16[1024,576]{1,0:T(8,128)(2,1)} %bitcast.48, bf16[2048,576]{1,0:T(8,128)(2,1)} %bitcast.55, f32[1024,1]{1,0:T(8,128)} %reshape.86.sums_ref), custom_call_target="tpu_custom_call" | custom-call | flops 2415919104 | bytes 3604480 | tf_op jit(solution)/shard_map/pallas_call | solution.py:237
  60.6 0.1 copy.29
  60.7 0.1 copy.30
  60.8 0.8 reshape_reshape.16.weight_ref
  61.6 0.7 copy.28
  62.3 5.1 %shard_map.96 = (bf16[512,128]{1,0:T(8,128)(2,1)}, f32[512,1]{1,0:T(8,128)}, f32[2048,128]{1,0:T(8,128)}) custom-call(s32[128]{0:T(128)} %starts_ref.3, bf16[512,128]{1,0:T(8,128)(2,1)} %bitcast.52, bf16[2048,128]{1,0:T(8,128)(2,1)} %bitcast.47, f32[512,1]{1,0:T(8,128)} %reshape_reshape.16.weight_ref, f32[8,2048]{1,0:T(8,128)} %shard_map.95.probs_ref), custom_call_target="tpu_custom_call" | custom-call | flops 805306368 | bytes 1703936 | tf_op jit(solution)/shard_map/pallas_call | solution.py:299
  67.4 1.2 %copy-done = f32[2048,128]{1,0:T(8,128)S(1)} copy-done((f32[2048,128]{1,0:T(8,128)S(1)}, f32[2048,128]{1,0:T(8,128)}, u32[]{:S(2)}) %copy-start) | copy-done | bytes 1048600
  68.6 2.4 %shard_map.97 = f32[8,128,128]{2,1,0:T(8,128)S(1)} custom-call(f32[16,128,128]{2,1,0:T(8,128)S(1)} %bitcast.36), custom_call_target="tpu_custom_call" | custom-call | bytes 1048576 | tf_op jit(solution)/shard_map/pallas_call | solution.py:197
  71.1 20.2 %shard_map.98 = f32[8,128,128]{2,1,0:T(8,128)S(1)} custom-call(f32[8,128,128]{2,1,0:T(8,128)S(1)} %bitcast_add_fusion.refs_0_), custom_call_target="tpu_custom_call" | custom-call | bytes 1048576 | tf_op jit(solution)/shard_map/pallas_call | solution.py:197
  91.4 0.1 reduce
  91.6 0.1 reshape_reshape.15
  91.7 0.1 copy.38
  91.8 0.1 copy.39.refs_2_
  91.9 13.8 %shard_map.99 = (f32[16,8,128]{2,1,0:T(8,128)S(1)}, bf16[16,32,128]{2,1,0:T(8,128)(2,1)S(1)}, f32[16,1,32]{2,1,0:T(1,128)S(1)}) custom-call(f32[16,8,128]{2,1,0:T(8,128)S(1)} %bitcast.40, bf16[16,32,128]{2,1,0:T(8,128)(2,1)S(1)} %bitcast.39, f32[16,1,32]{2,1,0:T(1,128)S(1)} %copy.39.refs_2_), custom_call_target="tpu_custom_call" | custom-call | bytes 397312 | tf_op jit(solution)/shard_map/pallas_call | solution.py:197
  105.7 0.5 broadcast.5
  106.2 0.7 reduce.4
  106.9 0.1 reshape.85
  107.0 0.7 copy.40
  107.6 10.7 %shard_map.100 = bf16[16,8,128]{2,1,0:T(8,128)(2,1)S(1)} custom-call(bf16[8,128]{1,0:T(8,128)(2,1)S(1)} %reduce_sum.19.refs_0_), custom_call_target="tpu_custom_call" | custom-call | bytes 65536 | tf_op jit(solution)/shard_map/pallas_call | solution.py:197
  118.4 0.7 copy.44
  119.0 0.6 copy.45
  (21 shorter events, 0.2 us)
Async XLA Ops:
  0.6 2.4 %copy-start.5 = (bf16[128,576]{0,1:T(8,128)(2,1)S(1)}, bf16[128,576]{0,1:T(8,128)(2,1)}, u32[]{:S(2)}) copy-start(bf16[128,576]{0,1:T(8,128)(2,1)} %param.8) | copy-start | bytes 442372
  0.7 2.5 %copy-start.7 = (f32[128,8]{0,1:T(8,128)S(1)}, f32[128,8]{0,1:T(8,128)}, u32[]{:S(2)}) copy-start(f32[128,8]{0,1:T(8,128)} %param.9) | copy-start | bytes 12292
  0.7 2.7 %copy-start.8 = (f32[128,4]{0,1:T(4,128)S(1)}, f32[128,4]{0,1:T(4,128)}, u32[]{:S(2)}) copy-start(f32[128,4]{0,1:T(4,128)} %param.13) | copy-start | bytes 6148
  0.7 2.9 %copy-start.1 = (bf16[128,4,128]{2,1,0:T(4,128)(2,1)S(1)}, bf16[128,4,128]{2,1,0:T(4,128)(2,1)}, u32[]{:S(2)}) copy-start(bf16[128,4,128]{2,1,0:T(4,128)(2,1)} %param.11) | copy-start | bytes 393220
  0.7 2.9 %copy-start.2 = (bf16[128,128]{1,0:T(8,128)(2,1)S(1)}, bf16[128,128]{1,0:T(8,128)(2,1)}, u32[]{:S(2)}) copy-start(bf16[128,128]{1,0:T(8,128)(2,1)} %refs_1_.1) | copy-start | bytes 98308
  51.1 1.2 %copy-start.3 = (bf16[16,128,128]{2,1,0:T(8,128)(2,1)}, bf16[16,128,128]{2,1,0:T(8,128)(2,1)S(1)}, u32[]{:S(2)}) copy-start(bf16[16,128,128]{2,1,0:T(8,128)(2,1)S(1)} %get-tuple-element.16) | copy-start | bytes 1572868
  67.4 1.2 %copy-start = (f32[2048,128]{1,0:T(8,128)S(1)}, f32[2048,128]{1,0:T(8,128)}, u32[]{:S(2)}) copy-start(f32[2048,128]{1,0:T(8,128)} %get-tuple-element.21) | copy-start | bytes 3145732
  71.0 20.4 %copy-start.6 = (bf16[512,128]{1,0:T(8,128)(2,1)S(1)}, bf16[512,128]{1,0:T(8,128)(2,1)}, u32[]{:S(2)}) copy-start(bf16[512,128]{1,0:T(8,128)(2,1)} %get-tuple-element.22) | copy-start | bytes 393220
  71.1 20.4 %copy-start.4 = (f32[512,1]{1,0:T(8,128)S(1)}, f32[512,1]{1,0:T(8,128)}, u32[]{:S(2)}) copy-start(f32[512,1]{1,0:T(8,128)} %get-tuple-element.23) | copy-start | bytes 6148

commit v15 on v14

--- a/solution.py
+++ b/solution.py
@@ -232,7 +232,7 @@
 def head_mass(flat_query, latent_piece, flat_sums, window_start, rows):
     query_rows = window_start.shape[0]
     tokens, latent_width = latent_piece.shape
-    width = math.gcd(tokens, 1024)
+    width = math.gcd(tokens, 2048)
     flat_rows = flat_query.shape[0]
     return pl.pallas_call(
         functools.partial(head_mass_kernel, query_rows),

time: 121 us -> 121 us (level)
  no operation moved by 1% of the time
where the time goes in v15:
time: 121 us; the launch traced here: 120 us
  Pallas kernels  107 us (88%)
  local copies, waits for them, and re-layouts  11.1 us (9%)
    pallas_call x5, Pallas kernels, exchange(): pl.pallas_call(functools.partial(exchange_kernel, items), out_shape=out_s...  94.7 us
    pallas_call x1, Pallas kernels, head_mass(): pl.pallas_call(functools.partial(head_mass_kernel, query_rows), out_shape...  7.11 us
    unnamed x25, local copies, waits for them, and re-layouts  5.89 us
    pallas_call x1, Pallas kernels, indexer_grads(): pl.pallas_call(functools.partial(indexer_kernel, window_start.shape[0]),...  5.06 us

profile of v15, /device:TPU:8, one launch (start us, length us, event | category | flops | bytes accessed | tf_op | source)
XLA Modules:
  0.0 119.7 jit_solution(11409500566998142076)
XLA Ops:
  0.7 2.3 %copy.22 = bf16[128,8,576]{2,1,0:T(8,128)(2,1)S(1)} copy(bf16[128,8,576]{0,2,1:T(8,128)(2,1)} %param.7) | data formatting | bytes 2359296 | tf_op args[0]
  3.0 0.2 copy.25.refs_0_
  3.2 0.1 copy.23
  3.3 0.1 reshape.67
  3.4 0.1 copy.24
  3.5 0.1 reshape.69
  3.6 47.5 %shard_map.94 = (bf16[16,128,576]{2,1,0:T(8,128)(2,1)}, bf16[16,128,128]{2,1,0:T(8,128)(2,1)S(1)}, bf16[16,64,576]{2,1,0:T(8,128)(2,1)S(1)}, f32[16,1,64]{2,1,0:...) custom-call(bf16[128,576]{1,0:T(8,128)(2,1)S(1)} %copy.25.refs_0_, ...), custom_call_target="tpu_custom_call" | custom-call | bytes 8400896 | tf_op jit(solution)/shard_map/pallas_call | solution.py:197
  51.2 1.2 %copy.31 = bf16[16,8,8,576]{3,2,0,1:T(8,128)(2,1)} copy(bf16[16,8,8,576]{3,2,1,0:T(8,128)(2,1)S(1)} %bitcast.38) | data formatting | bytes 2359296 | tf_op jit(solution)/shard_map/reshape | solution.py:350
  52.4 0.1 copy.32
  52.5 0.1 copy.33
  52.5 1.0 reshape.86.sums_ref
  53.6 7.1 %shard_map.95.probs_ref = f32[8,2048]{1,0:T(8,128)} custom-call(s32[128]{0:T(128)} %starts_ref.3, bf16[1024,576]{1,0:T(8,128)(2,1)} %bitcast.48, bf16[2048,576]{1,0:T(8,128)(2,1)} %bitcast.55, f32[1024,1]{1,0:T(8,128)} %reshape.86.sums_ref), custom_call_target="tpu_custom_call" | custom-call | flops 2415919104 | bytes 3604480 | tf_op jit(solution)/shard_map/pallas_call | solution.py:237
  60.7 0.1 copy.29
  60.7 0.1 copy.30
  60.9 0.8 reshape_reshape.16.weight_ref
  61.7 0.7 copy.28
  62.4 5.1 %shard_map.96 = (bf16[512,128]{1,0:T(8,128)(2,1)}, f32[512,1]{1,0:T(8,128)}, f32[2048,128]{1,0:T(8,128)}) custom-call(s32[128]{0:T(128)} %starts_ref.3, bf16[512,128]{1,0:T(8,128)(2,1)} %bitcast.52, bf16[2048,128]{1,0:T(8,128)(2,1)} %bitcast.47, f32[512,1]{1,0:T(8,128)} %reshape_reshape.16.weight_ref, f32[8,2048]{1,0:T(8,128)} %shard_map.95.probs_ref), custom_call_target="tpu_custom_call" | custom-call | flops 805306368 | bytes 1703936 | tf_op jit(solution)/shard_map/pallas_call | solution.py:299
  67.5 1.2 %copy-done = f32[2048,128]{1,0:T(8,128)S(1)} copy-done((f32[2048,128]{1,0:T(8,128)S(1)}, f32[2048,128]{1,0:T(8,128)}, u32[]{:S(2)}) %copy-start) | copy-done | bytes 1048600
  68.7 2.4 %shard_map.97 = f32[8,128,128]{2,1,0:T(8,128)S(1)} custom-call(f32[16,128,128]{2,1,0:T(8,128)S(1)} %bitcast.36), custom_call_target="tpu_custom_call" | custom-call | bytes 1048576 | tf_op jit(solution)/shard_map/pallas_call | solution.py:197
  71.1 20.2 %shard_map.98 = f32[8,128,128]{2,1,0:T(8,128)S(1)} custom-call(f32[8,128,128]{2,1,0:T(8,128)S(1)} %bitcast_add_fusion.refs_0_), custom_call_target="tpu_custom_call" | custom-call | bytes 1048576 | tf_op jit(solution)/shard_map/pallas_call | solution.py:197
  91.5 0.1 reduce
  91.6 0.1 reshape_reshape.15
  91.8 0.1 copy.38
  91.9 0.1 copy.39.refs_2_
  91.9 13.8 %shard_map.99 = (f32[16,8,128]{2,1,0:T(8,128)S(1)}, bf16[16,32,128]{2,1,0:T(8,128)(2,1)S(1)}, f32[16,1,32]{2,1,0:T(1,128)S(1)}) custom-call(f32[16,8,128]{2,1,0:T(8,128)S(1)} %bitcast.40, bf16[16,32,128]{2,1,0:T(8,128)(2,1)S(1)} %bitcast.39, f32[16,1,32]{2,1,0:T(1,128)S(1)} %copy.39.refs_2_), custom_call_target="tpu_custom_call" | custom-call | bytes 397312 | tf_op jit(solution)/shard_map/pallas_call | solution.py:197
  105.8 0.5 broadcast.5
  106.3 0.7 reduce.4
  106.9 0.1 reshape.85
  107.0 0.7 copy.40
  107.7 10.7 %shard_map.100 = bf16[16,8,128]{2,1,0:T(8,128)(2,1)S(1)} custom-call(bf16[8,128]{1,0:T(8,128)(2,1)S(1)} %reduce_sum.19.refs_0_), custom_call_target="tpu_custom_call" | custom-call | bytes 65536 | tf_op jit(solution)/shard_map/pallas_call | solution.py:197
  118.5 0.7 copy.44
  119.1 0.6 copy.45
  (21 shorter events, 0.2 us)
Async XLA Ops:
  0.6 2.4 %copy-start.5 = (bf16[128,576]{0,1:T(8,128)(2,1)S(1)}, bf16[128,576]{0,1:T(8,128)(2,1)}, u32[]{:S(2)}) copy-start(bf16[128,576]{0,1:T(8,128)(2,1)} %param.8) | copy-start | bytes 442372
  0.7 2.5 %copy-start.7 = (f32[128,8]{0,1:T(8,128)S(1)}, f32[128,8]{0,1:T(8,128)}, u32[]{:S(2)}) copy-start(f32[128,8]{0,1:T(8,128)} %param.9) | copy-start | bytes 12292
  0.7 2.7 %copy-start.8 = (f32[128,4]{0,1:T(4,128)S(1)}, f32[128,4]{0,1:T(4,128)}, u32[]{:S(2)}) copy-start(f32[128,4]{0,1:T(4,128)} %param.13) | copy-start | bytes 6148
  0.7 2.9 %copy-start.1 = (bf16[128,4,128]{2,1,0:T(4,128)(2,1)S(1)}, bf16[128,4,128]{2,1,0:T(4,128)(2,1)}, u32[]{:S(2)}) copy-start(bf16[128,4,128]{2,1,0:T(4,128)(2,1)} %param.11) | copy-start | bytes 393220
  0.7 2.9 %copy-start.2 = (bf16[128,128]{1,0:T(8,128)(2,1)S(1)}, bf16[128,128]{1,0:T(8,128)(2,1)}, u32[]{:S(2)}) copy-start(bf16[128,128]{1,0:T(8,128)(2,1)} %refs_1_.1) | copy-start | bytes 98308
  51.1 1.2 %copy-start.3 = (bf16[16,128,128]{2,1,0:T(8,128)(2,1)}, bf16[16,128,128]{2,1,0:T(8,128)(2,1)S(1)}, u32[]{:S(2)}) copy-start(bf16[16,128,128]{2,1,0:T(8,128)(2,1)S(1)} %get-tuple-element.16) | copy-start | bytes 1572868
  67.5 1.2 %copy-start = (f32[2048,128]{1,0:T(8,128)S(1)}, f32[2048,128]{1,0:T(8,128)}, u32[]{:S(2)}) copy-start(f32[2048,128]{1,0:T(8,128)} %get-tuple-element.21) | copy-start | bytes 3145732
  71.1 20.4 %copy-start.6 = (bf16[512,128]{1,0:T(8,128)(2,1)S(1)}, bf16[512,128]{1,0:T(8,128)(2,1)}, u32[]{:S(2)}) copy-start(bf16[512,128]{1,0:T(8,128)(2,1)} %get-tuple-element.22) | copy-start | bytes 393220
  71.1 20.4 %copy-start.4 = (f32[512,1]{1,0:T(8,128)S(1)}, f32[512,1]{1,0:T(8,128)}, u32[]{:S(2)}) copy-start(f32[512,1]{1,0:T(8,128)} %get-tuple-element.23) | copy-start | bytes 6148
